TPU v7x, 32 devices: a whole 2x2x4 slice. The times are simulated.
32 devices in a mesh: pipe: 4 (over y, core), expert: 4 (over z), dp: 2 (over x).
Axes of the slice: x: 2, y: 2, z: 4, core: 2. Of those that a mesh axis runs over, the one named last changes fastest.
Arguments:
- acts: bfloat16 [256, 3584], P(('pipe', 'expert', 'dp')), may hold values from -6 to 6
- cotangent: bfloat16 [256, 3584], P(('pipe', 'expert', 'dp')), may hold values from -6 to 6
- routes: int32 [256, 1], P(('pipe', 'expert', 'dp')), may hold values from 0 to 1; in each aligned block of 8 rows (0 to 7, 8 to 15, ...) at most 6 rows name the same one
- probs: bfloat16 [256, 1], P(('pipe', 'expert', 'dp')), may hold values from 0.19921875 to 1
- keep: int32 [4, 8], P('pipe', ('expert', 'dp')), may hold values 0 or 1
- w_gate: bfloat16 [4, 4, 3584, 512], P('pipe', 'expert', None, 'dp'), may hold values from -0.09375 to 0.09375
- w_up: bfloat16 [4, 4, 3584, 512], P('pipe', 'expert', None, 'dp'), may hold values from -0.09375 to 0.09375
- w_down: bfloat16 [4, 4, 512, 3584], P('pipe', 'expert', 'dp'), may hold values from -0.1875 to 0.1875
Outputs:
- layer_out: bfloat16 [256, 3584], P(('pipe', 'expert', 'dp'))
- grad_below: bfloat16 [256, 3584], P(('pipe', 'expert', 'dp'))
Inputs may be any that keep to these rules, and one draw needn't show every extreme that they name: `routes`: the 1 expert of a token differ. Among the rows of one device no expert is named more than 6 times, and in every draw some device names some expert exactly 6 times.
All inputs are finite; a program needn't handle non-finite values. No bound on the sum of `keep` on one device may be relied on, other than what follows from the above.
Results may differ from a plain program's by a relative error of at most 0.0075.
Values may be sent and summed in bfloat16 or wider, within the bound.
No kernel may reach another device: no remote copies, remote signals or barrier semaphores. Data moves between devices by JAX's collectives and lax.ppermute only.
A program may use at most 64 MiB of HBM per device.

v0:
```python
import jax
import jax.numpy as jnp
from jax import lax
from jax.sharding import PartitionSpec as P


def from_behind(shard, axis, by):
    count = lax.axis_size(axis)
    pairs = [(i, i + by) for i in range(count) if 0 <= i + by < count]
    return lax.ppermute(shard, axis, pairs)


def expert_pass(input_rows, rows_cot, gate_cols, up_cols, down_rows):
    contract = (((1,), (1,)), ((), ()))
    gate_pre = jnp.dot(input_rows, gate_cols, preferred_element_type=jnp.float32)
    up_pre = jnp.dot(input_rows, up_cols, preferred_element_type=jnp.float32)
    squash = jax.nn.sigmoid(gate_pre)
    hidden = (gate_pre * squash * up_pre).astype(jnp.bfloat16)
    grad_hidden = lax.dot_general(rows_cot, down_rows, contract, preferred_element_type=jnp.float32)
    grad_gate = (grad_hidden * up_pre * squash * (1.0 + gate_pre * (1.0 - squash))).astype(
        jnp.bfloat16
    )
    grad_up = (grad_hidden * gate_pre * squash).astype(jnp.bfloat16)
    part_out = jnp.dot(hidden, down_rows, preferred_element_type=jnp.float32)
    partial_gradient = lax.dot_general(
        grad_gate, gate_cols, contract, preferred_element_type=jnp.float32
    )
    partial_gradient = partial_gradient + lax.dot_general(
        grad_up, up_cols, contract, preferred_element_type=jnp.float32
    )
    return (part_out, partial_gradient)


def shared_rows(input_rows, rows_cot, gate_cols, up_cols, down_rows):
    every_in, every_cot = (
        lax.all_gather(input_rows, "dp", axis=0, tiled=True),
        lax.all_gather(rows_cot, "dp", axis=0, tiled=True),
    )
    part_out, partial_gradient = expert_pass(every_in, every_cot, gate_cols, up_cols, down_rows)
    summed_out, summed_grad = (
        lax.psum_scatter(
            part_out.astype(jnp.bfloat16), "dp", scatter_dimension=0, tiled=True
        ).astype(jnp.float32),
        lax.psum_scatter(
            partial_gradient.astype(jnp.bfloat16), "dp", scatter_dimension=0, tiled=True
        ).astype(jnp.float32),
    )
    return (summed_out.astype(jnp.bfloat16), summed_grad.astype(jnp.bfloat16))


def shards(acts, cotangent, routes, probs, keep, w_gate, w_up, w_down):
    n_expert = lax.axis_size("expert")
    experts = n_expert // 2
    token_count = acts.shape[0]
    width = acts.shape[1]
    top_count = routes.shape[1]
    capacity = 2 * ((token_count * top_count * 5 + 8 * experts - 1) // (8 * experts))
    slot_count = experts * capacity
    pair_count = token_count * top_count
    chosen = routes.reshape(pair_count)
    weights = probs.reshape(pair_count)
    expert_hot = (chosen[:, None] == jnp.arange(experts, dtype=jnp.int32)[None, :]).astype(
        jnp.int32
    )
    ranks = jnp.cumsum(expert_hot, axis=0) - 1
    placed = jnp.sum(expert_hot * ranks, axis=1)
    target = chosen * capacity + placed
    slot_hot = target[:, None] == jnp.arange(slot_count, dtype=jnp.int32)[None, :]
    owner = jnp.arange(pair_count, dtype=jnp.int32) // top_count
    token_hot = (owner[:, None] == jnp.arange(token_count, dtype=jnp.int32)[None, :]).astype(
        jnp.bfloat16
    )
    scatter_mat = jnp.dot(
        slot_hot.astype(jnp.bfloat16).T, token_hot, preferred_element_type=jnp.float32
    ).astype(jnp.bfloat16)
    weighted_hot = jnp.where(slot_hot, weights[:, None], jnp.zeros((), jnp.bfloat16))
    gather_matrix = jnp.dot(token_hot.T, weighted_hot, preferred_element_type=jnp.float32).astype(
        jnp.bfloat16
    )
    packed_in = jnp.dot(scatter_mat, acts, preferred_element_type=jnp.float32).astype(jnp.bfloat16)
    packed_cot = jnp.dot(scatter_mat, cotangent, preferred_element_type=jnp.float32).astype(
        jnp.bfloat16
    )
    gate_cols = w_gate[0, 0]
    up_cols = w_up[0, 0]
    down_rows = w_down[0, 0]
    send_in = jnp.repeat(packed_in.reshape(experts, capacity, width), 2, axis=0).reshape(
        n_expert * capacity, width
    )
    send_cot = jnp.repeat(packed_cot.reshape(experts, capacity, width), 2, axis=0).reshape(
        n_expert * capacity, width
    )
    got_in, got_cot = (
        lax.all_to_all(send_in, "expert", split_axis=0, concat_axis=0, tiled=True),
        lax.all_to_all(send_cot, "expert", split_axis=0, concat_axis=0, tiled=True),
    )
    half_out, half_grad = shared_rows(got_in, got_cot, gate_cols, up_cols, down_rows)
    back_out, back_grad = (
        lax.all_to_all(half_out, "expert", split_axis=0, concat_axis=0, tiled=True),
        lax.all_to_all(half_grad, "expert", split_axis=0, concat_axis=0, tiled=True),
    )
    expert_out = jnp.sum(back_out.reshape(experts, 2, capacity, width).astype(jnp.float32), axis=1)
    expert_out = expert_out.astype(jnp.bfloat16).reshape(slot_count, width)
    expert_grad = jnp.sum(
        back_grad.reshape(experts, 2, capacity, width).astype(jnp.float32), axis=1
    )
    expert_grad = expert_grad.astype(jnp.bfloat16).reshape(slot_count, width)
    mixed_out = jnp.dot(gather_matrix, expert_out, preferred_element_type=jnp.float32)
    mixed_grad = jnp.dot(gather_matrix, expert_grad, preferred_element_type=jnp.float32)
    keep_scale = keep[0, 0].astype(jnp.float32)
    layer_out = (acts.astype(jnp.float32) + keep_scale * mixed_out).astype(jnp.bfloat16)
    section_grad = (cotangent.astype(jnp.float32) + keep_scale * mixed_grad).astype(jnp.bfloat16)
    grad_below = from_behind(section_grad, "pipe", -1)
    return (layer_out, grad_below)


def solution(mesh):
    return jax.shard_map(
        shards,
        mesh=mesh,
        in_specs=(
            P(("pipe", "expert", "dp"), None),
            P(("pipe", "expert", "dp"), None),
            P(("pipe", "expert", "dp"), None),
            P(("pipe", "expert", "dp"), None),
            P("pipe", ("expert", "dp")),
            P("pipe", "expert", None, "dp"),
            P("pipe", "expert", None, "dp"),
            P("pipe", "expert", "dp", None),
        ),
        out_specs=(P(("pipe", "expert", "dp"), None), P(("pipe", "expert", "dp"), None)),
        check_vma=False,
    )
```

profile of v0, /device:TPU:0, one launch (start us, length us, event | category | flops | bytes accessed | tf_op | source)
XLA Modules:
  0.0 100.5 jit_solution(3909824233218656353)
XLA Ops:
  7.2 0.0 copy-start
  7.2 0.8 fusion.24
  8.0 0.2 reduce_window_sum.11
  8.2 0.7 select_reduce_fusion
  8.8 0.7 fusion.25
  9.5 0.2 convolution_convert_fusion.4
  9.7 1.0 %convolution_convert_fusion.2 = bf16[12,3584]{1,0:T(8,128)(2,1)S(1)} fusion(bf16[12,8]{0,1:T(8,128)(2,1)S(1)} %convolution_convert_fusion.4, bf16[8,3584]{1,0:T(8,128)(2,1)} %param.8), kind=kOutput, calls=%fused_computation.4 | convolution fusion | flops 731136 | bytes 143552 | tf_op jit(solution)/shard_map/dot_general | solution.py:80
  10.8 0.7 broadcast_in_dim.28
  11.5 6.3 %all-to-all-start = ((bf16[4,6,3584]{2,1,0:T(8,128)(2,1)}), bf16[4,6,3584]{2,1,0:T(8,128)(2,1)S(1)}, u32[]{:S(2)}, u32[]{:S(2)}) async-start(bf16[4,6,3584]{2,1,0:T(8,128)(2,1)} %bitcast.5), calls=%async_computation | async-start | bytes 458752 | tf_op jit(solution)/shard_map/all_to_all | solution.py:94
  17.8 1.0 %convolution_convert_fusion.1 = bf16[12,3584]{1,0:T(8,128)(2,1)S(1)} fusion(bf16[12,8]{0,1:T(8,128)(2,1)S(1)} %convolution_convert_fusion.4, bf16[8,3584]{1,0:T(8,128)(2,1)} %param.9), kind=kOutput, calls=%fused_computation.3 | convolution fusion | flops 731136 | bytes 143552 | tf_op jit(solution)/shard_map/dot_general | solution.py:81
  18.9 7.1 %all-to-all-done = bf16[4,6,3584]{2,1,0:T(8,128)(2,1)S(1)} async-done(((bf16[4,6,3584]{2,1,0:T(8,128)(2,1)}), bf16[4,6,3584]{2,1,0:T(8,128)(2,1)S(1)}, u32[]{:S(2)}, u32[]{:S(2)}) %all-to-all-start) | async-done | bytes 172064 | tf_op jit(solution)/shard_map/all_to_all | solution.py:94
  26.0 0.7 broadcast_in_dim.29
  26.7 3.4 %all-to-all-start.2 = ((bf16[4,6,3584]{2,1,0:T(8,128)(2,1)}), bf16[4,6,3584]{2,1,0:T(8,128)(2,1)S(1)}, u32[]{:S(2)}, u32[]{:S(2)}) async-start(bf16[4,6,3584]{2,1,0:T(8,128)(2,1)} %bitcast.10), calls=%async_computation.3 | async-start | bytes 458752 | tf_op jit(solution)/shard_map/all_to_all | solution.py:95
  30.1 0.0 reduce-scatter.5.cloned.1.call-start
  30.1 0.1 all_to_all.30
  30.2 0.0 copy-start.1
  30.2 6.2 %all_gather.6 = bf16[48,3584]{1,0:T(8,128)(2,1)S(1)} all-gather(bf16[24,3584]{1,0:T(8,128)(2,1)S(1)} %all_to_all.30), channel_id=1, replica_groups=mesh['pipe'=4,'expert'=4,'dp'=2] {'dp'}, dimensions={0}, use_global_device_ids=true | all-gather | bytes 516096 | tf_op jit(solution)/shard_map/all_gather | solution.py:36
  36.4 0.0 copy-done
  36.4 0.4 fusion.13
  36.9 0.0 copy-done.1
  36.9 0.4 fusion.9
  37.3 0.0 all-to-all-done.2
  37.3 0.1 all_to_all.35
  37.4 6.1 %all_gather.7 = bf16[48,3584]{1,0:T(8,128)(2,1)S(1)} all-gather(bf16[24,3584]{1,0:T(8,128)(2,1)S(1)} %all_to_all.35), channel_id=1, replica_groups=mesh['pipe'=4,'expert'=4,'dp'=2] {'dp'}, dimensions={0}, use_global_device_ids=true | all-gather | bytes 516096 | tf_op jit(solution)/shard_map/all_gather | solution.py:37
  43.5 2.1 %fusion.5 = f32[48,256]{1,0:T(8,128)S(1)} fusion(bf16[48,3584]{1,0:T(8,128)(2,1)S(1)} %all_gather.7, bf16[1,1,256,3584]{3,2,1,0:T(8,128)(2,1)} %param.15), kind=kOutput, calls=%fused_computation.11 | convolution fusion | flops 88080384 | bytes 2228224 | tf_op jit(solution)/shard_map/dot_general | solution.py:19
  45.6 0.0 copy-start.2
  45.6 0.6 fusion.11
  46.3 0.9 copy-done.2
  47.1 1.4 %fusion = bf16[48,3584]{1,0:T(8,128)(2,1)} fusion(f32[48,3584]{1,0:T(8,128)S(1)} %fusion.11, bf16[1,1,3584,256]{3,2,1,0:T(8,128)(2,1)S(1)} %copy-done.2, f32[48,256]{1,0:T(8,128)S(1)} %fusion.5, f32[48,256]{1,0:T(8,128)S(1)} %fusion.13), kind=kOutput, calls=%fused_computation.1 | convolution fusion | flops 88498176 | bytes 2965504 | tf_op jit(solution)/shard_map/dot_general | solution.py:28
  48.5 0.0 copy-start.5
  48.5 0.0 reduce-scatter.5.cloned.1.call-update
  48.6 0.0 reduce-scatter.3.cloned.1.call-start
  48.6 2.6 %convolution_convert_fusion = bf16[48,3584]{1,0:T(8,128)(2,1)} fusion(bf16[1,1,256,3584]{3,2,1,0:T(8,128)(2,1)} %param.15, f32[48,256]{1,0:T(8,128)S(1)} %fusion.9, f32[48,256]{1,0:T(8,128)S(1)} %fusion.13), kind=kOutput, calls=%fused_computation.2 | convolution fusion | flops 88326144 | bytes 2277376 | tf_op jit(solution)/shard_map/dot_general | solution.py:24
  51.2 0.0 copy-start.3
  51.2 0.0 copy-start.4
  51.2 0.0 reduce-scatter.3.cloned.1.call-update
  51.3 11.4 %reduce-scatter.5.cloned.1.call-done = bf16[24,3584]{1,0:T(8,128)(2,1)} async-done(((bf16[48,3584]{1,0:T(8,128)(2,1)}), bf16[24,3584]{1,0:T(8,128)(2,1)}) %reduce-scatter.5.cloned.1.call-update) | async-done | bytes 172048 | tf_op jit(solution)/shard_map/reduce_scatter | solution.py:44
  62.7 1.7 %all_to_all.36 = bf16[4,6,3584]{2,1,0:T(8,128)(2,1)} reshape(bf16[24,3584]{1,0:T(8,128)(2,1)} %reduce-scatter.5.cloned.1.call-done) | data formatting | bytes 344064 | tf_op jit(solution)/shard_map/all_to_all | solution.py:100
  64.3 4.6 %all-to-all-start.3 = ((bf16[4,6,3584]{2,1,0:T(8,128)(2,1)}), bf16[4,6,3584]{2,1,0:T(8,128)(2,1)S(1)}, u32[]{:S(2)}, u32[]{:S(2)}) async-start(bf16[4,6,3584]{2,1,0:T(8,128)(2,1)} %all_to_all.36), calls=%async_computation.5 | async-start | bytes 458752 | tf_op jit(solution)/shard_map/all_to_all | solution.py:100
  69.6 0.0 copy-done.5
  69.6 0.2 convolution_convert_fusion.3
  69.8 7.9 %reduce-scatter.3.cloned.1.call-done = bf16[24,3584]{1,0:T(8,128)(2,1)} async-done(((bf16[48,3584]{1,0:T(8,128)(2,1)}), bf16[24,3584]{1,0:T(8,128)(2,1)}) %reduce-scatter.3.cloned.1.call-update) | async-done | bytes 172048 | tf_op jit(solution)/shard_map/reduce_scatter | solution.py:41
  77.6 1.7 %all_to_all.31 = bf16[4,6,3584]{2,1,0:T(8,128)(2,1)} reshape(bf16[24,3584]{1,0:T(8,128)(2,1)} %reduce-scatter.3.cloned.1.call-done) | data formatting | bytes 344064 | tf_op jit(solution)/shard_map/all_to_all | solution.py:99
  79.3 0.0 all-to-all-done.3
  79.3 4.6 %all-to-all-start.1 = ((bf16[4,6,3584]{2,1,0:T(8,128)(2,1)}), bf16[4,6,3584]{2,1,0:T(8,128)(2,1)S(1)}, u32[]{:S(2)}, u32[]{:S(2)}) async-start(bf16[4,6,3584]{2,1,0:T(8,128)(2,1)} %all_to_all.31), calls=%async_computation.2 | async-start | bytes 458752 | tf_op jit(solution)/shard_map/all_to_all | solution.py:99
  84.0 0.0 copy-done.3
  84.0 0.1 fusion.4
  84.1 1.3 %collective-permute-start = (bf16[8,3584]{1,0:T(8,128)(2,1)S(1)}, bf16[8,3584]{1,0:T(8,128)(2,1)S(1)}, u32[]{:S(2)}, u32[]{:S(2)}) collective-permute-start(bf16[8,3584]{1,0:T(8,128)(2,1)S(1)} %fusion.4), channel_id=1, source_target_pairs={{8,0},{16,8},{24,16},{9,1},{17,9},{25,17},{10,2},{18,10},{26,18},{... | collective-permute-start | bytes 172040 | tf_op jit(solution)/shard_map/ppermute | solution.py:10
  85.4 6.7 %all-to-all-done.1 = bf16[4,6,3584]{2,1,0:T(8,128)(2,1)S(1)} async-done(((bf16[4,6,3584]{2,1,0:T(8,128)(2,1)}), bf16[4,6,3584]{2,1,0:T(8,128)(2,1)S(1)}, u32[]{:S(2)}, u32[]{:S(2)}) %all-to-all-start.1) | async-done | bytes 172064 | tf_op jit(solution)/shard_map/all_to_all | solution.py:99
  92.2 0.0 copy-done.4
  92.2 0.8 fusion.3
  93.0 0.0 collective-permute-done
  93.0 0.6 copy.12
  (6 shorter events, 0.2 us)
Async XLA Ops:
  7.2 29.3 %copy-start = (bf16[1,1,3584,256]{3,2,1,0:T(8,128)(2,1)S(1)}, bf16[1,1,3584,256]{3,2,1,0:T(8,128)(2,1)}, u32[]{:S(2)}) copy-start(bf16[1,1,3584,256]{3,2,1,0:T(8,128)(2,1)} %param.13) | copy-start | bytes 5505028
  11.5 14.5 %all-to-all-start = ((bf16[4,6,3584]{2,1,0:T(8,128)(2,1)}), bf16[4,6,3584]{2,1,0:T(8,128)(2,1)S(1)}, u32[]{:S(2)}, u32[]{:S(2)}) async-start(bf16[4,6,3584]{2,1,0:T(8,128)(2,1)} %bitcast.5), calls=%async_computation | async-start | bytes 458752 | tf_op jit(solution)/shard_map/all_to_all | solution.py:94
  26.7 10.6 %all-to-all-start.2 = ((bf16[4,6,3584]{2,1,0:T(8,128)(2,1)}), bf16[4,6,3584]{2,1,0:T(8,128)(2,1)S(1)}, u32[]{:S(2)}, u32[]{:S(2)}) async-start(bf16[4,6,3584]{2,1,0:T(8,128)(2,1)} %bitcast.10), calls=%async_computation.3 | async-start | bytes 458752 | tf_op jit(solution)/shard_map/all_to_all | solution.py:95
  30.1 32.6 %reduce-scatter.5.cloned.1.call-start = ((), (), s32[]{:S(2)}) async-start(), calls=%async_computation.7 | async-start | bytes 516096 | tf_op jit(solution)/shard_map/reduce_scatter | solution.py:44
  30.2 6.7 %copy-start.1 = (bf16[1,1,3584,256]{3,2,1,0:T(8,128)(2,1)S(1)}, bf16[1,1,3584,256]{3,2,1,0:T(8,128)(2,1)}, u32[]{:S(2)}) copy-start(bf16[1,1,3584,256]{3,2,1,0:T(8,128)(2,1)} %param.14) | copy-start | bytes 5505028
  45.6 1.5 %copy-start.2 = (bf16[1,1,3584,256]{3,2,1,0:T(8,128)(2,1)S(1)}, bf16[1,1,3584,256]{3,2,1,0:T(8,128)(2,1)}, u32[]{:S(2)}) copy-start(bf16[1,1,3584,256]{3,2,1,0:T(8,128)(2,1)} %param.14) | copy-start | bytes 5505028
  48.5 21.1 %copy-start.5 = (bf16[8,1]{0,1:T(2,128)(2,1)S(1)}, bf16[8,1]{0,1:T(2,128)(2,1)}, u32[]{:S(2)}) copy-start(bf16[8,1]{0,1:T(2,128)(2,1)} %param.11) | copy-start | bytes 52
  48.6 29.1 %reduce-scatter.3.cloned.1.call-start = ((), (), s32[]{:S(2)}) async-start(), calls=%async_computation.6 | async-start | bytes 516096 | tf_op jit(solution)/shard_map/reduce_scatter | solution.py:41
  51.2 32.8 %copy-start.3 = (bf16[8,3584]{1,0:T(8,128)(2,1)S(1)}, bf16[8,3584]{1,0:T(8,128)(2,1)}, u32[]{:S(2)}) copy-start(bf16[8,3584]{1,0:T(8,128)(2,1)} %param.9) | copy-start | bytes 172036
  51.2 41.0 %copy-start.4 = (bf16[8,3584]{1,0:T(8,128)(2,1)S(1)}, bf16[8,3584]{1,0:T(8,128)(2,1)}, u32[]{:S(2)}) copy-start(bf16[8,3584]{1,0:T(8,128)(2,1)} %param.8) | copy-start | bytes 172036
  64.3 14.9 %all-to-all-start.3 = ((bf16[4,6,3584]{2,1,0:T(8,128)(2,1)}), bf16[4,6,3584]{2,1,0:T(8,128)(2,1)S(1)}, u32[]{:S(2)}, u32[]{:S(2)}) async-start(bf16[4,6,3584]{2,1,0:T(8,128)(2,1)} %all_to_all.36), calls=%async_computation.5 | async-start | bytes 458752 | tf_op jit(solution)/shard_map/all_to_all | solution.py:100
  79.3 12.8 %all-to-all-start.1 = ((bf16[4,6,3584]{2,1,0:T(8,128)(2,1)}), bf16[4,6,3584]{2,1,0:T(8,128)(2,1)S(1)}, u32[]{:S(2)}, u32[]{:S(2)}) async-start(bf16[4,6,3584]{2,1,0:T(8,128)(2,1)} %all_to_all.31), calls=%async_computation.2 | async-start | bytes 458752 | tf_op jit(solution)/shard_map/all_to_all | solution.py:99
  84.1 8.8 %collective-permute-start = (bf16[8,3584]{1,0:T(8,128)(2,1)S(1)}, bf16[8,3584]{1,0:T(8,128)(2,1)S(1)}, u32[]{:S(2)}, u32[]{:S(2)}) collective-permute-start(bf16[8,3584]{1,0:T(8,128)(2,1)S(1)} %fusion.4), channel_id=1, source_target_pairs={{8,0},{16,8},{24,16},{9,1},{17,9},{25,17},{10,2},{18,10},{26,18},{... | collective-permute-start | bytes 172040 | tf_op jit(solution)/shard_map/ppermute | solution.py:10
Sparse Core Ops, SparseCore 0:
  48.7 13.9 reduce-scatter.4
  64.9 12.6 reduce-scatter.2
where the time goes:
time: 101 us; the launch traced here: 100 us
  waiting for transfers between devices  33.1 us (33%)
  starting transfers between devices  20.3 us (20%)
  between operations  14.9 us (15%)
  blocking collectives  12.3 us (12%)
  matrix products  11 us (11%)
  local copies, waits for them, and re-layouts  6.49 us (6%)
  other arithmetic  2.4 us (2%)
    reduce_scatter x1, waiting for transfers between devices, shared_rows(): lax.psum_scatter(partial_gradient.astype(jnp.bfloat16), 'dp', scatter_dim...  11.4 us
    reduce_scatter x1, waiting for transfers between devices, shared_rows(): lax.psum_scatter(part_out.astype(jnp.bfloat16), 'dp', scatter_dimension=0...  7.88 us
    all_to_all x1, waiting for transfers between devices, shards(): lax.all_to_all(send_in, 'expert', split_axis=0, concat_axis=0, tiled=True)  7.13 us
    all_to_all x1, waiting for transfers between devices, shards(): lax.all_to_all(half_out, 'expert', split_axis=0, concat_axis=0, tiled=True)  6.68 us
    all_to_all x1, starting transfers between devices, shards(): lax.all_to_all(send_in, 'expert', split_axis=0, concat_axis=0, tiled=True)  6.32 us
    all_gather x1, blocking collectives, shared_rows(): lax.all_gather(input_rows, 'dp', axis=0, tiled=True)  6.22 us
    all_gather x1, blocking collectives, shared_rows(): lax.all_gather(rows_cot, 'dp', axis=0, tiled=True)  6.08 us
    all_to_all x1, starting transfers between devices, shards(): lax.all_to_all(half_out, 'expert', split_axis=0, concat_axis=0, tiled=True)  4.61 us
  transfers between devices with their start and end apart: 7, of which 4 were waited for; matrix products, arithmetic and copies ran while one was open for 6% of the time, Pallas kernels for 0%

commit v1 on v0

v1 whole, which is shorter than its diff:
```python
import jax
import jax.numpy as jnp
from jax import lax
from jax.sharding import PartitionSpec as P


def rotate(shard, axis, by):
    count = lax.axis_size(axis)
    return lax.ppermute(shard, axis, [(i, (i + by) % count) for i in range(count)])


def flip(shard, axis):
    count = lax.axis_size(axis)
    return lax.ppermute(shard, axis, [(i, i ^ 1) for i in range(count)])


def from_behind(shard, axis, by):
    count = lax.axis_size(axis)
    pairs = [(i, i + by) for i in range(count) if 0 <= i + by < count]
    return lax.ppermute(shard, axis, pairs)


def rounded(x):
    return x.astype(jnp.bfloat16)


def dot(a, b, dims=(((1,), (0,)), ((), ()))):
    return lax.dot_general(a, b, dims, preferred_element_type=jnp.float32)


CROSS = (((1,), (1,)), ((), ()))


def gather_rows(hots, rows):
    cap = hots.shape[1]
    packed = [rounded(dot(hot, rows)) for hot in hots]
    parts = [packed[0]] + [rotate(packed[k], "expert", 2 * k) for k in range(1, len(packed))]
    own = jnp.concatenate(parts, axis=0)
    both = jnp.concatenate([own, flip(own, "expert")], axis=0)
    r = lax.axis_size("dp")
    return jnp.concatenate([both] + [rotate(both, "dp", k) for k in range(1, r)], axis=0)


def return_rows(partial, cap):
    r = lax.axis_size("dp")
    experts = lax.axis_size("expert") // 2
    blocks = partial.reshape(r, 2 * experts * cap, partial.shape[1])
    total = blocks[0].astype(jnp.float32)
    for k in range(1, r):
        total = total + rotate(blocks[k], "dp", -k).astype(jnp.float32)
    half = rounded(total).reshape(2, experts * cap, partial.shape[1])
    whole = rounded(half[0].astype(jnp.float32) + flip(half[1], "expert").astype(jnp.float32))
    whole = whole.reshape(experts, cap, partial.shape[1])
    back = [whole[0]] + [rotate(whole[k], "expert", -2 * k) for k in range(1, experts)]
    return jnp.concatenate(back, axis=0)


def shards(acts, cotangent, routes, probs, keep, w_gate, w_up, w_down):
    n_expert = lax.axis_size("expert")
    experts = n_expert // 2
    token_count, width = acts.shape
    top_count = routes.shape[1]
    capacity = 2 * ((token_count * top_count * 5 + 8 * experts - 1) // (8 * experts))
    pair_count = token_count * top_count
    chosen = routes.reshape(pair_count)
    weights = probs.reshape(pair_count)
    expert_hot = (chosen[:, None] == jnp.arange(experts, dtype=jnp.int32)[None, :]).astype(jnp.int32)
    ranks = jnp.cumsum(expert_hot, axis=0) - 1
    placed = jnp.sum(expert_hot * ranks, axis=1)
    mine = lax.axis_index("expert") // 2
    distance = (chosen - mine + experts) % experts
    slot = distance * capacity + placed
    slot_hot = slot[:, None] == jnp.arange(experts * capacity, dtype=jnp.int32)[None, :]
    owner = jnp.arange(pair_count, dtype=jnp.int32) // top_count
    token_hot = rounded(owner[:, None] == jnp.arange(token_count, dtype=jnp.int32)[None, :])
    hots = rounded(dot(rounded(slot_hot).T, token_hot)).reshape(experts, capacity, token_count)
    weighted_hot = jnp.where(slot_hot, weights[:, None], jnp.zeros((), jnp.bfloat16))
    spread = rounded(dot(token_hot.T, weighted_hot))

    gate_cols, up_cols, down_rows = w_gate[0, 0], w_up[0, 0], w_down[0, 0]
    rows_in = gather_rows(hots, acts)
    rows_cot = gather_rows(hots, cotangent)
    gate_pre = dot(rows_in, gate_cols)
    up_pre = dot(rows_in, up_cols)
    squash = jax.nn.sigmoid(gate_pre)
    hidden = rounded(gate_pre * squash * up_pre)
    part_out = rounded(dot(hidden, down_rows))
    grad_hidden = dot(rows_cot, down_rows, CROSS)
    grad_gate = rounded(grad_hidden * up_pre * squash * (1.0 + gate_pre * (1.0 - squash)))
    grad_up = rounded(grad_hidden * gate_pre * squash)
    part_grad = rounded(dot(grad_gate, gate_cols, CROSS) + dot(grad_up, up_cols, CROSS))
    expert_out = return_rows(part_out, capacity)
    expert_grad = return_rows(part_grad, capacity)
    keep_scale = keep[0, 0].astype(jnp.float32)
    layer_out = rounded(acts.astype(jnp.float32) + keep_scale * dot(spread, expert_out))
    section_grad = rounded(cotangent.astype(jnp.float32) + keep_scale * dot(spread, expert_grad))
    return layer_out, from_behind(section_grad, "pipe", -1)


def solution(mesh):
    rows = P(("pipe", "expert", "dp"), None)
    return jax.shard_map(
        shards,
        mesh=mesh,
        in_specs=(
            rows,
            rows,
            rows,
            rows,
            P("pipe", ("expert", "dp")),
            P("pipe", "expert", None, "dp"),
            P("pipe", "expert", None, "dp"),
            P("pipe", "expert", "dp", None),
        ),
        out_specs=(rows, rows),
        check_vma=False,
    )
```

time: 101 us -> 53.5 us (0.53)
  the two profiles are of different devices: /device:TPU:0 before, /device:TPU:1 now
where the time goes in v1:
time: 53.5 us; the launch traced here: 53.1 us
  starting transfers between devices  28.1 us (53%)
  waiting for transfers between devices  10.8 us (20%)
  matrix products  9.22 us (17%)
  other arithmetic  2.7 us (5%)
  between operations  1.57 us (3%)
  local copies, waits for them, and re-layouts  0.79 us (1%)
    ppermute x8, starting transfers between devices, rotate(): lax.ppermute(shard, axis, [(i, (i + by) % count) for i in range(count)])  15.4 us
    dot_general x14, matrix products, dot(): return lax.dot_general(a, b, dims, preferred_element_type=jnp.float32)  9.22 us
    ppermute x1, starting transfers between devices, from_behind(): return lax.ppermute(shard, axis, pairs)  8.3 us
    ppermute x8, waiting for transfers between devices, rotate(): lax.ppermute(shard, axis, [(i, (i + by) % count) for i in range(count)])  5.69 us
    ppermute x4, starting transfers between devices, flip(): return lax.ppermute(shard, axis, [(i, i ^ 1) for i in range(count)])  4.36 us
    ppermute x4, waiting for transfers between devices, flip(): return lax.ppermute(shard, axis, [(i, i ^ 1) for i in range(count)])  2.92 us
    ppermute x1, waiting for transfers between devices, from_behind(): return lax.ppermute(shard, axis, pairs)  2.16 us
  transfers between devices with their start and end apart: 13, of which 9 were waited for; matrix products, arithmetic and copies ran while one was open for 12% of the time, Pallas kernels for 0%

profile of v1, /device:TPU:1, one launch (start us, length us, event | category | flops | bytes accessed | tf_op | source)
XLA Modules:
  0.0 53.1 jit_solution(12336815010561433761)
XLA Ops:
  0.6 0.0 copy-start
  0.7 0.8 %fusion.41 = s32[8,2]{0,1:T(2,128)S(1)} fusion(s32[8]{0:T(128)} %bitcast.30), kind=kLoop, calls=%fused_computation.70 | loop fusion | flops 32 | bytes 96 | tf_op jit(solution)/shard_map/convert_element_type | solution.py:67
  1.4 0.2 reduce_window_sum.11
  1.6 0.7 %select_reduce_fusion = s32[8]{0:T(128)S(1)} fusion(s32[8,2]{0,1:T(2,128)S(1)} %reduce_window_sum.11, s32[8]{0:T(128)} %bitcast.31), kind=kLoop, calls=%fused_computation.68 | loop fusion | flops 56 | bytes 128 | tf_op jit(solution)/shard_map/reduce_sum | solution.py:69
  2.3 0.7 %fusion.45 = s32[8]{0:T(128)S(1)} fusion(s32[8]{0:T(128)S(1)} %select_reduce_fusion, s32[8,1]{0,1:T(1,128)} %param.10, s32[]{:T(128)S(6)} %select_n.20), kind=kLoop, calls=%fused_computation.74 | loop fusion | flops 120 | bytes 100 | tf_op jit(solution)/shard_map/eq | solution.py:73
  3.0 0.2 convolution_convert_fusion.6
  3.2 1.1 %convolution_convert_fusion.1 = bf16[6,3584]{1,0:T(8,128)(2,1)S(1)} fusion(bf16[8,3584]{1,0:T(8,128)(2,1)} %param.9, bf16[12,8]{0,1:T(8,128)(2,1)S(1)} %convolution_convert_fusion.6), kind=kOutput, calls=%fused_computation.9 | convolution fusion | flops 365568 | bytes 100544 | tf_op jit(solution)/shard_map/dot_general | solution.py:28
  4.3 3.2 %collective-permute-start.6 = (bf16[6,3584]{1,0:T(8,128)(2,1)S(1)}, bf16[6,3584]{1,0:T(8,128)(2,1)S(1)}, u32[]{:S(2)}, u32[]{:S(2)}) collective-permute-start(bf16[6,3584]{1,0:T(8,128)(2,1)S(1)} %convolution_convert_fusion.1), channel_id=1, source_target_pairs={{0,4},{2,6},{4,0},{6,2},{1,5},{3,7},{5,1},{7,3},{8,12},{10,14},{12... | collective-permute-start | bytes 129032 | tf_op jit(solution)/shard_map/ppermute | solution.py:9
  7.5 1.1 %convolution_convert_fusion.3 = bf16[6,3584]{1,0:T(8,128)(2,1)S(1)} fusion(bf16[8,3584]{1,0:T(8,128)(2,1)} %param.8, bf16[12,8]{0,1:T(8,128)(2,1)S(1)} %convolution_convert_fusion.6), kind=kOutput, calls=%fused_computation.11 | convolution fusion | flops 365568 | bytes 100544 | tf_op jit(solution)/shard_map/dot_general | solution.py:28
  8.6 0.1 collective-permute-start
  8.6 1.0 %convolution_convert_fusion.2 = bf16[6,3584]{1,0:T(8,128)(2,1)S(1)} fusion(bf16[8,3584]{1,0:T(8,128)(2,1)} %param.9, bf16[12,8]{0,1:T(8,128)(2,1)S(1)} %convolution_convert_fusion.6), kind=kOutput, calls=%fused_computation.10 | convolution fusion | flops 365568 | bytes 100544 | tf_op jit(solution)/shard_map/dot_general | solution.py:28
  9.7 1.0 %convolution_convert_fusion.4 = bf16[6,3584]{1,0:T(8,128)(2,1)S(1)} fusion(bf16[8,3584]{1,0:T(8,128)(2,1)} %param.8, bf16[12,8]{0,1:T(8,128)(2,1)S(1)} %convolution_convert_fusion.6), kind=kOutput, calls=%fused_computation.12 | convolution fusion | flops 365568 | bytes 100544 | tf_op jit(solution)/shard_map/dot_general | solution.py:28
  10.7 0.8 %convolution_convert_fusion.5 = bf16[8,12]{1,0:T(8,128)(2,1)S(1)} fusion(s32[8]{0:T(128)S(1)} %fusion.45, bf16[8]{0:T(256)(128)(2,1)} %bitcast.32), kind=kOutput, calls=%fused_computation.23 | convolution fusion | flops 1888 | bytes 240 | tf_op jit(solution)/shard_map/dot_general | solution.py:28
  12.2 0.0 copy-start.1
  12.2 0.3 collective-permute-done
  12.6 1.4 %collective-permute-start.1 = (bf16[12,3584]{1,0:T(8,128)(2,1)S(1)}, bf16[12,3584]{1,0:T(8,128)(2,1)S(1)}, u32[]{:S(2)}, u32[]{:S(2)}) collective-permute-start(bf16[12,3584]{1,0:T(8,128)(2,1)S(1)} %pad_maximum_fusion.3), channel_id=1, source_target_pairs={{0,2},{2,0},{4,6},{6,4},{1,3},{3,1},{5,7},{7,5},{8,10},{10,8},{12,... | collective-permute-start | bytes 258056 | tf_op jit(solution)/shard_map/ppermute | solution.py:14
  14.0 0.0 collective-permute-done.6
  14.0 0.2 collective-permute-start.7
  14.2 2.1 %collective-permute-done.1 = bf16[12,3584]{1,0:T(8,128)(2,1)S(1)} collective-permute-done((bf16[12,3584]{1,0:T(8,128)(2,1)S(1)}, bf16[12,3584]{1,0:T(8,128)(2,1)S(1)}, u32[]{:S(2)}, u32[]{:S(2)}) %collective-permute-start.1) | collective-permute-done | bytes 86048 | tf_op jit(solution)/shard_map/ppermute | solution.py:14
  16.3 0.1 pad_maximum_fusion.1
  16.4 1.3 %collective-permute-start.2 = (bf16[24,3584]{1,0:T(8,128)(2,1)S(1)}, bf16[24,3584]{1,0:T(8,128)(2,1)S(1)}, u32[]{:S(2)}, u32[]{:S(2)}) collective-permute-start(bf16[24,3584]{1,0:T(8,128)(2,1)S(1)} %pad_maximum_fusion.1), channel_id=1, source_target_pairs={{0,1},{1,0},{2,3},{3,2},{4,5},{5,4},{6,7},{7,6},{8,9},{9,8},{10,11... | collective-permute-start | bytes 516104 | tf_op jit(solution)/shard_map/ppermute | solution.py:9
  17.7 0.1 collective-permute-done.7
  17.7 0.1 pad_maximum_fusion.2
  17.8 0.0 copy-start.2
  17.8 1.3 %collective-permute-start.8 = (bf16[24,3584]{1,0:T(8,128)(2,1)S(1)}, bf16[24,3584]{1,0:T(8,128)(2,1)S(1)}, u32[]{:S(2)}, u32[]{:S(2)}) collective-permute-start(bf16[24,3584]{1,0:T(8,128)(2,1)S(1)} %pad_maximum_fusion.2), channel_id=1, source_target_pairs={{0,1},{1,0},{2,3},{3,2},{4,5},{5,4},{6,7},{7,6},{8,9},{9,8},{10,11... | collective-permute-start | bytes 516104 | tf_op jit(solution)/shard_map/ppermute | solution.py:9
  19.1 1.8 %collective-permute-done.2 = bf16[24,3584]{1,0:T(8,128)(2,1)S(1)} collective-permute-done((bf16[24,3584]{1,0:T(8,128)(2,1)S(1)}, bf16[24,3584]{1,0:T(8,128)(2,1)S(1)}, u32[]{:S(2)}, u32[]{:S(2)}) %collective-permute-start.2) | collective-permute-done | bytes 172064 | tf_op jit(solution)/shard_map/ppermute | solution.py:9
  20.9 0.0 copy-done
  20.9 0.4 fusion.13
  21.2 0.0 copy-done.1
  21.2 0.4 fusion.9
  21.6 0.9 %collective-permute-done.8 = bf16[24,3584]{1,0:T(8,128)(2,1)S(1)} collective-permute-done((bf16[24,3584]{1,0:T(8,128)(2,1)S(1)}, bf16[24,3584]{1,0:T(8,128)(2,1)S(1)}, u32[]{:S(2)}, u32[]{:S(2)}) %collective-permute-start.8) | collective-permute-done | bytes 172064 | tf_op jit(solution)/shard_map/ppermute | solution.py:9
  22.5 0.0 copy-done.2
  22.5 0.6 %fusion.5 = f32[48,256]{1,0:T(8,128)S(1)} fusion(bf16[1,1,256,3584]{3,2,1,0:T(8,128)(2,1)S(1)} %copy-done.2, bf16[24,3584]{1,0:T(8,128)(2,1)S(1)} %collective-permute-done.8, bf16[12,3584]{1,0:T(8,128)(2,1)S(1)} %collective-permute-done.7, bf16[6,3584]{1,0:T(8,128)(2,1)S(1)} %collective-permute-done.6, bf16[6,3584]{1,0:T(8,128)(2,1)S(1)} %convolution_convert_fusion.2), kind=kOutput, calls=%fused_computation.13 | convolution fusion | flops 89456640 | bytes 2228224 | tf_op jit(solution)/shard_map/dot_general | solution.py:28
  23.2 0.6 %fusion.11 = f32[48,3584]{1,0:T(8,128)S(1)} fusion(bf16[1,1,3584,256]{3,2,1,0:T(8,128)(2,1)S(1)} %copy-done, f32[48,256]{1,0:T(8,128)S(1)} %fusion.13, f32[48,256]{1,0:T(8,128)S(1)} %fusion.5, f32[48,256]{1,0:T(8,128)S(1)} %fusion.9), kind=kOutput, calls=%fused_computation.19 | convolution fusion | flops 88203264 | bytes 2670592 | tf_op jit(solution)/shard_map/dot_general | solution.py:28
  23.8 0.7 %fusion = bf16[48,3584]{1,0:T(8,128)(2,1)S(1)} fusion(f32[48,3584]{1,0:T(8,128)S(1)} %fusion.11, bf16[1,1,3584,256]{3,2,1,0:T(8,128)(2,1)S(1)} %copy-done.1, f32[48,256]{1,0:T(8,128)S(1)} %fusion.5, f32[48,256]{1,0:T(8,128)S(1)} %fusion.13), kind=kOutput, calls=%fused_computation.1 | convolution fusion | flops 88498176 | bytes 2965504 | tf_op jit(solution)/shard_map/dot_general | solution.py:28
  24.5 1.3 %collective-permute-start.9 = (bf16[24,3584]{1,0:T(8,128)(2,1)S(1)}, bf16[24,3584]{1,0:T(8,128)(2,1)S(1)}, u32[]{:S(2)}, u32[]{:S(2)}) collective-permute-start(bf16[24,3584]{1,0:T(8,128)(2,1)S(1)} %slice.69), channel_id=1, source_target_pairs={{0,1},{1,0},{2,3},{3,2},{4,5},{5,4},{6,7},{7,6},{8,9},{9,8},{10,11... | collective-permute-start | bytes 516104 | tf_op jit(solution)/shard_map/ppermute | solution.py:9
  25.8 0.4 convolution_convert_fusion
  26.2 0.0 copy-start.3
  26.2 0.0 copy-start.4
  26.2 0.3 collective-permute-start.3
  26.6 2.3 %collective-permute-done.9 = bf16[24,3584]{1,0:T(8,128)(2,1)S(1)} collective-permute-done((bf16[24,3584]{1,0:T(8,128)(2,1)S(1)}, bf16[24,3584]{1,0:T(8,128)(2,1)S(1)}, u32[]{:S(2)}, u32[]{:S(2)}) %collective-permute-start.9) | collective-permute-done | bytes 172064 | tf_op jit(solution)/shard_map/ppermute | solution.py:9
  28.9 1.4 %collective-permute-start.10 = (bf16[12,3584]{1,0:T(8,128)(2,1)S(1)}, bf16[12,3584]{1,0:T(8,128)(2,1)S(1)}, u32[]{:S(2)}, u32[]{:S(2)}) collective-permute-start(bf16[12,3584]{1,0:T(8,128)(2,1)S(1)} %slice.71), channel_id=1, source_target_pairs={{0,2},{2,0},{4,6},{6,4},{1,3},{3,1},{5,7},{7,5},{8,10},{10,8},{12,... | collective-permute-start | bytes 258056 | tf_op jit(solution)/shard_map/ppermute | solution.py:14
  30.3 0.4 collective-permute-done.3
  30.8 1.4 %collective-permute-start.4 = (bf16[12,3584]{1,0:T(8,128)(2,1)S(1)}, bf16[12,3584]{1,0:T(8,128)(2,1)S(1)}, u32[]{:S(2)}, u32[]{:S(2)}) collective-permute-start(bf16[12,3584]{1,0:T(8,128)(2,1)S(1)} %slice.65), channel_id=1, source_target_pairs={{0,2},{2,0},{4,6},{6,4},{1,3},{3,1},{5,7},{7,5},{8,10},{10,8},{12,... | collective-permute-start | bytes 258056 | tf_op jit(solution)/shard_map/ppermute | solution.py:14
  32.1 0.8 %collective-permute-done.10 = bf16[12,3584]{1,0:T(8,128)(2,1)S(1)} collective-permute-done((bf16[12,3584]{1,0:T(8,128)(2,1)S(1)}, bf16[12,3584]{1,0:T(8,128)(2,1)S(1)}, u32[]{:S(2)}, u32[]{:S(2)}) %collective-permute-start.10) | collective-permute-done | bytes 86048 | tf_op jit(solution)/shard_map/ppermute | solution.py:14
  33.0 5.6 %collective-permute-start.11 = (bf16[6,3584]{1,0:T(8,128)(2,1)S(1)}, bf16[6,3584]{1,0:T(8,128)(2,1)S(1)}, u32[]{:S(2)}, u32[]{:S(2)}) collective-permute-start(bf16[6,3584]{1,0:T(8,128)(2,1)S(1)} %get-tuple-element.3), channel_id=1, source_target_pairs={{0,4},{2,6},{4,0},{6,2},{1,5},{3,7},{5,1},{7,3},{8,12},{10,14},{12... | collective-permute-start | bytes 129032 | tf_op jit(solution)/shard_map/ppermute | solution.py:9
  38.6 0.0 collective-permute-done.4
  38.7 2.4 %collective-permute-start.5 = (bf16[6,3584]{1,0:T(8,128)(2,1)S(1)}, bf16[6,3584]{1,0:T(8,128)(2,1)S(1)}, u32[]{:S(2)}, u32[]{:S(2)}) collective-permute-start(bf16[6,3584]{1,0:T(8,128)(2,1)S(1)} %get-tuple-element.5), channel_id=1, source_target_pairs={{0,4},{2,6},{4,0},{6,2},{1,5},{3,7},{5,1},{7,3},{8,12},{10,14},{12... | collective-permute-start | bytes 129032 | tf_op jit(solution)/shard_map/ppermute | solution.py:9
  41.0 0.0 collective-permute-done.11
  41.0 0.0 copy-done.3
  41.0 0.2 fusion.4
  41.2 8.3 %collective-permute-start.12 = (bf16[8,3584]{1,0:T(8,128)(2,1)S(1)}, bf16[8,3584]{1,0:T(8,128)(2,1)S(1)}, u32[]{:S(2)}, u32[]{:S(2)}) collective-permute-start(bf16[8,3584]{1,0:T(8,128)(2,1)S(1)} %fusion.4), channel_id=1, source_target_pairs={{8,0},{16,8},{24,16},{9,1},{17,9},{25,17},{10,2},{18,10},{26,18},{... | collective-permute-start | bytes 172040 | tf_op jit(solution)/shard_map/ppermute | solution.py:20
  49.5 0.0 collective-permute-done.5
  49.5 0.0 copy-done.4
  49.5 0.8 %fusion.3 = bf16[8,3584]{1,0:T(8,128)(2,1)} fusion(bf16[8,12]{1,0:T(8,128)(2,1)S(1)} %convolution_convert_fusion.5, bf16[6,3584]{1,0:T(8,128)(2,1)S(1)} %collective-permute-done.5, bf16[6,3584]{1,0:T(8,128)(2,1)S(1)} %get-tuple-element.4, bf16[8,3584]{1,0:T(8,128)(2,1)S(1)} %copy-done.4, f32[]{:T(128)} %bitcast), kind=kOutput, calls=%fused_computation.7 | convolution fusion | flops 974848 | bytes 200900 | tf_op jit(solution)/shard_map/dot_general | solution.py:28
  50.3 2.2 %collective-permute-done.12 = bf16[8,3584]{1,0:T(8,128)(2,1)S(1)} collective-permute-done((bf16[8,3584]{1,0:T(8,128)(2,1)S(1)}, bf16[8,3584]{1,0:T(8,128)(2,1)S(1)}, u32[]{:S(2)}, u32[]{:S(2)}) %collective-permute-start.12) | collective-permute-done | bytes 57376 | tf_op jit(solution)/shard_map/ppermute | solution.py:20
  52.5 0.6 %copy.12 = bf16[8,3584]{1,0:T(8,128)(2,1)} copy(bf16[8,3584]{1,0:T(8,128)(2,1)S(1)} %collective-permute-done.12) | data formatting | bytes 114688
  (12 shorter events, 0.4 us)
Async XLA Ops:
  0.6 20.2 %copy-start = (bf16[1,1,3584,256]{3,2,1,0:T(8,128)(2,1)S(1)}, bf16[1,1,3584,256]{3,2,1,0:T(8,128)(2,1)}, u32[]{:S(2)}) copy-start(bf16[1,1,3584,256]{3,2,1,0:T(8,128)(2,1)} %param.13) | copy-start | bytes 5505028
  4.3 9.7 %collective-permute-start.6 = (bf16[6,3584]{1,0:T(8,128)(2,1)S(1)}, bf16[6,3584]{1,0:T(8,128)(2,1)S(1)}, u32[]{:S(2)}, u32[]{:S(2)}) collective-permute-start(bf16[6,3584]{1,0:T(8,128)(2,1)S(1)} %convolution_convert_fusion.1), channel_id=1, source_target_pairs={{0,4},{2,6},{4,0},{6,2},{1,5},{3,7},{5,1},{7,3},{8,12},{10,14},{12... | collective-permute-start | bytes 129032 | tf_op jit(solution)/shard_map/ppermute | solution.py:9
  8.6 4.0 %collective-permute-start = (bf16[6,3584]{1,0:T(8,128)(2,1)S(1)}, bf16[6,3584]{1,0:T(8,128)(2,1)S(1)}, u32[]{:S(2)}, u32[]{:S(2)}) collective-permute-start(bf16[6,3584]{1,0:T(8,128)(2,1)S(1)} %convolution_convert_fusion.3), channel_id=1, source_target_pairs={{0,4},{2,6},{4,0},{6,2},{1,5},{3,7},{5,1},{7,3},{8,12},{10,14},{12... | collective-permute-start | bytes 129032 | tf_op jit(solution)/shard_map/ppermute | solution.py:9
  12.2 9.0 %copy-start.1 = (bf16[1,1,3584,256]{3,2,1,0:T(8,128)(2,1)S(1)}, bf16[1,1,3584,256]{3,2,1,0:T(8,128)(2,1)}, u32[]{:S(2)}) copy-start(bf16[1,1,3584,256]{3,2,1,0:T(8,128)(2,1)} %param.14) | copy-start | bytes 5505028
  12.6 3.7 %collective-permute-start.1 = (bf16[12,3584]{1,0:T(8,128)(2,1)S(1)}, bf16[12,3584]{1,0:T(8,128)(2,1)S(1)}, u32[]{:S(2)}, u32[]{:S(2)}) collective-permute-start(bf16[12,3584]{1,0:T(8,128)(2,1)S(1)} %pad_maximum_fusion.3), channel_id=1, source_target_pairs={{0,2},{2,0},{4,6},{6,4},{1,3},{3,1},{5,7},{7,5},{8,10},{10,8},{12,... | collective-permute-start | bytes 258056 | tf_op jit(solution)/shard_map/ppermute | solution.py:14
  14.0 3.7 %collective-permute-start.7 = (bf16[12,3584]{1,0:T(8,128)(2,1)S(1)}, bf16[12,3584]{1,0:T(8,128)(2,1)S(1)}, u32[]{:S(2)}, u32[]{:S(2)}) collective-permute-start(bf16[12,3584]{1,0:T(8,128)(2,1)S(1)} %pad_maximum_fusion.4), channel_id=1, source_target_pairs={{0,2},{2,0},{4,6},{6,4},{1,3},{3,1},{5,7},{7,5},{8,10},{10,8},{12,... | collective-permute-start | bytes 258056 | tf_op jit(solution)/shard_map/ppermute | solution.py:14
  16.4 4.5 %collective-permute-start.2 = (bf16[24,3584]{1,0:T(8,128)(2,1)S(1)}, bf16[24,3584]{1,0:T(8,128)(2,1)S(1)}, u32[]{:S(2)}, u32[]{:S(2)}) collective-permute-start(bf16[24,3584]{1,0:T(8,128)(2,1)S(1)} %pad_maximum_fusion.1), channel_id=1, source_target_pairs={{0,1},{1,0},{2,3},{3,2},{4,5},{5,4},{6,7},{7,6},{8,9},{9,8},{10,11... | collective-permute-start | bytes 516104 | tf_op jit(solution)/shard_map/ppermute | solution.py:9
  17.8 4.7 %copy-start.2 = (bf16[1,1,256,3584]{3,2,1,0:T(8,128)(2,1)S(1)}, bf16[1,1,256,3584]{3,2,1,0:T(8,128)(2,1)}, u32[]{:S(2)}) copy-start(bf16[1,1,256,3584]{3,2,1,0:T(8,128)(2,1)} %param.15) | copy-start | bytes 5505028
  17.8 4.7 %collective-permute-start.8 = (bf16[24,3584]{1,0:T(8,128)(2,1)S(1)}, bf16[24,3584]{1,0:T(8,128)(2,1)S(1)}, u32[]{:S(2)}, u32[]{:S(2)}) collective-permute-start(bf16[24,3584]{1,0:T(8,128)(2,1)S(1)} %pad_maximum_fusion.2), channel_id=1, source_target_pairs={{0,1},{1,0},{2,3},{3,2},{4,5},{5,4},{6,7},{7,6},{8,9},{9,8},{10,11... | collective-permute-start | bytes 516104 | tf_op jit(solution)/shard_map/ppermute | solution.py:9
  24.5 4.3 %collective-permute-start.9 = (bf16[24,3584]{1,0:T(8,128)(2,1)S(1)}, bf16[24,3584]{1,0:T(8,128)(2,1)S(1)}, u32[]{:S(2)}, u32[]{:S(2)}) collective-permute-start(bf16[24,3584]{1,0:T(8,128)(2,1)S(1)} %slice.69), channel_id=1, source_target_pairs={{0,1},{1,0},{2,3},{3,2},{4,5},{5,4},{6,7},{7,6},{8,9},{9,8},{10,11... | collective-permute-start | bytes 516104 | tf_op jit(solution)/shard_map/ppermute | solution.py:9
  26.2 14.9 %copy-start.3 = (bf16[8,3584]{1,0:T(8,128)(2,1)S(1)}, bf16[8,3584]{1,0:T(8,128)(2,1)}, u32[]{:S(2)}) copy-start(bf16[8,3584]{1,0:T(8,128)(2,1)} %param.9) | copy-start | bytes 172036
  26.2 23.3 %copy-start.4 = (bf16[8,3584]{1,0:T(8,128)(2,1)S(1)}, bf16[8,3584]{1,0:T(8,128)(2,1)}, u32[]{:S(2)}) copy-start(bf16[8,3584]{1,0:T(8,128)(2,1)} %param.8) | copy-start | bytes 172036
  26.2 4.4 %collective-permute-start.3 = (bf16[24,3584]{1,0:T(8,128)(2,1)S(1)}, bf16[24,3584]{1,0:T(8,128)(2,1)S(1)}, u32[]{:S(2)}, u32[]{:S(2)}) collective-permute-start(bf16[24,3584]{1,0:T(8,128)(2,1)S(1)} %slice.63), channel_id=1, source_target_pairs={{0,1},{1,0},{2,3},{3,2},{4,5},{5,4},{6,7},{7,6},{8,9},{9,8},{10,11... | collective-permute-start | bytes 516104 | tf_op jit(solution)/shard_map/ppermute | solution.py:9
  28.9 4.0 %collective-permute-start.10 = (bf16[12,3584]{1,0:T(8,128)(2,1)S(1)}, bf16[12,3584]{1,0:T(8,128)(2,1)S(1)}, u32[]{:S(2)}, u32[]{:S(2)}) collective-permute-start(bf16[12,3584]{1,0:T(8,128)(2,1)S(1)} %slice.71), channel_id=1, source_target_pairs={{0,2},{2,0},{4,6},{6,4},{1,3},{3,1},{5,7},{7,5},{8,10},{10,8},{12,... | collective-permute-start | bytes 258056 | tf_op jit(solution)/shard_map/ppermute | solution.py:14
  30.8 7.8 %collective-permute-start.4 = (bf16[12,3584]{1,0:T(8,128)(2,1)S(1)}, bf16[12,3584]{1,0:T(8,128)(2,1)S(1)}, u32[]{:S(2)}, u32[]{:S(2)}) collective-permute-start(bf16[12,3584]{1,0:T(8,128)(2,1)S(1)} %slice.65), channel_id=1, source_target_pairs={{0,2},{2,0},{4,6},{6,4},{1,3},{3,1},{5,7},{7,5},{8,10},{10,8},{12,... | collective-permute-start | bytes 258056 | tf_op jit(solution)/shard_map/ppermute | solution.py:14
  33.0 8.1 %collective-permute-start.11 = (bf16[6,3584]{1,0:T(8,128)(2,1)S(1)}, bf16[6,3584]{1,0:T(8,128)(2,1)S(1)}, u32[]{:S(2)}, u32[]{:S(2)}) collective-permute-start(bf16[6,3584]{1,0:T(8,128)(2,1)S(1)} %get-tuple-element.3), channel_id=1, source_target_pairs={{0,4},{2,6},{4,0},{6,2},{1,5},{3,7},{5,1},{7,3},{8,12},{10,14},{12... | collective-permute-start | bytes 129032 | tf_op jit(solution)/shard_map/ppermute | solution.py:9
  38.7 10.9 %collective-permute-start.5 = (bf16[6,3584]{1,0:T(8,128)(2,1)S(1)}, bf16[6,3584]{1,0:T(8,128)(2,1)S(1)}, u32[]{:S(2)}, u32[]{:S(2)}) collective-permute-start(bf16[6,3584]{1,0:T(8,128)(2,1)S(1)} %get-tuple-element.5), channel_id=1, source_target_pairs={{0,4},{2,6},{4,0},{6,2},{1,5},{3,7},{5,1},{7,3},{8,12},{10,14},{12... | collective-permute-start | bytes 129032 | tf_op jit(solution)/shard_map/ppermute | solution.py:9
  41.2 11.3 %collective-permute-start.12 = (bf16[8,3584]{1,0:T(8,128)(2,1)S(1)}, bf16[8,3584]{1,0:T(8,128)(2,1)S(1)}, u32[]{:S(2)}, u32[]{:S(2)}) collective-permute-start(bf16[8,3584]{1,0:T(8,128)(2,1)S(1)} %fusion.4), channel_id=1, source_target_pairs={{8,0},{16,8},{24,16},{9,1},{17,9},{25,17},{10,2},{18,10},{26,18},{... | collective-permute-start | bytes 172040 | tf_op jit(solution)/shard_map/ppermute | solution.py:20

commit v2 on v1

v2 whole, which is shorter than its diff:
```python
import functools

import jax
import jax.numpy as jnp
from jax import lax
from jax.experimental import pallas as pl
from jax.experimental.pallas import tpu as pltpu
from jax.sharding import PartitionSpec as P

CROSS = (((1,), (1,)), ((), ()))
LANES = 128
TILE = 4
MIB = 1024 * 1024


def room(mib):
    return pltpu.CompilerParams(vmem_limit_bytes=mib * MIB)


def rounded(x):
    return x.astype(jnp.bfloat16)


def in_hbm(x):
    return pltpu.with_memory_space_constraint(x, pltpu.HBM)


def near_core(x):
    return pltpu.with_memory_space_constraint(x, pltpu.VMEM)


def dot(a, b, dims=(((1,), (0,)), ((), ()))):
    return lax.dot_general(a, b, dims, preferred_element_type=jnp.float32)


def to_member(shard, half, by):
    n, r = lax.axis_size("expert"), lax.axis_size("dp")
    pairs = [(e * r + d, (e ^ half) * r + (d + by) % r) for e in range(n) for d in range(r)]
    return lax.ppermute(shard, ("expert", "dp"), pairs)


def to_expert(shard, by):
    n = lax.axis_size("expert")
    return lax.ppermute(shard, "expert", [(e, (e + 2 * by) % n) for e in range(n)])


def to_below(shard):
    return lax.ppermute(shard, "pipe", [(p, p - 1) for p in range(1, lax.axis_size("pipe"))])


def pack_kernel(experts, cap, top, *refs):
    keep, stored, mix_out, blocks = refs[0], refs[1:5], refs[5], refs[6 : 6 + experts]
    held, sems = refs[6 + experts : -1], refs[-1]
    copies = [pltpu.make_async_copy(s, h, sems.at[i]) for i, (s, h) in enumerate(zip(stored, held))]
    for copy in copies:
        copy.start()
    routes, probs, acts, cot = held
    pairs = routes.shape[1]
    tokens = pairs // top
    copies[0].wait()
    chosen = jnp.broadcast_to(routes[...], (pairs, pairs))
    p = lax.broadcasted_iota(jnp.int32, (pairs, pairs), 0)
    q = lax.broadcasted_iota(jnp.int32, (pairs, pairs), 1)
    column = jnp.sum(jnp.where(p == q, chosen, 0), axis=1, keepdims=True)
    alike = column == chosen
    mine = lax.axis_index("expert") // 2

    def slot_of(expert, rank):
        far = expert - mine
        return jnp.where(far < 0, far + experts, far) * (2 * cap) + rank

    row_slot = slot_of(routes[...], jnp.sum(jnp.where(alike & (p < q), 1, 0), axis=0, keepdims=True))
    col_slot = slot_of(column, jnp.sum(jnp.where(alike & (q < p), 1, 0), axis=1, keepdims=True))
    slot = lax.broadcasted_iota(jnp.int32, (2 * experts * cap, pairs), 0)
    scatter = [jnp.where(slot == row_slot + t * cap, 1.0, 0.0) for t in range(2)]
    owner = None
    if top > 1:
        owner = lax.broadcasted_iota(jnp.int32, (tokens, pairs), 1) // top
        owner = rounded(jnp.where(owner == lax.broadcasted_iota(jnp.int32, (tokens, pairs), 0), 1.0, 0.0))
        scatter = [dot(rounded(s), owner, CROSS) for s in scatter]
    copies[2].wait()
    packed = dot(rounded(scatter[0]), acts[...])
    copies[3].wait()
    packed = rounded(packed + dot(rounded(scatter[1]), cot[...]))
    tiles = blocks[0].shape[0]
    for k, block in enumerate(blocks):
        for i in range(tiles):
            at = (k * tiles + i) * TILE
            block[i] = packed[at : at + TILE]
    copies[1].wait()
    weight = jnp.broadcast_to(probs[...].astype(jnp.float32) * keep[...].astype(jnp.float32), (pairs, pairs))
    weight = jnp.sum(jnp.where(p == q, weight, 0.0), axis=1, keepdims=True)
    slot = lax.broadcasted_iota(jnp.int32, (pairs, LANES), 1)
    for t in range(2):
        mix = jnp.where(slot == col_slot + t * cap, weight, 0.0)
        mix_out[t] = mix if owner is None else dot(owner, rounded(mix))


def fill(rows, at, ins, first, deep, tiles):
    spots = [(ref, b + first + i) for ref in ins for b in range(0, ref.shape[0], tiles) for i in range(deep)]
    for i in range(0, len(spots), 2):
        pair = [ref[b] for ref, b in spots[i : i + 2]]
        rows[at + i * TILE : at + (i + 2) * TILE] = jnp.concatenate(pair, axis=0)


def near_kernel(cap, count, *refs):
    stored, ins, (acts, cot), held, sems = refs[:3], refs[3 : 3 + count], refs[3 + count : 5 + count], refs[5 + count : -1], refs[-1]
    copies = [pltpu.make_async_copy(s, h, sems.at[i]) for i, (s, h) in enumerate(zip(stored, held))]
    for copy in copies:
        copy.start()
    deep, tiles = -(-cap // TILE), 2 * cap // TILE
    fill(acts, 0, ins, 0, deep, tiles)
    fill(cot, 0, ins, tiles - deep, deep, tiles)
    for copy in copies:
        copy.wait()


def expert_kernel(cap, count, w_gate, w_up, w_down, acts_in, cot_in, *refs):
    ins, outs, (acts, cot) = refs[:count], refs[count : 3 * count], refs[3 * count :]
    width = acts.shape[1]
    tiles = 2 * cap // TILE
    deep = -(-cap // TILE)
    lead = deep * TILE - cap
    places = [(out, b) for out in outs for b in range(0, out.shape[0], tiles)]
    tall = len(places) * deep * TILE
    near = count * deep * TILE
    fill(acts, near, ins, 0, deep, tiles)
    fill(cot, near, ins, tiles - deep, deep, tiles)
    gate_pre = dot(acts[...], w_gate[...])
    up_pre = dot(acts[...], w_up[...])
    grad_hidden = dot(cot[...], w_down[...], CROSS)
    if lead:
        grad_hidden = pltpu.roll(grad_hidden, tall - lead, 0)
    live = lax.broadcasted_iota(jnp.int32, gate_pre.shape, 0) % (deep * TILE) < cap
    squash = jax.nn.sigmoid(gate_pre)
    silu = gate_pre * squash
    hidden = rounded(jnp.where(live, silu * up_pre, 0.0))
    grad_gate = jnp.where(live, grad_hidden * up_pre * squash * (1.0 + gate_pre * (1.0 - squash)), 0.0)
    grad_up = jnp.where(live, grad_hidden * silu, 0.0)
    if lead:
        grad_gate, grad_up = pltpu.roll(grad_gate, lead, 0), pltpu.roll(grad_up, lead, 0)
    grad_gate, grad_up = rounded(grad_gate), rounded(grad_up)
    step = 512
    for at in range(0, width, step):
        cols = slice(at, at + step)
        out = dot(hidden, w_down[:, cols])
        grad = dot(grad_gate, w_gate[cols, :], CROSS) + dot(grad_up, w_up[cols, :], CROSS)
        for n, (ref, b) in enumerate(places):
            base = n * deep * TILE
            for i in range(tiles):
                parts = []
                if i < deep:
                    parts.append(out[base + i * TILE : base + (i + 1) * TILE])
                if i >= tiles - deep:
                    j = i - (tiles - deep)
                    parts.append(grad[base + j * TILE : base + (j + 1) * TILE])
                ref[b + i, :, cols] = rounded(sum(parts))


def sum_kernel(*refs):
    total = refs[0][...].astype(jnp.float32)
    for ref in refs[1:-1]:
        total = total + ref[...].astype(jnp.float32)
    refs[-1][...] = rounded(total)


def finish_kernel(which, cap, count, mix, base, *refs):
    own, back, result = refs[:count], refs[count:-1], refs[-1]
    tiles, deep = 2 * cap // TILE, -(-cap // TILE)
    total = base[...].astype(jnp.float32)
    weights = rounded(mix[which])
    for i in range(deep) if which == 0 else range(tiles - deep, tiles):
        rows = own[0][i].astype(jnp.float32)
        for ref in own[1:]:
            rows = rows + ref[i].astype(jnp.float32)
        for k, rows in enumerate([rounded(rows)] + [ref[i] for ref in back]):
            at = (k * tiles + i) * TILE
            total = total + dot(weights[:, at : at + TILE], rows)
    result[...] = rounded(total)


def shards(acts, cotangent, routes, probs, keep, w_gate, w_up, w_down):
    experts = lax.axis_size("expert") // 2
    r = lax.axis_size("dp")
    token_count, width = acts.shape
    top = routes.shape[1]
    capacity = 2 * ((token_count * top * 5 + 8 * experts - 1) // (8 * experts))
    pairs = token_count * top
    tiles = 2 * capacity // TILE
    hidden = w_gate.shape[-1]
    shape = jax.ShapeDtypeStruct
    block = pltpu.VMEM((tiles, TILE, width), jnp.bfloat16)
    rest = pltpu.VMEM(((experts - 1) * tiles, TILE, width), jnp.bfloat16)
    far_off, vmem = pl.BlockSpec(memory_space=pltpu.HBM), pl.BlockSpec(memory_space=pltpu.VMEM)
    inputs = (routes.reshape(1, pairs), probs.reshape(1, pairs), acts, cotangent)
    mix, *sent = pl.pallas_call(
        functools.partial(pack_kernel, experts, capacity, top),
        in_specs=[vmem] + [far_off] * 4,
        out_specs=[vmem] * (1 + experts),
        out_shape=[pltpu.VMEM((2, token_count, LANES), jnp.float32)] + [block] * experts,
        scratch_shapes=[pltpu.VMEM(x.shape, x.dtype) for x in inputs] + [pltpu.SemaphoreType.DMA((4,))],
        compiler_params=room(4),
        name="pack",
    )(keep, *map(in_hbm, inputs))

    members = [(half, by) for half in range(2) for by in range(r)]
    near = [sent[0]]
    got = [to_expert(sent[k], k) for k in range(1, experts)]
    near += [to_member(sent[0], half, by) for half, by in members[1:]]
    got = got[0] if experts == 2 else jnp.concatenate(got, axis=0)
    far = [got] + [to_member(got, half, by) for half, by in members[1:]]
    weights = (w_gate.reshape(width, hidden), w_up.reshape(width, hidden), w_down.reshape(hidden, width))
    tall = experts * 2 * r * (-(-capacity // TILE)) * TILE
    count = len(members)
    laid = pltpu.VMEM((tall, width), jnp.bfloat16)
    acts_rows, cot_rows, *held = pl.pallas_call(
        functools.partial(near_kernel, capacity, count),
        in_specs=[far_off] * 3 + [vmem] * count,
        out_specs=[vmem] * 5,
        out_shape=[laid] * 2 + [pltpu.VMEM(w.shape, w.dtype) for w in weights],
        scratch_shapes=[pltpu.SemaphoreType.DMA((3,))],
        compiler_params=room(4),
        name="near",
    )(*map(in_hbm, weights), *map(near_core, near))
    *parts, _, _ = pl.pallas_call(
        functools.partial(expert_kernel, capacity, count),
        in_specs=[vmem] * (5 + count),
        out_specs=[vmem] * (2 * count + 2),
        out_shape=[block] * count + [rest] * count + [laid] * 2,
        input_output_aliases={3: 2 * count, 4: 2 * count + 1},
        compiler_params=room(8),
        name="expert",
    )(*map(near_core, (*held, acts_rows, cot_rows, *far)))
    near, far = parts[:count], parts[count:]
    far = [far[0]] + [to_member(x, half, -by) for x, (half, by) in zip(far[1:], members[1:])]
    near = [near[0]] + [to_member(x, half, -by) for x, (half, by) in zip(near[1:], members[1:])]
    total = pl.pallas_call(sum_kernel, out_shape=rest, compiler_params=room(4), name="total")(*map(near_core, far))
    back = [to_expert(total[(k - 1) * tiles : k * tiles], -k) for k in range(1, experts)]
    layer_out, section_grad = [
        pl.pallas_call(
            functools.partial(finish_kernel, which, capacity, count),
            out_shape=shape(acts.shape, jnp.bfloat16) if which == 0 else pltpu.VMEM(acts.shape, jnp.bfloat16),
            compiler_params=room(4),
            name=name,
        )(*map(near_core, (mix, base, *near, *back)))
        for which, name, base in ((0, "out", acts), (1, "grad", cotangent))
    ]
    return layer_out, to_below(section_grad)


def solution(mesh):
    rows = P(("pipe", "expert", "dp"), None)
    return jax.shard_map(
        shards,
        mesh=mesh,
        in_specs=(
            rows,
            rows,
            rows,
            rows,
            P("pipe", ("expert", "dp")),
            P("pipe", "expert", None, "dp"),
            P("pipe", "expert", None, "dp"),
            P("pipe", "expert", "dp", None),
        ),
        out_specs=(rows, rows),
        check_vma=False,
    )
```

time: 53.5 us -> 43.4 us (0.81)
  matrix products: 9.22 us -> 0 us
  Pallas kernels: 0 us -> 8.8 us
  waiting for transfers between devices: 10.8 us -> 6.9 us
  other arithmetic: 2.7 us -> 0 us
  starting transfers between devices: 28.1 us -> 25.6 us
    dot_general x14 -> x0, matrix products: 9.22 us -> none  [dot(): return lax.dot_general(a, b, dims, preferred_element_type=jnp.float32)]
    pallas_call x0 -> x6, Pallas kernels: none -> 8.8 us  [the longest x1 3.55 us: shards(): pl.pallas_call(functools.partial(expert_kernel, capacity, count), in_spec...]
    ppermute x13 -> x15, waiting for transfers between devices: 10.8 us -> 6.9 us  [the longest x12 2.72 us: to_member(): return lax.ppermute(shard, ('expert', 'dp'), pairs)]
    ppermute x13 -> x15, starting transfers between devices: 28.1 us -> 25.6 us  [the longest x12 11.7 us: to_member(): return lax.ppermute(shard, ('expert', 'dp'), pairs)]
    convert_element_type x5 -> x0, other arithmetic: 0.94 us -> none  [the longest x1 0.79 us: shards(): (chosen[:, None] == jnp.arange(experts, dtype=jnp.int32)[None, :]).astype...]
    reduce_sum x1 -> x0, other arithmetic: 0.67 us -> none  [shards(): placed = jnp.sum(expert_hot * ranks, axis=1)]
    eq x1 -> x0, other arithmetic: 0.67 us -> none  [shards(): slot[:, None] == jnp.arange(experts * capacity, dtype=jnp.int32)[None, :]]
  transfers between devices with their start and end apart: 13 -> 15, of which waited for: 9 -> 6; matrix products, arithmetic and copies ran while one was open for 12% -> 0% of each run, Pallas kernels for 0% -> 8%
where the time goes in v2:
time: 43.4 us; the launch traced here: 43.3 us
  starting transfers between devices  25.6 us (59%)
  Pallas kernels  8.8 us (20%)
  waiting for transfers between devices  6.9 us (16%)
  between operations  1.35 us (3%)
  local copies, waits for them, and re-layouts  0.63 us (1%)
    ppermute x12, starting transfers between devices, to_member(): return lax.ppermute(shard, ('expert', 'dp'), pairs)  11.7 us
    ppermute x2, starting transfers between devices, to_expert(): lax.ppermute(shard, 'expert', [(e, (e + 2 * by) % n) for e in range(n)])  7.06 us
    ppermute x1, starting transfers between devices, to_below(): lax.ppermute(shard, 'pipe', [(p, p - 1) for p in range(1, lax.axis_size('...  6.77 us
    pallas_call x1, Pallas kernels, shards(): pl.pallas_call(functools.partial(expert_kernel, capacity, count), in_spec...  3.55 us
    ppermute x12, waiting for transfers between devices, to_member(): return lax.ppermute(shard, ('expert', 'dp'), pairs)  2.72 us
    pallas_call x1, Pallas kernels, shards(): pl.pallas_call(functools.partial(near_kernel, capacity, count), in_specs=...  2.63 us
    ppermute x2, waiting for transfers between devices, to_expert(): lax.ppermute(shard, 'expert', [(e, (e + 2 * by) % n) for e in range(n)])  2.13 us
    ppermute x1, waiting for transfers between devices, to_below(): lax.ppermute(shard, 'pipe', [(p, p - 1) for p in range(1, lax.axis_size('...  2.05 us
  transfers between devices with their start and end apart: 15, of which 6 were waited for; matrix products, arithmetic and copies ran while one was open for 0% of the time, Pallas kernels for 8%

profile of v2, /device:TPU:1, one launch (start us, length us, event | category | flops | bytes accessed | tf_op | source)
XLA Modules:
  0.0 43.3 jit_solution(4028653882055745958)
XLA Ops:
  1.3 1.3 %pack.1 = (f32[2,8,128]{2,1,0:T(8,128)S(1)}, bf16[3,4,3584]{2,1,0:T(4,128)(2,1)S(1)}, bf16[3,4,3584]{2,1,0:T(4,128)(2,1)S(1)}) custom-call(s32[1,1]{1,0:T(1,128)S(6)} %copy.15.refs_0_, s32[1,8]{1,0:T(1,128)} %bitcast.8, bf16[1,8]{1,0:T(2,128)(2,1)} %bitcast.9, bf16[8,3584]{1,0:T(8,128)(2,1)} %base.2, bf16[8,3584]{1,0:T(8,128)(2,1)} %base.3), custom_call_target="tpu_custom_call" | custom-call | tf_op jit(solution)/shard_map/pack/pallas_call | solution.py:196
  2.6 3.2 %collective-permute-start.3 = (bf16[3,4,3584]{2,1,0:T(4,128)(2,1)S(1)}, bf16[3,4,3584]{2,1,0:T(4,128)(2,1)S(1)}, u32[]{:S(2)}, u32[]{:S(2)}) collective-permute-start(bf16[3,4,3584]{2,1,0:T(4,128)(2,1)S(1)} %get-tuple-element.25), channel_id=1, source_target_pairs={{0,4},{2,6},{4,0},{6,2},{1,5},{3,7},{5,1},{7,3},{8,12},{10,14},{12... | collective-permute-start | bytes 258056 | tf_op jit(solution)/shard_map/ppermute | solution.py:44
  5.8 2.2 %collective-permute-start.2 = (bf16[3,4,3584]{2,1,0:T(4,128)(2,1)S(1)}, bf16[3,4,3584]{2,1,0:T(4,128)(2,1)S(1)}, u32[]{:S(2)}, u32[]{:S(2)}) collective-permute-start(bf16[3,4,3584]{2,1,0:T(4,128)(2,1)S(1)} %get-tuple-element.19.refs_3_), channel_id=1, source_target_pairs={{0,3},{1,2},{2,1},{3,0},{4,7},{5,6},{6,5},{7,4},{8,11},{9,10},{10,... | collective-permute-start | bytes 258056 | tf_op jit(solution)/shard_map/ppermute | solution.py:39
  8.0 0.2 collective-permute-start.1
  8.2 0.2 collective-permute-start
  8.4 0.0 collective-permute-done.3.refs_0_
  8.5 3.3 %collective-permute-start.6 = (bf16[3,4,3584]{2,1,0:T(4,128)(2,1)S(1)}, bf16[3,4,3584]{2,1,0:T(4,128)(2,1)S(1)}, u32[]{:S(2)}, u32[]{:S(2)}) collective-permute-start(bf16[3,4,3584]{2,1,0:T(4,128)(2,1)S(1)} %collective-permute-done.3.refs_0_), channel_id=1, source_target_pairs={{0,3},{1,2},{2,1},{3,0},{4,7},{5,6},{6,5},{7,4},{8,11},{9,10},{10,... | collective-permute-start | bytes 258056 | tf_op jit(solution)/shard_map/ppermute | solution.py:39
  11.8 0.0 collective-permute-start.5
  11.8 0.0 collective-permute-done.2.refs_6_
  11.8 0.4 collective-permute-start.4
  12.2 0.4 collective-permute-done.1.refs_5_
  12.6 0.0 collective-permute-done.refs_4_
  12.6 2.6 %near.1 = (bf16[64,3584]{1,0:T(8,128)(2,1)S(1)}, bf16[64,3584]{1,0:T(8,128)(2,1)S(1)}, bf16[3584,256]{1,0:T(8,128)(2,1)S(1)}, bf16[3584,256]{1,0:T(8,128)(2,1)S(1)}, bf16[256,3584]{1,0:T(8,128)(2,1)S(1)}) custom-call(bf16[3584,256]{1,0:T(8,128)(2,1)} %bitcast.5, bf16[3584,256]{1,0:T(8,128)(2,1)} %bitcast.6, bf16[256,3584]{1,0:T(8,128)(2,1)} %bitcast.7, ...), custom_call_target="tpu_custom_call" | custom-call | tf_op jit(solution)/shard_map/near/pallas_call | solution.py:216
  15.2 0.0 collective-permute-done.6.refs_3_
  15.2 0.5 %collective-permute-done.5.refs_2_ = bf16[3,4,3584]{2,1,0:T(4,128)(2,1)S(1)} collective-permute-done((bf16[3,4,3584]{2,1,0:T(4,128)(2,1)S(1)}, bf16[3,4,3584]{2,1,0:T(4,128)(2,1)S(1)}, u32[]{:S(2)}, u32[]{:S(2)}) %collective-permute-start.5) | collective-permute-done | bytes 86048 | tf_op jit(solution)/shard_map/ppermute | solution.py:39
  15.8 0.8 %collective-permute-done.4.refs_1_ = bf16[3,4,3584]{2,1,0:T(4,128)(2,1)S(1)} collective-permute-done((bf16[3,4,3584]{2,1,0:T(4,128)(2,1)S(1)}, bf16[3,4,3584]{2,1,0:T(4,128)(2,1)S(1)}, u32[]{:S(2)}, u32[]{:S(2)}) %collective-permute-start.4) | collective-permute-done | bytes 86048 | tf_op jit(solution)/shard_map/ppermute | solution.py:39
  16.6 0.0 copy-start
  16.6 0.0 copy-start.1
  16.6 3.5 %expert.1 = (bf16[3,4,3584]{2,1,0:T(4,128)(2,1)S(1)}, bf16[3,4,3584]{2,1,0:T(4,128)(2,1)S(1)}, bf16[3,4,3584]{2,1,0:T(4,128)(2,1)S(1)}, bf16[3,4,3584]{2,1,0:T(4...) custom-call(bf16[3584,256]{1,0:T(8,128)(2,1)S(1)} %get-tuple-element, ...), custom_call_target="tpu_custom_call", output_to_operand_aliasing={{8}: (3, {}), {9}: (4, {})} | custom-call | tf_op jit(solution)/shard_map/expert/pallas_call | solution.py:225
  20.1 0.5 %collective-permute-start.10 = (bf16[3,4,3584]{2,1,0:T(4,128)(2,1)S(1)}, bf16[3,4,3584]{2,1,0:T(4,128)(2,1)S(1)}, u32[]{:S(2)}, u32[]{:S(2)}) collective-permute-start(bf16[3,4,3584]{2,1,0:T(4,128)(2,1)S(1)} %get-tuple-element.31), channel_id=1, source_target_pairs={{0,1},{1,0},{2,3},{3,2},{4,5},{5,4},{6,7},{7,6},{8,9},{9,8},{10,11... | collective-permute-start | bytes 258056 | tf_op jit(solution)/shard_map/ppermute | solution.py:39
  20.6 1.5 %collective-permute-start.11 = (bf16[3,4,3584]{2,1,0:T(4,128)(2,1)S(1)}, bf16[3,4,3584]{2,1,0:T(4,128)(2,1)S(1)}, u32[]{:S(2)}, u32[]{:S(2)}) collective-permute-start(bf16[3,4,3584]{2,1,0:T(4,128)(2,1)S(1)} %get-tuple-element.32), channel_id=1, source_target_pairs={{0,2},{1,3},{2,0},{3,1},{4,6},{5,7},{6,4},{7,5},{8,10},{9,11},{10,... | collective-permute-start | bytes 258056 | tf_op jit(solution)/shard_map/ppermute | solution.py:39
  22.1 0.7 %collective-permute-start.12 = (bf16[3,4,3584]{2,1,0:T(4,128)(2,1)S(1)}, bf16[3,4,3584]{2,1,0:T(4,128)(2,1)S(1)}, u32[]{:S(2)}, u32[]{:S(2)}) collective-permute-start(bf16[3,4,3584]{2,1,0:T(4,128)(2,1)S(1)} %get-tuple-element.33), channel_id=1, source_target_pairs={{0,3},{1,2},{2,1},{3,0},{4,7},{5,6},{6,5},{7,4},{8,11},{9,10},{10,... | collective-permute-start | bytes 258056 | tf_op jit(solution)/shard_map/ppermute | solution.py:39
  22.8 0.4 %collective-permute-start.7 = (bf16[3,4,3584]{2,1,0:T(4,128)(2,1)S(1)}, bf16[3,4,3584]{2,1,0:T(4,128)(2,1)S(1)}, u32[]{:S(2)}, u32[]{:S(2)}) collective-permute-start(bf16[3,4,3584]{2,1,0:T(4,128)(2,1)S(1)} %get-tuple-element.27), channel_id=1, source_target_pairs={{0,1},{1,0},{2,3},{3,2},{4,5},{5,4},{6,7},{7,6},{8,9},{9,8},{10,11... | collective-permute-start | bytes 258056 | tf_op jit(solution)/shard_map/ppermute | solution.py:39
  23.3 1.5 %collective-permute-start.8 = (bf16[3,4,3584]{2,1,0:T(4,128)(2,1)S(1)}, bf16[3,4,3584]{2,1,0:T(4,128)(2,1)S(1)}, u32[]{:S(2)}, u32[]{:S(2)}) collective-permute-start(bf16[3,4,3584]{2,1,0:T(4,128)(2,1)S(1)} %get-tuple-element.28), channel_id=1, source_target_pairs={{0,2},{1,3},{2,0},{3,1},{4,6},{5,7},{6,4},{7,5},{8,10},{9,11},{10,... | collective-permute-start | bytes 258056 | tf_op jit(solution)/shard_map/ppermute | solution.py:39
  24.7 0.0 collective-permute-done.10.refs_1_
  24.7 0.7 %collective-permute-start.9 = (bf16[3,4,3584]{2,1,0:T(4,128)(2,1)S(1)}, bf16[3,4,3584]{2,1,0:T(4,128)(2,1)S(1)}, u32[]{:S(2)}, u32[]{:S(2)}) collective-permute-start(bf16[3,4,3584]{2,1,0:T(4,128)(2,1)S(1)} %get-tuple-element.29), channel_id=1, source_target_pairs={{0,3},{1,2},{2,1},{3,0},{4,7},{5,6},{6,5},{7,4},{8,11},{9,10},{10,... | collective-permute-start | bytes 258056 | tf_op jit(solution)/shard_map/ppermute | solution.py:39
  25.5 0.0 collective-permute-done.11.refs_2_
  25.5 0.9 %collective-permute-done.12.refs_3_ = bf16[3,4,3584]{2,1,0:T(4,128)(2,1)S(1)} collective-permute-done((bf16[3,4,3584]{2,1,0:T(4,128)(2,1)S(1)}, bf16[3,4,3584]{2,1,0:T(4,128)(2,1)S(1)}, u32[]{:S(2)}, u32[]{:S(2)}) %collective-permute-start.12) | collective-permute-done | bytes 86048 | tf_op jit(solution)/shard_map/ppermute | solution.py:39
  26.4 0.1 total.1
  26.5 3.9 %collective-permute-start.13 = (bf16[3,4,3584]{2,1,0:T(4,128)(2,1)S(1)}, bf16[3,4,3584]{2,1,0:T(4,128)(2,1)S(1)}, u32[]{:S(2)}, u32[]{:S(2)}) collective-permute-start(bf16[3,4,3584]{2,1,0:T(4,128)(2,1)S(1)} %total.1), channel_id=1, source_target_pairs={{0,4},{2,6},{4,0},{6,2},{1,5},{3,7},{5,1},{7,3},{8,12},{10,14},{12... | collective-permute-start | bytes 258056 | tf_op jit(solution)/shard_map/ppermute | solution.py:44
  30.4 0.0 collective-permute-done.7.refs_1_
  30.4 0.0 collective-permute-done.8.refs_2_
  30.4 0.0 collective-permute-done.9.refs_3_
  30.4 2.1 %collective-permute-done.13.refs_4_ = bf16[3,4,3584]{2,1,0:T(4,128)(2,1)S(1)} collective-permute-done((bf16[3,4,3584]{2,1,0:T(4,128)(2,1)S(1)}, bf16[3,4,3584]{2,1,0:T(4,128)(2,1)S(1)}, u32[]{:S(2)}, u32[]{:S(2)}) %collective-permute-start.13) | collective-permute-done | bytes 86048 | tf_op jit(solution)/shard_map/ppermute | solution.py:44
  32.5 0.0 copy-done
  32.5 0.3 grad.1
  32.9 6.8 %collective-permute-start.14 = (bf16[8,3584]{1,0:T(8,128)(2,1)S(1)}, bf16[8,3584]{1,0:T(8,128)(2,1)S(1)}, u32[]{:S(2)}, u32[]{:S(2)}) collective-permute-start(bf16[8,3584]{1,0:T(8,128)(2,1)S(1)} %grad.1), channel_id=1, source_target_pairs={{8,0},{16,8},{24,16},{9,1},{17,9},{25,17},{10,2},{18,10},{26,18},{... | collective-permute-start | bytes 172040 | tf_op jit(solution)/shard_map/ppermute | solution.py:48
  39.6 0.0 copy-done.1
  39.7 0.9 %out.1 = bf16[8,3584]{1,0:T(8,128)(2,1)} custom-call(f32[2,8,128]{2,1,0:T(8,128)S(1)} %get-tuple-element.18.mix, bf16[8,3584]{1,0:T(8,128)(2,1)S(1)} %copy-done.1, bf16[3,4,3584]{2,1,0:T(4,128)(2,1)S(1)} %get-tuple-element.26.refs_0_, bf16[3,4,3584]{2,1,0:T(4,128)(2,1)S(1)} %collective-permute-done.7.refs_1_, ...), custom_call_target="tpu_custom_call" | custom-call | tf_op jit(solution)/shard_map/out/pallas_call | solution.py:240
  40.6 2.1 %collective-permute-done.14 = bf16[8,3584]{1,0:T(8,128)(2,1)S(1)} collective-permute-done((bf16[8,3584]{1,0:T(8,128)(2,1)S(1)}, bf16[8,3584]{1,0:T(8,128)(2,1)S(1)}, u32[]{:S(2)}, u32[]{:S(2)}) %collective-permute-start.14) | collective-permute-done | bytes 57376 | tf_op jit(solution)/shard_map/ppermute | solution.py:48
  42.6 0.6 %copy.16 = bf16[8,3584]{1,0:T(8,128)(2,1)} copy(bf16[8,3584]{1,0:T(8,128)(2,1)S(1)} %collective-permute-done.14) | data formatting | bytes 114688
Async XLA Ops:
  2.6 5.9 %collective-permute-start.3 = (bf16[3,4,3584]{2,1,0:T(4,128)(2,1)S(1)}, bf16[3,4,3584]{2,1,0:T(4,128)(2,1)S(1)}, u32[]{:S(2)}, u32[]{:S(2)}) collective-permute-start(bf16[3,4,3584]{2,1,0:T(4,128)(2,1)S(1)} %get-tuple-element.25), channel_id=1, source_target_pairs={{0,4},{2,6},{4,0},{6,2},{1,5},{3,7},{5,1},{7,3},{8,12},{10,14},{12... | collective-permute-start | bytes 258056 | tf_op jit(solution)/shard_map/ppermute | solution.py:44
  5.8 6.0 %collective-permute-start.2 = (bf16[3,4,3584]{2,1,0:T(4,128)(2,1)S(1)}, bf16[3,4,3584]{2,1,0:T(4,128)(2,1)S(1)}, u32[]{:S(2)}, u32[]{:S(2)}) collective-permute-start(bf16[3,4,3584]{2,1,0:T(4,128)(2,1)S(1)} %get-tuple-element.19.refs_3_), channel_id=1, source_target_pairs={{0,3},{1,2},{2,1},{3,0},{4,7},{5,6},{6,5},{7,4},{8,11},{9,10},{10,... | collective-permute-start | bytes 258056 | tf_op jit(solution)/shard_map/ppermute | solution.py:39
  8.0 4.5 %collective-permute-start.1 = (bf16[3,4,3584]{2,1,0:T(4,128)(2,1)S(1)}, bf16[3,4,3584]{2,1,0:T(4,128)(2,1)S(1)}, u32[]{:S(2)}, u32[]{:S(2)}) collective-permute-start(bf16[3,4,3584]{2,1,0:T(4,128)(2,1)S(1)} %get-tuple-element.19.refs_3_), channel_id=1, source_target_pairs={{0,2},{1,3},{2,0},{3,1},{4,6},{5,7},{6,4},{7,5},{8,10},{9,11},{10,... | collective-permute-start | bytes 258056 | tf_op jit(solution)/shard_map/ppermute | solution.py:39
  8.2 4.4 %collective-permute-start = (bf16[3,4,3584]{2,1,0:T(4,128)(2,1)S(1)}, bf16[3,4,3584]{2,1,0:T(4,128)(2,1)S(1)}, u32[]{:S(2)}, u32[]{:S(2)}) collective-permute-start(bf16[3,4,3584]{2,1,0:T(4,128)(2,1)S(1)} %get-tuple-element.19.refs_3_), channel_id=1, source_target_pairs={{0,1},{1,0},{2,3},{3,2},{4,5},{5,4},{6,7},{7,6},{8,9},{9,8},{10,11... | collective-permute-start | bytes 258056 | tf_op jit(solution)/shard_map/ppermute | solution.py:39
  8.5 6.8 %collective-permute-start.6 = (bf16[3,4,3584]{2,1,0:T(4,128)(2,1)S(1)}, bf16[3,4,3584]{2,1,0:T(4,128)(2,1)S(1)}, u32[]{:S(2)}, u32[]{:S(2)}) collective-permute-start(bf16[3,4,3584]{2,1,0:T(4,128)(2,1)S(1)} %collective-permute-done.3.refs_0_), channel_id=1, source_target_pairs={{0,3},{1,2},{2,1},{3,0},{4,7},{5,6},{6,5},{7,4},{8,11},{9,10},{10,... | collective-permute-start | bytes 258056 | tf_op jit(solution)/shard_map/ppermute | solution.py:39
  11.8 4.0 %collective-permute-start.5 = (bf16[3,4,3584]{2,1,0:T(4,128)(2,1)S(1)}, bf16[3,4,3584]{2,1,0:T(4,128)(2,1)S(1)}, u32[]{:S(2)}, u32[]{:S(2)}) collective-permute-start(bf16[3,4,3584]{2,1,0:T(4,128)(2,1)S(1)} %collective-permute-done.3.refs_0_), channel_id=1, source_target_pairs={{0,2},{1,3},{2,0},{3,1},{4,6},{5,7},{6,4},{7,5},{8,10},{9,11},{10,... | collective-permute-start | bytes 258056 | tf_op jit(solution)/shard_map/ppermute | solution.py:39
  11.8 4.8 %collective-permute-start.4 = (bf16[3,4,3584]{2,1,0:T(4,128)(2,1)S(1)}, bf16[3,4,3584]{2,1,0:T(4,128)(2,1)S(1)}, u32[]{:S(2)}, u32[]{:S(2)}) collective-permute-start(bf16[3,4,3584]{2,1,0:T(4,128)(2,1)S(1)} %collective-permute-done.3.refs_0_), channel_id=1, source_target_pairs={{0,1},{1,0},{2,3},{3,2},{4,5},{5,4},{6,7},{7,6},{8,9},{9,8},{10,11... | collective-permute-start | bytes 258056 | tf_op jit(solution)/shard_map/ppermute | solution.py:39
  16.6 16.0 %copy-start = (bf16[8,3584]{1,0:T(8,128)(2,1)S(1)}, bf16[8,3584]{1,0:T(8,128)(2,1)}, u32[]{:S(2)}) copy-start(bf16[8,3584]{1,0:T(8,128)(2,1)} %base.3) | copy-start | bytes 172036
  16.6 23.1 %copy-start.1 = (bf16[8,3584]{1,0:T(8,128)(2,1)S(1)}, bf16[8,3584]{1,0:T(8,128)(2,1)}, u32[]{:S(2)}) copy-start(bf16[8,3584]{1,0:T(8,128)(2,1)} %base.2) | copy-start | bytes 172036
  20.1 4.6 %collective-permute-start.10 = (bf16[3,4,3584]{2,1,0:T(4,128)(2,1)S(1)}, bf16[3,4,3584]{2,1,0:T(4,128)(2,1)S(1)}, u32[]{:S(2)}, u32[]{:S(2)}) collective-permute-start(bf16[3,4,3584]{2,1,0:T(4,128)(2,1)S(1)} %get-tuple-element.31), channel_id=1, source_target_pairs={{0,1},{1,0},{2,3},{3,2},{4,5},{5,4},{6,7},{7,6},{8,9},{9,8},{10,11... | collective-permute-start | bytes 258056 | tf_op jit(solution)/shard_map/ppermute | solution.py:39
  20.6 4.9 %collective-permute-start.11 = (bf16[3,4,3584]{2,1,0:T(4,128)(2,1)S(1)}, bf16[3,4,3584]{2,1,0:T(4,128)(2,1)S(1)}, u32[]{:S(2)}, u32[]{:S(2)}) collective-permute-start(bf16[3,4,3584]{2,1,0:T(4,128)(2,1)S(1)} %get-tuple-element.32), channel_id=1, source_target_pairs={{0,2},{1,3},{2,0},{3,1},{4,6},{5,7},{6,4},{7,5},{8,10},{9,11},{10,... | collective-permute-start | bytes 258056 | tf_op jit(solution)/shard_map/ppermute | solution.py:39
  22.1 4.3 %collective-permute-start.12 = (bf16[3,4,3584]{2,1,0:T(4,128)(2,1)S(1)}, bf16[3,4,3584]{2,1,0:T(4,128)(2,1)S(1)}, u32[]{:S(2)}, u32[]{:S(2)}) collective-permute-start(bf16[3,4,3584]{2,1,0:T(4,128)(2,1)S(1)} %get-tuple-element.33), channel_id=1, source_target_pairs={{0,3},{1,2},{2,1},{3,0},{4,7},{5,6},{6,5},{7,4},{8,11},{9,10},{10,... | collective-permute-start | bytes 258056 | tf_op jit(solution)/shard_map/ppermute | solution.py:39
  22.8 7.5 %collective-permute-start.7 = (bf16[3,4,3584]{2,1,0:T(4,128)(2,1)S(1)}, bf16[3,4,3584]{2,1,0:T(4,128)(2,1)S(1)}, u32[]{:S(2)}, u32[]{:S(2)}) collective-permute-start(bf16[3,4,3584]{2,1,0:T(4,128)(2,1)S(1)} %get-tuple-element.27), channel_id=1, source_target_pairs={{0,1},{1,0},{2,3},{3,2},{4,5},{5,4},{6,7},{7,6},{8,9},{9,8},{10,11... | collective-permute-start | bytes 258056 | tf_op jit(solution)/shard_map/ppermute | solution.py:39
  23.3 7.1 %collective-permute-start.8 = (bf16[3,4,3584]{2,1,0:T(4,128)(2,1)S(1)}, bf16[3,4,3584]{2,1,0:T(4,128)(2,1)S(1)}, u32[]{:S(2)}, u32[]{:S(2)}) collective-permute-start(bf16[3,4,3584]{2,1,0:T(4,128)(2,1)S(1)} %get-tuple-element.28), channel_id=1, source_target_pairs={{0,2},{1,3},{2,0},{3,1},{4,6},{5,7},{6,4},{7,5},{8,10},{9,11},{10,... | collective-permute-start | bytes 258056 | tf_op jit(solution)/shard_map/ppermute | solution.py:39
  24.7 5.7 %collective-permute-start.9 = (bf16[3,4,3584]{2,1,0:T(4,128)(2,1)S(1)}, bf16[3,4,3584]{2,1,0:T(4,128)(2,1)S(1)}, u32[]{:S(2)}, u32[]{:S(2)}) collective-permute-start(bf16[3,4,3584]{2,1,0:T(4,128)(2,1)S(1)} %get-tuple-element.29), channel_id=1, source_target_pairs={{0,3},{1,2},{2,1},{3,0},{4,7},{5,6},{6,5},{7,4},{8,11},{9,10},{10,... | collective-permute-start | bytes 258056 | tf_op jit(solution)/shard_map/ppermute | solution.py:39
  26.5 6.0 %collective-permute-start.13 = (bf16[3,4,3584]{2,1,0:T(4,128)(2,1)S(1)}, bf16[3,4,3584]{2,1,0:T(4,128)(2,1)S(1)}, u32[]{:S(2)}, u32[]{:S(2)}) collective-permute-start(bf16[3,4,3584]{2,1,0:T(4,128)(2,1)S(1)} %total.1), channel_id=1, source_target_pairs={{0,4},{2,6},{4,0},{6,2},{1,5},{3,7},{5,1},{7,3},{8,12},{10,14},{12... | collective-permute-start | bytes 258056 | tf_op jit(solution)/shard_map/ppermute | solution.py:44
  32.9 9.8 %collective-permute-start.14 = (bf16[8,3584]{1,0:T(8,128)(2,1)S(1)}, bf16[8,3584]{1,0:T(8,128)(2,1)S(1)}, u32[]{:S(2)}, u32[]{:S(2)}) collective-permute-start(bf16[8,3584]{1,0:T(8,128)(2,1)S(1)} %grad.1), channel_id=1, source_target_pairs={{8,0},{16,8},{24,16},{9,1},{17,9},{25,17},{10,2},{18,10},{26,18},{... | collective-permute-start | bytes 172040 | tf_op jit(solution)/shard_map/ppermute | solution.py:48

commit v3 on v2

--- a/solution.py
+++ b/solution.py
@@ -49,8 +49,8 @@
 
 
 def pack_kernel(experts, cap, top, *refs):
-    keep, stored, mix_out, blocks = refs[0], refs[1:5], refs[5], refs[6 : 6 + experts]
-    held, sems = refs[6 + experts : -1], refs[-1]
+    stored, mix_out, blocks = refs[:4], refs[4], refs[5 : 5 + experts]
+    held, sems = refs[5 + experts : -1], refs[-1]
     copies = [pltpu.make_async_copy(s, h, sems.at[i]) for i, (s, h) in enumerate(zip(stored, held))]
     for copy in copies:
         copy.start()
@@ -88,7 +88,7 @@
             at = (k * tiles + i) * TILE
             block[i] = packed[at : at + TILE]
     copies[1].wait()
-    weight = jnp.broadcast_to(probs[...].astype(jnp.float32) * keep[...].astype(jnp.float32), (pairs, pairs))
+    weight = jnp.broadcast_to(probs[...].astype(jnp.float32), (pairs, pairs))
     weight = jnp.sum(jnp.where(p == q, weight, 0.0), axis=1, keepdims=True)
     slot = lax.broadcasted_iota(jnp.int32, (pairs, LANES), 1)
     for t in range(2):
@@ -126,9 +126,9 @@
     near = count * deep * TILE
     fill(acts, near, ins, 0, deep, tiles)
     fill(cot, near, ins, tiles - deep, deep, tiles)
+    grad_hidden = dot(w_down[...], cot[...], CROSS).T
     gate_pre = dot(acts[...], w_gate[...])
     up_pre = dot(acts[...], w_up[...])
-    grad_hidden = dot(cot[...], w_down[...], CROSS)
     if lead:
         grad_hidden = pltpu.roll(grad_hidden, tall - lead, 0)
     live = lax.broadcasted_iota(jnp.int32, gate_pre.shape, 0) % (deep * TILE) < cap
@@ -140,11 +140,12 @@
     if lead:
         grad_gate, grad_up = pltpu.roll(grad_gate, lead, 0), pltpu.roll(grad_up, lead, 0)
     grad_gate, grad_up = rounded(grad_gate), rounded(grad_up)
-    step = 512
+    step = width // 2
     for at in range(0, width, step):
         cols = slice(at, at + step)
         out = dot(hidden, w_down[:, cols])
-        grad = dot(grad_gate, w_gate[cols, :], CROSS) + dot(grad_up, w_up[cols, :], CROSS)
+        grad = dot(w_gate[cols, :], grad_gate, CROSS) + dot(w_up[cols, :], grad_up, CROSS)
+        grad = rounded(grad).T.astype(jnp.float32)
         for n, (ref, b) in enumerate(places):
             base = n * deep * TILE
             for i in range(tiles):
@@ -164,10 +165,10 @@
     refs[-1][...] = rounded(total)
 
 
-def finish_kernel(which, cap, count, mix, base, *refs):
+def finish_kernel(which, cap, count, keep, mix, base, *refs):
     own, back, result = refs[:count], refs[count:-1], refs[-1]
     tiles, deep = 2 * cap // TILE, -(-cap // TILE)
-    total = base[...].astype(jnp.float32)
+    mixed = jnp.zeros(base.shape, jnp.float32)
     weights = rounded(mix[which])
     for i in range(deep) if which == 0 else range(tiles - deep, tiles):
         rows = own[0][i].astype(jnp.float32)
@@ -175,8 +176,8 @@
             rows = rows + ref[i].astype(jnp.float32)
         for k, rows in enumerate([rounded(rows)] + [ref[i] for ref in back]):
             at = (k * tiles + i) * TILE
-            total = total + dot(weights[:, at : at + TILE], rows)
-    result[...] = rounded(total)
+            mixed = mixed + dot(weights[:, at : at + TILE], rows)
+    result[...] = rounded(base[...].astype(jnp.float32) + keep[0, 0].astype(jnp.float32) * mixed)
 
 
 def shards(acts, cotangent, routes, probs, keep, w_gate, w_up, w_down):
@@ -195,13 +196,13 @@
     inputs = (routes.reshape(1, pairs), probs.reshape(1, pairs), acts, cotangent)
     mix, *sent = pl.pallas_call(
         functools.partial(pack_kernel, experts, capacity, top),
-        in_specs=[vmem] + [far_off] * 4,
+        in_specs=[far_off] * 4,
         out_specs=[vmem] * (1 + experts),
         out_shape=[pltpu.VMEM((2, token_count, LANES), jnp.float32)] + [block] * experts,
         scratch_shapes=[pltpu.VMEM(x.shape, x.dtype) for x in inputs] + [pltpu.SemaphoreType.DMA((4,))],
         compiler_params=room(4),
         name="pack",
-    )(keep, *map(in_hbm, inputs))
+    )(*map(in_hbm, inputs))
 
     members = [(half, by) for half in range(2) for by in range(r)]
     near = [sent[0]]
@@ -232,17 +233,19 @@
         name="expert",
     )(*map(near_core, (*held, acts_rows, cot_rows, *far)))
     near, far = parts[:count], parts[count:]
-    far = [far[0]] + [to_member(x, half, -by) for x, (half, by) in zip(far[1:], members[1:])]
-    near = [near[0]] + [to_member(x, half, -by) for x, (half, by) in zip(near[1:], members[1:])]
+    order = range(count - 1, 0, -1)
+    far = [far[0]] + [to_member(far[i], members[i][0], -members[i][1]) for i in order]
+    near = [near[0]] + [to_member(near[i], members[i][0], -members[i][1]) for i in order]
     total = pl.pallas_call(sum_kernel, out_shape=rest, compiler_params=room(4), name="total")(*map(near_core, far))
     back = [to_expert(total[(k - 1) * tiles : k * tiles], -k) for k in range(1, experts)]
     layer_out, section_grad = [
         pl.pallas_call(
             functools.partial(finish_kernel, which, capacity, count),
+            in_specs=[pl.BlockSpec(memory_space=pltpu.SMEM)] + [vmem] * (2 + count + len(back)),
             out_shape=shape(acts.shape, jnp.bfloat16) if which == 0 else pltpu.VMEM(acts.shape, jnp.bfloat16),
             compiler_params=room(4),
             name=name,
-        )(*map(near_core, (mix, base, *near, *back)))
+        )(keep, *map(near_core, (mix, base, *near, *back)))
         for which, name, base in ((0, "out", acts), (1, "grad", cotangent))
     ]
     return layer_out, to_below(section_grad)

time: 43.4 us -> 41.7 us (0.961)
  starting transfers between devices: 25.6 us -> 23.4 us
  waiting for transfers between devices: 6.9 us -> 8.22 us
  Pallas kernels: 8.8 us -> 7.89 us
    ppermute x12, waiting for transfers between devices: 2.72 us -> 5.29 us  [to_member(): return lax.ppermute(shard, ('expert', 'dp'), pairs)]
    ppermute x2, starting transfers between devices: 7.06 us -> 4.59 us  [to_expert(): lax.ppermute(shard, 'expert', [(e, (e + 2 * by) % n) for e in range(n)])]
    ppermute x2, waiting for transfers between devices: 2.13 us -> 0.92 us  [to_expert(): lax.ppermute(shard, 'expert', [(e, (e + 2 * by) % n) for e in range(n)])]
    pallas_call x1, Pallas kernels: 3.55 us -> 2.66 us  [shards(): pl.pallas_call(functools.partial(expert_kernel, capacity, count), in_spec...]
    ppermute x1, starting transfers between devices: 6.77 us -> 7.55 us  [to_below(): lax.ppermute(shard, 'pipe', [(p, p - 1) for p in range(1, lax.axis_size('...]
    ppermute x12, starting transfers between devices: 11.7 us -> 11.3 us  [to_member(): return lax.ppermute(shard, ('expert', 'dp'), pairs)]
  transfers between devices with their start and end apart: 15 -> 15, of which waited for: 6 -> 8; matrix products, arithmetic and copies ran while one was open for 0% -> 0% of each run, Pallas kernels for 8% -> 9%
where the time goes in v3:
time: 41.7 us; the launch traced here: 41.5 us
  starting transfers between devices  23.4 us (56%)
  waiting for transfers between devices  8.22 us (20%)
  Pallas kernels  7.89 us (19%)
  between operations  1.37 us (3%)
  local copies, waits for them, and re-layouts  0.63 us (2%)
    ppermute x12, starting transfers between devices, to_member(): return lax.ppermute(shard, ('expert', 'dp'), pairs)  11.3 us
    ppermute x1, starting transfers between devices, to_below(): lax.ppermute(shard, 'pipe', [(p, p - 1) for p in range(1, lax.axis_size('...  7.55 us
    ppermute x12, waiting for transfers between devices, to_member(): return lax.ppermute(shard, ('expert', 'dp'), pairs)  5.29 us
    ppermute x2, starting transfers between devices, to_expert(): lax.ppermute(shard, 'expert', [(e, (e + 2 * by) % n) for e in range(n)])  4.59 us
    pallas_call x1, Pallas kernels, shards(): pl.pallas_call(functools.partial(expert_kernel, capacity, count), in_spec...  2.66 us
    pallas_call x1, Pallas kernels, shards(): pl.pallas_call(functools.partial(near_kernel, capacity, count), in_specs=...  2.63 us
    ppermute x1, waiting for transfers between devices, to_below(): lax.ppermute(shard, 'pipe', [(p, p - 1) for p in range(1, lax.axis_size('...  2.01 us
    pallas_call x2, Pallas kernels, shards(): pl.pallas_call(functools.partial(finish_kernel, which, capacity, count),...  1.28 us
  transfers between devices with their start and end apart: 15, of which 8 were waited for; matrix products, arithmetic and copies ran while one was open for 0% of the time, Pallas kernels for 9%

profile of v3, /device:TPU:1, one launch (start us, length us, event | category | flops | bytes accessed | tf_op | source)
XLA Modules:
  0.0 41.5 jit_solution(17854015595340235669)
XLA Ops:
  0.6 1.2 %pack.1 = (f32[2,8,128]{2,1,0:T(8,128)S(1)}, bf16[3,4,3584]{2,1,0:T(4,128)(2,1)S(1)}, bf16[3,4,3584]{2,1,0:T(4,128)(2,1)S(1)}) custom-call(s32[1,8]{1,0:T(1,128)} %bitcast.8, bf16[1,8]{1,0:T(2,128)(2,1)} %bitcast.9, bf16[8,3584]{1,0:T(8,128)(2,1)} %base.2, bf16[8,3584]{1,0:T(8,128)(2,1)} %base.3), custom_call_target="tpu_custom_call" | custom-call | tf_op jit(solution)/shard_map/pack/pallas_call | solution.py:197
  1.9 3.2 %collective-permute-start.3 = (bf16[3,4,3584]{2,1,0:T(4,128)(2,1)S(1)}, bf16[3,4,3584]{2,1,0:T(4,128)(2,1)S(1)}, u32[]{:S(2)}, u32[]{:S(2)}) collective-permute-start(bf16[3,4,3584]{2,1,0:T(4,128)(2,1)S(1)} %get-tuple-element.25), channel_id=1, source_target_pairs={{0,4},{2,6},{4,0},{6,2},{1,5},{3,7},{5,1},{7,3},{8,12},{10,14},{12... | collective-permute-start | bytes 258056 | tf_op jit(solution)/shard_map/ppermute | solution.py:44
  5.1 1.2 %collective-permute-start = (bf16[3,4,3584]{2,1,0:T(4,128)(2,1)S(1)}, bf16[3,4,3584]{2,1,0:T(4,128)(2,1)S(1)}, u32[]{:S(2)}, u32[]{:S(2)}) collective-permute-start(bf16[3,4,3584]{2,1,0:T(4,128)(2,1)S(1)} %get-tuple-element.19.refs_3_), channel_id=1, source_target_pairs={{0,1},{1,0},{2,3},{3,2},{4,5},{5,4},{6,7},{7,6},{8,9},{9,8},{10,11... | collective-permute-start | bytes 258056 | tf_op jit(solution)/shard_map/ppermute | solution.py:39
  6.3 1.3 %collective-permute-start.1 = (bf16[3,4,3584]{2,1,0:T(4,128)(2,1)S(1)}, bf16[3,4,3584]{2,1,0:T(4,128)(2,1)S(1)}, u32[]{:S(2)}, u32[]{:S(2)}) collective-permute-start(bf16[3,4,3584]{2,1,0:T(4,128)(2,1)S(1)} %get-tuple-element.19.refs_3_), channel_id=1, source_target_pairs={{0,2},{1,3},{2,0},{3,1},{4,6},{5,7},{6,4},{7,5},{8,10},{9,11},{10,... | collective-permute-start | bytes 258056 | tf_op jit(solution)/shard_map/ppermute | solution.py:39
  7.6 0.1 collective-permute-start.2
  7.7 0.0 collective-permute-done.3.refs_0_
  7.7 1.2 %collective-permute-start.4 = (bf16[3,4,3584]{2,1,0:T(4,128)(2,1)S(1)}, bf16[3,4,3584]{2,1,0:T(4,128)(2,1)S(1)}, u32[]{:S(2)}, u32[]{:S(2)}) collective-permute-start(bf16[3,4,3584]{2,1,0:T(4,128)(2,1)S(1)} %collective-permute-done.3.refs_0_), channel_id=1, source_target_pairs={{0,1},{1,0},{2,3},{3,2},{4,5},{5,4},{6,7},{7,6},{8,9},{9,8},{10,11... | collective-permute-start | bytes 258056 | tf_op jit(solution)/shard_map/ppermute | solution.py:39
  9.0 2.5 %collective-permute-start.5 = (bf16[3,4,3584]{2,1,0:T(4,128)(2,1)S(1)}, bf16[3,4,3584]{2,1,0:T(4,128)(2,1)S(1)}, u32[]{:S(2)}, u32[]{:S(2)}) collective-permute-start(bf16[3,4,3584]{2,1,0:T(4,128)(2,1)S(1)} %collective-permute-done.3.refs_0_), channel_id=1, source_target_pairs={{0,2},{1,3},{2,0},{3,1},{4,6},{5,7},{6,4},{7,5},{8,10},{9,11},{10,... | collective-permute-start | bytes 258056 | tf_op jit(solution)/shard_map/ppermute | solution.py:39
  11.5 0.0 collective-permute-done.refs_4_
  11.5 0.0 collective-permute-start.6
  11.5 0.0 collective-permute-done.1.refs_5_
  11.5 0.8 %collective-permute-done.2.refs_6_ = bf16[3,4,3584]{2,1,0:T(4,128)(2,1)S(1)} collective-permute-done((bf16[3,4,3584]{2,1,0:T(4,128)(2,1)S(1)}, bf16[3,4,3584]{2,1,0:T(4,128)(2,1)S(1)}, u32[]{:S(2)}, u32[]{:S(2)}) %collective-permute-start.2) | collective-permute-done | bytes 86048 | tf_op jit(solution)/shard_map/ppermute | solution.py:39
  12.3 2.6 %near.1 = (bf16[64,3584]{1,0:T(8,128)(2,1)S(1)}, bf16[64,3584]{1,0:T(8,128)(2,1)S(1)}, bf16[3584,256]{1,0:T(8,128)(2,1)S(1)}, bf16[3584,256]{1,0:T(8,128)(2,1)S(1)}, bf16[256,3584]{1,0:T(8,128)(2,1)S(1)}) custom-call(bf16[3584,256]{1,0:T(8,128)(2,1)} %bitcast.5, bf16[3584,256]{1,0:T(8,128)(2,1)} %bitcast.6, bf16[256,3584]{1,0:T(8,128)(2,1)} %bitcast.7, ...), custom_call_target="tpu_custom_call" | custom-call | tf_op jit(solution)/shard_map/near/pallas_call | solution.py:217
  15.0 0.0 collective-permute-done.4.refs_1_
  15.0 0.0 collective-permute-done.5.refs_2_
  15.0 1.9 %collective-permute-done.6.refs_3_ = bf16[3,4,3584]{2,1,0:T(4,128)(2,1)S(1)} collective-permute-done((bf16[3,4,3584]{2,1,0:T(4,128)(2,1)S(1)}, bf16[3,4,3584]{2,1,0:T(4,128)(2,1)S(1)}, u32[]{:S(2)}, u32[]{:S(2)}) %collective-permute-start.6) | collective-permute-done | bytes 86048 | tf_op jit(solution)/shard_map/ppermute | solution.py:39
  16.9 0.0 copy-start
  16.9 0.0 copy-start.1
  16.9 2.7 %expert.1 = (bf16[3,4,3584]{2,1,0:T(4,128)(2,1)S(1)}, bf16[3,4,3584]{2,1,0:T(4,128)(2,1)S(1)}, bf16[3,4,3584]{2,1,0:T(4,128)(2,1)S(1)}, bf16[3,4,3584]{2,1,0:T(4...) custom-call(bf16[3584,256]{1,0:T(8,128)(2,1)S(1)} %get-tuple-element, ...), custom_call_target="tpu_custom_call", output_to_operand_aliasing={{8}: (3, {}), {9}: (4, {})} | custom-call | tf_op jit(solution)/shard_map/expert/pallas_call | solution.py:226
  19.6 0.5 %collective-permute-start.10 = (bf16[3,4,3584]{2,1,0:T(4,128)(2,1)S(1)}, bf16[3,4,3584]{2,1,0:T(4,128)(2,1)S(1)}, u32[]{:S(2)}, u32[]{:S(2)}) collective-permute-start(bf16[3,4,3584]{2,1,0:T(4,128)(2,1)S(1)} %get-tuple-element.31), channel_id=1, source_target_pairs={{0,3},{1,2},{2,1},{3,0},{4,7},{5,6},{6,5},{7,4},{8,11},{9,10},{10,... | collective-permute-start | bytes 258056 | tf_op jit(solution)/shard_map/ppermute | solution.py:39
  20.1 0.0 collective-permute-start.11
  20.1 2.2 %collective-permute-start.12 = (bf16[3,4,3584]{2,1,0:T(4,128)(2,1)S(1)}, bf16[3,4,3584]{2,1,0:T(4,128)(2,1)S(1)}, u32[]{:S(2)}, u32[]{:S(2)}) collective-permute-start(bf16[3,4,3584]{2,1,0:T(4,128)(2,1)S(1)} %get-tuple-element.33), channel_id=1, source_target_pairs={{0,1},{1,0},{2,3},{3,2},{4,5},{5,4},{6,7},{7,6},{8,9},{9,8},{10,11... | collective-permute-start | bytes 258056 | tf_op jit(solution)/shard_map/ppermute | solution.py:39
  22.3 0.5 %collective-permute-start.7 = (bf16[3,4,3584]{2,1,0:T(4,128)(2,1)S(1)}, bf16[3,4,3584]{2,1,0:T(4,128)(2,1)S(1)}, u32[]{:S(2)}, u32[]{:S(2)}) collective-permute-start(bf16[3,4,3584]{2,1,0:T(4,128)(2,1)S(1)} %get-tuple-element.27), channel_id=1, source_target_pairs={{0,3},{1,2},{2,1},{3,0},{4,7},{5,6},{6,5},{7,4},{8,11},{9,10},{10,... | collective-permute-start | bytes 258056 | tf_op jit(solution)/shard_map/ppermute | solution.py:39
  22.8 0.7 %collective-permute-start.8 = (bf16[3,4,3584]{2,1,0:T(4,128)(2,1)S(1)}, bf16[3,4,3584]{2,1,0:T(4,128)(2,1)S(1)}, u32[]{:S(2)}, u32[]{:S(2)}) collective-permute-start(bf16[3,4,3584]{2,1,0:T(4,128)(2,1)S(1)} %get-tuple-element.28), channel_id=1, source_target_pairs={{0,2},{1,3},{2,0},{3,1},{4,6},{5,7},{6,4},{7,5},{8,10},{9,11},{10,... | collective-permute-start | bytes 258056 | tf_op jit(solution)/shard_map/ppermute | solution.py:39
  23.5 0.5 %collective-permute-done.10.refs_1_ = bf16[3,4,3584]{2,1,0:T(4,128)(2,1)S(1)} collective-permute-done((bf16[3,4,3584]{2,1,0:T(4,128)(2,1)S(1)}, bf16[3,4,3584]{2,1,0:T(4,128)(2,1)S(1)}, u32[]{:S(2)}, u32[]{:S(2)}) %collective-permute-start.10) | collective-permute-done | bytes 86048 | tf_op jit(solution)/shard_map/ppermute | solution.py:39
  24.0 1.0 %collective-permute-start.9 = (bf16[3,4,3584]{2,1,0:T(4,128)(2,1)S(1)}, bf16[3,4,3584]{2,1,0:T(4,128)(2,1)S(1)}, u32[]{:S(2)}, u32[]{:S(2)}) collective-permute-start(bf16[3,4,3584]{2,1,0:T(4,128)(2,1)S(1)} %get-tuple-element.29), channel_id=1, source_target_pairs={{0,1},{1,0},{2,3},{3,2},{4,5},{5,4},{6,7},{7,6},{8,9},{9,8},{10,11... | collective-permute-start | bytes 258056 | tf_op jit(solution)/shard_map/ppermute | solution.py:39
  25.0 0.0 collective-permute-done.11.refs_2_
  25.0 0.6 %collective-permute-done.12.refs_3_ = bf16[3,4,3584]{2,1,0:T(4,128)(2,1)S(1)} collective-permute-done((bf16[3,4,3584]{2,1,0:T(4,128)(2,1)S(1)}, bf16[3,4,3584]{2,1,0:T(4,128)(2,1)S(1)}, u32[]{:S(2)}, u32[]{:S(2)}) %collective-permute-start.12) | collective-permute-done | bytes 86048 | tf_op jit(solution)/shard_map/ppermute | solution.py:39
  25.6 0.1 total.1
  25.6 1.4 %collective-permute-start.13 = (bf16[3,4,3584]{2,1,0:T(4,128)(2,1)S(1)}, bf16[3,4,3584]{2,1,0:T(4,128)(2,1)S(1)}, u32[]{:S(2)}, u32[]{:S(2)}) collective-permute-start(bf16[3,4,3584]{2,1,0:T(4,128)(2,1)S(1)} %total.1), channel_id=1, source_target_pairs={{0,4},{2,6},{4,0},{6,2},{1,5},{3,7},{5,1},{7,3},{8,12},{10,14},{12... | collective-permute-start | bytes 258056 | tf_op jit(solution)/shard_map/ppermute | solution.py:44
  27.7 0.0 collective-permute-done.7.refs_1_
  27.7 0.4 collective-permute-done.8.refs_2_
  28.1 1.1 %collective-permute-done.9.refs_3_ = bf16[3,4,3584]{2,1,0:T(4,128)(2,1)S(1)} collective-permute-done((bf16[3,4,3584]{2,1,0:T(4,128)(2,1)S(1)}, bf16[3,4,3584]{2,1,0:T(4,128)(2,1)S(1)}, u32[]{:S(2)}, u32[]{:S(2)}) %collective-permute-start.9) | collective-permute-done | bytes 86048 | tf_op jit(solution)/shard_map/ppermute | solution.py:39
  29.1 0.9 %collective-permute-done.13.refs_4_ = bf16[3,4,3584]{2,1,0:T(4,128)(2,1)S(1)} collective-permute-done((bf16[3,4,3584]{2,1,0:T(4,128)(2,1)S(1)}, bf16[3,4,3584]{2,1,0:T(4,128)(2,1)S(1)}, u32[]{:S(2)}, u32[]{:S(2)}) %collective-permute-start.13) | collective-permute-done | bytes 86048 | tf_op jit(solution)/shard_map/ppermute | solution.py:44
  30.0 0.0 copy-done
  30.0 0.3 grad.1
  30.4 7.6 %collective-permute-start.14 = (bf16[8,3584]{1,0:T(8,128)(2,1)S(1)}, bf16[8,3584]{1,0:T(8,128)(2,1)S(1)}, u32[]{:S(2)}, u32[]{:S(2)}) collective-permute-start(bf16[8,3584]{1,0:T(8,128)(2,1)S(1)} %grad.1), channel_id=1, source_target_pairs={{8,0},{16,8},{24,16},{9,1},{17,9},{25,17},{10,2},{18,10},{26,18},{... | collective-permute-start | bytes 172040 | tf_op jit(solution)/shard_map/ppermute | solution.py:48
  37.9 0.0 copy-done.1
  37.9 1.0 %out.1 = bf16[8,3584]{1,0:T(8,128)(2,1)} custom-call(s32[1,1]{1,0:T(1,128)S(6)} %copy.15.keep, f32[2,8,128]{2,1,0:T(8,128)S(1)} %get-tuple-element.18.mix, bf16[8,3584]{1,0:T(8,128)(2,1)S(1)} %copy-done.1, bf16[3,4,3584]{2,1,0:T(4,128)(2,1)S(1)} %get-tuple-element.26.refs_0_, bf16[3,4,3584]{2,1,0:T(4,128)(2,1)S(1)} %collective-permute-done.7.refs_1_, ...), custom_call_target="tpu_custom_call" | custom-call | tf_op jit(solution)/shard_map/out/pallas_call | solution.py:242
  38.9 2.0 %collective-permute-done.14 = bf16[8,3584]{1,0:T(8,128)(2,1)S(1)} collective-permute-done((bf16[8,3584]{1,0:T(8,128)(2,1)S(1)}, bf16[8,3584]{1,0:T(8,128)(2,1)S(1)}, u32[]{:S(2)}, u32[]{:S(2)}) %collective-permute-start.14) | collective-permute-done | bytes 57376 | tf_op jit(solution)/shard_map/ppermute | solution.py:48
  40.9 0.6 %copy.16 = bf16[8,3584]{1,0:T(8,128)(2,1)} copy(bf16[8,3584]{1,0:T(8,128)(2,1)S(1)} %collective-permute-done.14) | data formatting | bytes 114688
Async XLA Ops:
  1.9 5.9 %collective-permute-start.3 = (bf16[3,4,3584]{2,1,0:T(4,128)(2,1)S(1)}, bf16[3,4,3584]{2,1,0:T(4,128)(2,1)S(1)}, u32[]{:S(2)}, u32[]{:S(2)}) collective-permute-start(bf16[3,4,3584]{2,1,0:T(4,128)(2,1)S(1)} %get-tuple-element.25), channel_id=1, source_target_pairs={{0,4},{2,6},{4,0},{6,2},{1,5},{3,7},{5,1},{7,3},{8,12},{10,14},{12... | collective-permute-start | bytes 258056 | tf_op jit(solution)/shard_map/ppermute | solution.py:44
  5.1 6.4 %collective-permute-start = (bf16[3,4,3584]{2,1,0:T(4,128)(2,1)S(1)}, bf16[3,4,3584]{2,1,0:T(4,128)(2,1)S(1)}, u32[]{:S(2)}, u32[]{:S(2)}) collective-permute-start(bf16[3,4,3584]{2,1,0:T(4,128)(2,1)S(1)} %get-tuple-element.19.refs_3_), channel_id=1, source_target_pairs={{0,1},{1,0},{2,3},{3,2},{4,5},{5,4},{6,7},{7,6},{8,9},{9,8},{10,11... | collective-permute-start | bytes 258056 | tf_op jit(solution)/shard_map/ppermute | solution.py:39
  6.3 5.2 %collective-permute-start.1 = (bf16[3,4,3584]{2,1,0:T(4,128)(2,1)S(1)}, bf16[3,4,3584]{2,1,0:T(4,128)(2,1)S(1)}, u32[]{:S(2)}, u32[]{:S(2)}) collective-permute-start(bf16[3,4,3584]{2,1,0:T(4,128)(2,1)S(1)} %get-tuple-element.19.refs_3_), channel_id=1, source_target_pairs={{0,2},{1,3},{2,0},{3,1},{4,6},{5,7},{6,4},{7,5},{8,10},{9,11},{10,... | collective-permute-start | bytes 258056 | tf_op jit(solution)/shard_map/ppermute | solution.py:39
  7.6 4.7 %collective-permute-start.2 = (bf16[3,4,3584]{2,1,0:T(4,128)(2,1)S(1)}, bf16[3,4,3584]{2,1,0:T(4,128)(2,1)S(1)}, u32[]{:S(2)}, u32[]{:S(2)}) collective-permute-start(bf16[3,4,3584]{2,1,0:T(4,128)(2,1)S(1)} %get-tuple-element.19.refs_3_), channel_id=1, source_target_pairs={{0,3},{1,2},{2,1},{3,0},{4,7},{5,6},{6,5},{7,4},{8,11},{9,10},{10,... | collective-permute-start | bytes 258056 | tf_op jit(solution)/shard_map/ppermute | solution.py:39
  7.7 7.2 %collective-permute-start.4 = (bf16[3,4,3584]{2,1,0:T(4,128)(2,1)S(1)}, bf16[3,4,3584]{2,1,0:T(4,128)(2,1)S(1)}, u32[]{:S(2)}, u32[]{:S(2)}) collective-permute-start(bf16[3,4,3584]{2,1,0:T(4,128)(2,1)S(1)} %collective-permute-done.3.refs_0_), channel_id=1, source_target_pairs={{0,1},{1,0},{2,3},{3,2},{4,5},{5,4},{6,7},{7,6},{8,9},{9,8},{10,11... | collective-permute-start | bytes 258056 | tf_op jit(solution)/shard_map/ppermute | solution.py:39
  9.0 6.0 %collective-permute-start.5 = (bf16[3,4,3584]{2,1,0:T(4,128)(2,1)S(1)}, bf16[3,4,3584]{2,1,0:T(4,128)(2,1)S(1)}, u32[]{:S(2)}, u32[]{:S(2)}) collective-permute-start(bf16[3,4,3584]{2,1,0:T(4,128)(2,1)S(1)} %collective-permute-done.3.refs_0_), channel_id=1, source_target_pairs={{0,2},{1,3},{2,0},{3,1},{4,6},{5,7},{6,4},{7,5},{8,10},{9,11},{10,... | collective-permute-start | bytes 258056 | tf_op jit(solution)/shard_map/ppermute | solution.py:39
  11.5 5.5 %collective-permute-start.6 = (bf16[3,4,3584]{2,1,0:T(4,128)(2,1)S(1)}, bf16[3,4,3584]{2,1,0:T(4,128)(2,1)S(1)}, u32[]{:S(2)}, u32[]{:S(2)}) collective-permute-start(bf16[3,4,3584]{2,1,0:T(4,128)(2,1)S(1)} %collective-permute-done.3.refs_0_), channel_id=1, source_target_pairs={{0,3},{1,2},{2,1},{3,0},{4,7},{5,6},{6,5},{7,4},{8,11},{9,10},{10,... | collective-permute-start | bytes 258056 | tf_op jit(solution)/shard_map/ppermute | solution.py:39
  16.9 13.1 %copy-start = (bf16[8,3584]{1,0:T(8,128)(2,1)S(1)}, bf16[8,3584]{1,0:T(8,128)(2,1)}, u32[]{:S(2)}) copy-start(bf16[8,3584]{1,0:T(8,128)(2,1)} %base.3) | copy-start | bytes 172036
  16.9 21.0 %copy-start.1 = (bf16[8,3584]{1,0:T(8,128)(2,1)S(1)}, bf16[8,3584]{1,0:T(8,128)(2,1)}, u32[]{:S(2)}) copy-start(bf16[8,3584]{1,0:T(8,128)(2,1)} %base.2) | copy-start | bytes 172036
  19.6 4.4 %collective-permute-start.10 = (bf16[3,4,3584]{2,1,0:T(4,128)(2,1)S(1)}, bf16[3,4,3584]{2,1,0:T(4,128)(2,1)S(1)}, u32[]{:S(2)}, u32[]{:S(2)}) collective-permute-start(bf16[3,4,3584]{2,1,0:T(4,128)(2,1)S(1)} %get-tuple-element.31), channel_id=1, source_target_pairs={{0,3},{1,2},{2,1},{3,0},{4,7},{5,6},{6,5},{7,4},{8,11},{9,10},{10,... | collective-permute-start | bytes 258056 | tf_op jit(solution)/shard_map/ppermute | solution.py:39
  20.1 4.8 %collective-permute-start.11 = (bf16[3,4,3584]{2,1,0:T(4,128)(2,1)S(1)}, bf16[3,4,3584]{2,1,0:T(4,128)(2,1)S(1)}, u32[]{:S(2)}, u32[]{:S(2)}) collective-permute-start(bf16[3,4,3584]{2,1,0:T(4,128)(2,1)S(1)} %get-tuple-element.32), channel_id=1, source_target_pairs={{0,2},{1,3},{2,0},{3,1},{4,6},{5,7},{6,4},{7,5},{8,10},{9,11},{10,... | collective-permute-start | bytes 258056 | tf_op jit(solution)/shard_map/ppermute | solution.py:39
  20.1 5.4 %collective-permute-start.12 = (bf16[3,4,3584]{2,1,0:T(4,128)(2,1)S(1)}, bf16[3,4,3584]{2,1,0:T(4,128)(2,1)S(1)}, u32[]{:S(2)}, u32[]{:S(2)}) collective-permute-start(bf16[3,4,3584]{2,1,0:T(4,128)(2,1)S(1)} %get-tuple-element.33), channel_id=1, source_target_pairs={{0,1},{1,0},{2,3},{3,2},{4,5},{5,4},{6,7},{7,6},{8,9},{9,8},{10,11... | collective-permute-start | bytes 258056 | tf_op jit(solution)/shard_map/ppermute | solution.py:39
  22.3 5.4 %collective-permute-start.7 = (bf16[3,4,3584]{2,1,0:T(4,128)(2,1)S(1)}, bf16[3,4,3584]{2,1,0:T(4,128)(2,1)S(1)}, u32[]{:S(2)}, u32[]{:S(2)}) collective-permute-start(bf16[3,4,3584]{2,1,0:T(4,128)(2,1)S(1)} %get-tuple-element.27), channel_id=1, source_target_pairs={{0,3},{1,2},{2,1},{3,0},{4,7},{5,6},{6,5},{7,4},{8,11},{9,10},{10,... | collective-permute-start | bytes 258056 | tf_op jit(solution)/shard_map/ppermute | solution.py:39
  22.8 5.3 %collective-permute-start.8 = (bf16[3,4,3584]{2,1,0:T(4,128)(2,1)S(1)}, bf16[3,4,3584]{2,1,0:T(4,128)(2,1)S(1)}, u32[]{:S(2)}, u32[]{:S(2)}) collective-permute-start(bf16[3,4,3584]{2,1,0:T(4,128)(2,1)S(1)} %get-tuple-element.28), channel_id=1, source_target_pairs={{0,2},{1,3},{2,0},{3,1},{4,6},{5,7},{6,4},{7,5},{8,10},{9,11},{10,... | collective-permute-start | bytes 258056 | tf_op jit(solution)/shard_map/ppermute | solution.py:39
  24.0 5.2 %collective-permute-start.9 = (bf16[3,4,3584]{2,1,0:T(4,128)(2,1)S(1)}, bf16[3,4,3584]{2,1,0:T(4,128)(2,1)S(1)}, u32[]{:S(2)}, u32[]{:S(2)}) collective-permute-start(bf16[3,4,3584]{2,1,0:T(4,128)(2,1)S(1)} %get-tuple-element.29), channel_id=1, source_target_pairs={{0,1},{1,0},{2,3},{3,2},{4,5},{5,4},{6,7},{7,6},{8,9},{9,8},{10,11... | collective-permute-start | bytes 258056 | tf_op jit(solution)/shard_map/ppermute | solution.py:39
  25.6 4.4 %collective-permute-start.13 = (bf16[3,4,3584]{2,1,0:T(4,128)(2,1)S(1)}, bf16[3,4,3584]{2,1,0:T(4,128)(2,1)S(1)}, u32[]{:S(2)}, u32[]{:S(2)}) collective-permute-start(bf16[3,4,3584]{2,1,0:T(4,128)(2,1)S(1)} %total.1), channel_id=1, source_target_pairs={{0,4},{2,6},{4,0},{6,2},{1,5},{3,7},{5,1},{7,3},{8,12},{10,14},{12... | collective-permute-start | bytes 258056 | tf_op jit(solution)/shard_map/ppermute | solution.py:44
  30.4 10.5 %collective-permute-start.14 = (bf16[8,3584]{1,0:T(8,128)(2,1)S(1)}, bf16[8,3584]{1,0:T(8,128)(2,1)S(1)}, u32[]{:S(2)}, u32[]{:S(2)}) collective-permute-start(bf16[8,3584]{1,0:T(8,128)(2,1)S(1)} %grad.1), channel_id=1, source_target_pairs={{8,0},{16,8},{24,16},{9,1},{17,9},{25,17},{10,2},{18,10},{26,18},{... | collective-permute-start | bytes 172040 | tf_op jit(solution)/shard_map/ppermute | solution.py:48

commit v4 on v3

--- a/solution.py
+++ b/solution.py
@@ -116,7 +116,7 @@
 
 
 def expert_kernel(cap, count, w_gate, w_up, w_down, acts_in, cot_in, *refs):
-    ins, outs, (acts, cot) = refs[:count], refs[count : 3 * count], refs[3 * count :]
+    ins, outs, (acts, cot) = (refs[0], *refs[count - 1 : 0 : -1]), refs[count : 3 * count], refs[3 * count :]
     width = acts.shape[1]
     tiles = 2 * cap // TILE
     deep = -(-cap // TILE)
@@ -231,11 +231,10 @@
         input_output_aliases={3: 2 * count, 4: 2 * count + 1},
         compiler_params=room(8),
         name="expert",
-    )(*map(near_core, (*held, acts_rows, cot_rows, *far)))
+    )(*map(near_core, (*held, acts_rows, cot_rows, far[0], *far[:0:-1])))
     near, far = parts[:count], parts[count:]
-    order = range(count - 1, 0, -1)
-    far = [far[0]] + [to_member(far[i], members[i][0], -members[i][1]) for i in order]
-    near = [near[0]] + [to_member(near[i], members[i][0], -members[i][1]) for i in order]
+    far = [far[0]] + [to_member(x, half, -by) for x, (half, by) in zip(far[:0:-1], members[:0:-1])]
+    near = [near[0]] + [to_member(x, half, -by) for x, (half, by) in zip(near[1:], members[1:])]
     total = pl.pallas_call(sum_kernel, out_shape=rest, compiler_params=room(4), name="total")(*map(near_core, far))
     back = [to_expert(total[(k - 1) * tiles : k * tiles], -k) for k in range(1, experts)]
     layer_out, section_grad = [

time: 41.7 us -> 39.9 us (0.957)
  waiting for transfers between devices: 8.22 us -> 5.1 us
  starting transfers between devices: 23.4 us -> 24.4 us
    ppermute x12, waiting for transfers between devices: 5.29 us -> 1.59 us  [to_member(): return lax.ppermute(shard, ('expert', 'dp'), pairs)]
    ppermute x1, starting transfers between devices: 7.55 us -> 5.35 us  [to_below(): lax.ppermute(shard, 'pipe', [(p, p - 1) for p in range(1, lax.axis_size('...]
    ppermute x12, starting transfers between devices: 11.3 us -> 12.9 us  [to_member(): return lax.ppermute(shard, ('expert', 'dp'), pairs)]
    ppermute x2, starting transfers between devices: 4.59 us -> 6.16 us  [to_expert(): lax.ppermute(shard, 'expert', [(e, (e + 2 * by) % n) for e in range(n)])]
    ppermute x2, waiting for transfers between devices: 0.92 us -> 1.51 us  [to_expert(): lax.ppermute(shard, 'expert', [(e, (e + 2 * by) % n) for e in range(n)])]
  transfers between devices with their start and end apart: 15 -> 15, of which waited for: 8 -> 5; matrix products, arithmetic and copies ran while one was open for 0% -> 0% of each run, Pallas kernels for 9% -> 9%
where the time goes in v4:
time: 39.9 us; the launch traced here: 39.4 us
  starting transfers between devices  24.4 us (61%)
  Pallas kernels  7.89 us (20%)
  waiting for transfers between devices  5.1 us (13%)
  between operations  1.38 us (3%)
  local copies, waits for them, and re-layouts  0.63 us (2%)
    ppermute x12, starting transfers between devices, to_member(): return lax.ppermute(shard, ('expert', 'dp'), pairs)  12.9 us
    ppermute x2, starting transfers between devices, to_expert(): lax.ppermute(shard, 'expert', [(e, (e + 2 * by) % n) for e in range(n)])  6.16 us
    ppermute x1, starting transfers between devices, to_below(): lax.ppermute(shard, 'pipe', [(p, p - 1) for p in range(1, lax.axis_size('...  5.35 us
    pallas_call x1, Pallas kernels, shards(): pl.pallas_call(functools.partial(expert_kernel, capacity, count), in_spec...  2.67 us
    pallas_call x1, Pallas kernels, shards(): pl.pallas_call(functools.partial(near_kernel, capacity, count), in_specs=...  2.63 us
    ppermute x1, waiting for transfers between devices, to_below(): lax.ppermute(shard, 'pipe', [(p, p - 1) for p in range(1, lax.axis_size('...  2 us
    ppermute x12, waiting for transfers between devices, to_member(): return lax.ppermute(shard, ('expert', 'dp'), pairs)  1.59 us
    ppermute x2, waiting for transfers between devices, to_expert(): lax.ppermute(shard, 'expert', [(e, (e + 2 * by) % n) for e in range(n)])  1.51 us
  transfers between devices with their start and end apart: 15, of which 5 were waited for; matrix products, arithmetic and copies ran while one was open for 0% of the time, Pallas kernels for 9%

profile of v4, /device:TPU:1, one launch (start us, length us, event | category | flops | bytes accessed | tf_op | source)
XLA Modules:
  0.0 39.4 jit_solution(12679648875165861841)
XLA Ops:
  0.6 1.2 %pack.1 = (f32[2,8,128]{2,1,0:T(8,128)S(1)}, bf16[3,4,3584]{2,1,0:T(4,128)(2,1)S(1)}, bf16[3,4,3584]{2,1,0:T(4,128)(2,1)S(1)}) custom-call(s32[1,8]{1,0:T(1,128)} %bitcast.8, bf16[1,8]{1,0:T(2,128)(2,1)} %bitcast.9, bf16[8,3584]{1,0:T(8,128)(2,1)} %base.2, bf16[8,3584]{1,0:T(8,128)(2,1)} %base.3), custom_call_target="tpu_custom_call" | custom-call | tf_op jit(solution)/shard_map/pack/pallas_call | solution.py:197
  1.9 3.2 %collective-permute-start.3 = (bf16[3,4,3584]{2,1,0:T(4,128)(2,1)S(1)}, bf16[3,4,3584]{2,1,0:T(4,128)(2,1)S(1)}, u32[]{:S(2)}, u32[]{:S(2)}) collective-permute-start(bf16[3,4,3584]{2,1,0:T(4,128)(2,1)S(1)} %get-tuple-element.25), channel_id=1, source_target_pairs={{0,4},{2,6},{4,0},{6,2},{1,5},{3,7},{5,1},{7,3},{8,12},{10,14},{12... | collective-permute-start | bytes 258056 | tf_op jit(solution)/shard_map/ppermute | solution.py:44
  5.1 1.2 %collective-permute-start = (bf16[3,4,3584]{2,1,0:T(4,128)(2,1)S(1)}, bf16[3,4,3584]{2,1,0:T(4,128)(2,1)S(1)}, u32[]{:S(2)}, u32[]{:S(2)}) collective-permute-start(bf16[3,4,3584]{2,1,0:T(4,128)(2,1)S(1)} %get-tuple-element.19.refs_3_), channel_id=1, source_target_pairs={{0,1},{1,0},{2,3},{3,2},{4,5},{5,4},{6,7},{7,6},{8,9},{9,8},{10,11... | collective-permute-start | bytes 258056 | tf_op jit(solution)/shard_map/ppermute | solution.py:39
  6.3 1.3 %collective-permute-start.1 = (bf16[3,4,3584]{2,1,0:T(4,128)(2,1)S(1)}, bf16[3,4,3584]{2,1,0:T(4,128)(2,1)S(1)}, u32[]{:S(2)}, u32[]{:S(2)}) collective-permute-start(bf16[3,4,3584]{2,1,0:T(4,128)(2,1)S(1)} %get-tuple-element.19.refs_3_), channel_id=1, source_target_pairs={{0,2},{1,3},{2,0},{3,1},{4,6},{5,7},{6,4},{7,5},{8,10},{9,11},{10,... | collective-permute-start | bytes 258056 | tf_op jit(solution)/shard_map/ppermute | solution.py:39
  7.6 0.1 collective-permute-start.2
  7.7 0.0 collective-permute-done.3.refs_0_
  7.7 3.4 %collective-permute-start.4 = (bf16[3,4,3584]{2,1,0:T(4,128)(2,1)S(1)}, bf16[3,4,3584]{2,1,0:T(4,128)(2,1)S(1)}, u32[]{:S(2)}, u32[]{:S(2)}) collective-permute-start(bf16[3,4,3584]{2,1,0:T(4,128)(2,1)S(1)} %collective-permute-done.3.refs_0_), channel_id=1, source_target_pairs={{0,3},{1,2},{2,1},{3,0},{4,7},{5,6},{6,5},{7,4},{8,11},{9,10},{10,... | collective-permute-start | bytes 258056 | tf_op jit(solution)/shard_map/ppermute | solution.py:39
  11.2 0.0 collective-permute-start.5
  11.2 0.0 collective-permute-done.refs_4_
  11.2 0.3 collective-permute-start.6
  11.5 0.0 collective-permute-done.1.refs_5_
  11.5 0.8 %collective-permute-done.2.refs_6_ = bf16[3,4,3584]{2,1,0:T(4,128)(2,1)S(1)} collective-permute-done((bf16[3,4,3584]{2,1,0:T(4,128)(2,1)S(1)}, bf16[3,4,3584]{2,1,0:T(4,128)(2,1)S(1)}, u32[]{:S(2)}, u32[]{:S(2)}) %collective-permute-start.2) | collective-permute-done | bytes 86048 | tf_op jit(solution)/shard_map/ppermute | solution.py:39
  12.3 2.6 %near.1 = (bf16[64,3584]{1,0:T(8,128)(2,1)S(1)}, bf16[64,3584]{1,0:T(8,128)(2,1)S(1)}, bf16[3584,256]{1,0:T(8,128)(2,1)S(1)}, bf16[3584,256]{1,0:T(8,128)(2,1)S(1)}, bf16[256,3584]{1,0:T(8,128)(2,1)S(1)}) custom-call(bf16[3584,256]{1,0:T(8,128)(2,1)} %bitcast.5, bf16[3584,256]{1,0:T(8,128)(2,1)} %bitcast.6, bf16[256,3584]{1,0:T(8,128)(2,1)} %bitcast.7, ...), custom_call_target="tpu_custom_call" | custom-call | tf_op jit(solution)/shard_map/near/pallas_call | solution.py:217
  15.0 0.0 collective-permute-done.4.refs_1_
  15.0 0.6 %collective-permute-done.5.refs_2_ = bf16[3,4,3584]{2,1,0:T(4,128)(2,1)S(1)} collective-permute-done((bf16[3,4,3584]{2,1,0:T(4,128)(2,1)S(1)}, bf16[3,4,3584]{2,1,0:T(4,128)(2,1)S(1)}, u32[]{:S(2)}, u32[]{:S(2)}) %collective-permute-start.5) | collective-permute-done | bytes 86048 | tf_op jit(solution)/shard_map/ppermute | solution.py:39
  15.6 0.1 collective-permute-done.6.refs_3_
  15.7 0.0 copy-start
  15.7 0.0 copy-start.1
  15.7 2.7 %expert.1 = (bf16[3,4,3584]{2,1,0:T(4,128)(2,1)S(1)}, bf16[3,4,3584]{2,1,0:T(4,128)(2,1)S(1)}, bf16[3,4,3584]{2,1,0:T(4,128)(2,1)S(1)}, bf16[3,4,3584]{2,1,0:T(4...) custom-call(bf16[3584,256]{1,0:T(8,128)(2,1)S(1)} %get-tuple-element, ...), custom_call_target="tpu_custom_call", output_to_operand_aliasing={{8}: (3, {}), {9}: (4, {})} | custom-call | tf_op jit(solution)/shard_map/expert/pallas_call | solution.py:226
  18.4 2.2 %collective-permute-start.10 = (bf16[3,4,3584]{2,1,0:T(4,128)(2,1)S(1)}, bf16[3,4,3584]{2,1,0:T(4,128)(2,1)S(1)}, u32[]{:S(2)}, u32[]{:S(2)}) collective-permute-start(bf16[3,4,3584]{2,1,0:T(4,128)(2,1)S(1)} %get-tuple-element.31), channel_id=1, source_target_pairs={{0,3},{1,2},{2,1},{3,0},{4,7},{5,6},{6,5},{7,4},{8,11},{9,10},{10,... | collective-permute-start | bytes 258056 | tf_op jit(solution)/shard_map/ppermute | solution.py:39
  20.6 0.1 collective-permute-start.11
  20.7 0.6 %collective-permute-start.12 = (bf16[3,4,3584]{2,1,0:T(4,128)(2,1)S(1)}, bf16[3,4,3584]{2,1,0:T(4,128)(2,1)S(1)}, u32[]{:S(2)}, u32[]{:S(2)}) collective-permute-start(bf16[3,4,3584]{2,1,0:T(4,128)(2,1)S(1)} %get-tuple-element.33), channel_id=1, source_target_pairs={{0,1},{1,0},{2,3},{3,2},{4,5},{5,4},{6,7},{7,6},{8,9},{9,8},{10,11... | collective-permute-start | bytes 258056 | tf_op jit(solution)/shard_map/ppermute | solution.py:39
  21.3 0.8 %collective-permute-start.7 = (bf16[3,4,3584]{2,1,0:T(4,128)(2,1)S(1)}, bf16[3,4,3584]{2,1,0:T(4,128)(2,1)S(1)}, u32[]{:S(2)}, u32[]{:S(2)}) collective-permute-start(bf16[3,4,3584]{2,1,0:T(4,128)(2,1)S(1)} %get-tuple-element.27), channel_id=1, source_target_pairs={{0,1},{1,0},{2,3},{3,2},{4,5},{5,4},{6,7},{7,6},{8,9},{9,8},{10,11... | collective-permute-start | bytes 258056 | tf_op jit(solution)/shard_map/ppermute | solution.py:39
  22.2 1.4 %collective-permute-start.8 = (bf16[3,4,3584]{2,1,0:T(4,128)(2,1)S(1)}, bf16[3,4,3584]{2,1,0:T(4,128)(2,1)S(1)}, u32[]{:S(2)}, u32[]{:S(2)}) collective-permute-start(bf16[3,4,3584]{2,1,0:T(4,128)(2,1)S(1)} %get-tuple-element.28), channel_id=1, source_target_pairs={{0,2},{1,3},{2,0},{3,1},{4,6},{5,7},{6,4},{7,5},{8,10},{9,11},{10,... | collective-permute-start | bytes 258056 | tf_op jit(solution)/shard_map/ppermute | solution.py:39
  23.6 0.0 collective-permute-done.10.refs_1_
  23.6 1.3 %collective-permute-start.9 = (bf16[3,4,3584]{2,1,0:T(4,128)(2,1)S(1)}, bf16[3,4,3584]{2,1,0:T(4,128)(2,1)S(1)}, u32[]{:S(2)}, u32[]{:S(2)}) collective-permute-start(bf16[3,4,3584]{2,1,0:T(4,128)(2,1)S(1)} %get-tuple-element.29), channel_id=1, source_target_pairs={{0,3},{1,2},{2,1},{3,0},{4,7},{5,6},{6,5},{7,4},{8,11},{9,10},{10,... | collective-permute-start | bytes 258056 | tf_op jit(solution)/shard_map/ppermute | solution.py:39
  24.9 0.0 collective-permute-done.11.refs_2_
  24.9 0.0 collective-permute-done.12.refs_3_
  24.9 0.1 total.1
  24.9 2.9 %collective-permute-start.13 = (bf16[3,4,3584]{2,1,0:T(4,128)(2,1)S(1)}, bf16[3,4,3584]{2,1,0:T(4,128)(2,1)S(1)}, u32[]{:S(2)}, u32[]{:S(2)}) collective-permute-start(bf16[3,4,3584]{2,1,0:T(4,128)(2,1)S(1)} %total.1), channel_id=1, source_target_pairs={{0,4},{2,6},{4,0},{6,2},{1,5},{3,7},{5,1},{7,3},{8,12},{10,14},{12... | collective-permute-start | bytes 258056 | tf_op jit(solution)/shard_map/ppermute | solution.py:44
  28.5 0.0 collective-permute-done.7.refs_1_
  28.6 0.0 collective-permute-done.8.refs_2_
  28.6 0.0 collective-permute-done.9.refs_3_
  28.6 1.5 %collective-permute-done.13.refs_4_ = bf16[3,4,3584]{2,1,0:T(4,128)(2,1)S(1)} collective-permute-done((bf16[3,4,3584]{2,1,0:T(4,128)(2,1)S(1)}, bf16[3,4,3584]{2,1,0:T(4,128)(2,1)S(1)}, u32[]{:S(2)}, u32[]{:S(2)}) %collective-permute-start.13) | collective-permute-done | bytes 86048 | tf_op jit(solution)/shard_map/ppermute | solution.py:44
  30.1 0.0 copy-done
  30.1 0.3 grad.1
  30.4 5.4 %collective-permute-start.14 = (bf16[8,3584]{1,0:T(8,128)(2,1)S(1)}, bf16[8,3584]{1,0:T(8,128)(2,1)S(1)}, u32[]{:S(2)}, u32[]{:S(2)}) collective-permute-start(bf16[8,3584]{1,0:T(8,128)(2,1)S(1)} %grad.1), channel_id=1, source_target_pairs={{8,0},{16,8},{24,16},{9,1},{17,9},{25,17},{10,2},{18,10},{26,18},{... | collective-permute-start | bytes 172040 | tf_op jit(solution)/shard_map/ppermute | solution.py:48
  35.8 0.0 copy-done.1
  35.8 1.0 %out.1 = bf16[8,3584]{1,0:T(8,128)(2,1)} custom-call(s32[1,1]{1,0:T(1,128)S(6)} %copy.15.keep, f32[2,8,128]{2,1,0:T(8,128)S(1)} %get-tuple-element.18.mix, bf16[8,3584]{1,0:T(8,128)(2,1)S(1)} %copy-done.1, bf16[3,4,3584]{2,1,0:T(4,128)(2,1)S(1)} %get-tuple-element.26.refs_0_, bf16[3,4,3584]{2,1,0:T(4,128)(2,1)S(1)} %collective-permute-done.7.refs_1_, ...), custom_call_target="tpu_custom_call" | custom-call | tf_op jit(solution)/shard_map/out/pallas_call | solution.py:241
  36.7 2.0 %collective-permute-done.14 = bf16[8,3584]{1,0:T(8,128)(2,1)S(1)} collective-permute-done((bf16[8,3584]{1,0:T(8,128)(2,1)S(1)}, bf16[8,3584]{1,0:T(8,128)(2,1)S(1)}, u32[]{:S(2)}, u32[]{:S(2)}) %collective-permute-start.14) | collective-permute-done | bytes 57376 | tf_op jit(solution)/shard_map/ppermute | solution.py:48
  38.7 0.6 %copy.16 = bf16[8,3584]{1,0:T(8,128)(2,1)} copy(bf16[8,3584]{1,0:T(8,128)(2,1)S(1)} %collective-permute-done.14) | data formatting | bytes 114688
Async XLA Ops:
  1.9 5.9 %collective-permute-start.3 = (bf16[3,4,3584]{2,1,0:T(4,128)(2,1)S(1)}, bf16[3,4,3584]{2,1,0:T(4,128)(2,1)S(1)}, u32[]{:S(2)}, u32[]{:S(2)}) collective-permute-start(bf16[3,4,3584]{2,1,0:T(4,128)(2,1)S(1)} %get-tuple-element.25), channel_id=1, source_target_pairs={{0,4},{2,6},{4,0},{6,2},{1,5},{3,7},{5,1},{7,3},{8,12},{10,14},{12... | collective-permute-start | bytes 258056 | tf_op jit(solution)/shard_map/ppermute | solution.py:44
  5.1 6.1 %collective-permute-start = (bf16[3,4,3584]{2,1,0:T(4,128)(2,1)S(1)}, bf16[3,4,3584]{2,1,0:T(4,128)(2,1)S(1)}, u32[]{:S(2)}, u32[]{:S(2)}) collective-permute-start(bf16[3,4,3584]{2,1,0:T(4,128)(2,1)S(1)} %get-tuple-element.19.refs_3_), channel_id=1, source_target_pairs={{0,1},{1,0},{2,3},{3,2},{4,5},{5,4},{6,7},{7,6},{8,9},{9,8},{10,11... | collective-permute-start | bytes 258056 | tf_op jit(solution)/shard_map/ppermute | solution.py:39
  6.3 5.2 %collective-permute-start.1 = (bf16[3,4,3584]{2,1,0:T(4,128)(2,1)S(1)}, bf16[3,4,3584]{2,1,0:T(4,128)(2,1)S(1)}, u32[]{:S(2)}, u32[]{:S(2)}) collective-permute-start(bf16[3,4,3584]{2,1,0:T(4,128)(2,1)S(1)} %get-tuple-element.19.refs_3_), channel_id=1, source_target_pairs={{0,2},{1,3},{2,0},{3,1},{4,6},{5,7},{6,4},{7,5},{8,10},{9,11},{10,... | collective-permute-start | bytes 258056 | tf_op jit(solution)/shard_map/ppermute | solution.py:39
  7.6 4.7 %collective-permute-start.2 = (bf16[3,4,3584]{2,1,0:T(4,128)(2,1)S(1)}, bf16[3,4,3584]{2,1,0:T(4,128)(2,1)S(1)}, u32[]{:S(2)}, u32[]{:S(2)}) collective-permute-start(bf16[3,4,3584]{2,1,0:T(4,128)(2,1)S(1)} %get-tuple-element.19.refs_3_), channel_id=1, source_target_pairs={{0,3},{1,2},{2,1},{3,0},{4,7},{5,6},{6,5},{7,4},{8,11},{9,10},{10,... | collective-permute-start | bytes 258056 | tf_op jit(solution)/shard_map/ppermute | solution.py:39
  7.7 7.2 %collective-permute-start.4 = (bf16[3,4,3584]{2,1,0:T(4,128)(2,1)S(1)}, bf16[3,4,3584]{2,1,0:T(4,128)(2,1)S(1)}, u32[]{:S(2)}, u32[]{:S(2)}) collective-permute-start(bf16[3,4,3584]{2,1,0:T(4,128)(2,1)S(1)} %collective-permute-done.3.refs_0_), channel_id=1, source_target_pairs={{0,3},{1,2},{2,1},{3,0},{4,7},{5,6},{6,5},{7,4},{8,11},{9,10},{10,... | collective-permute-start | bytes 258056 | tf_op jit(solution)/shard_map/ppermute | solution.py:39
  11.2 4.4 %collective-permute-start.5 = (bf16[3,4,3584]{2,1,0:T(4,128)(2,1)S(1)}, bf16[3,4,3584]{2,1,0:T(4,128)(2,1)S(1)}, u32[]{:S(2)}, u32[]{:S(2)}) collective-permute-start(bf16[3,4,3584]{2,1,0:T(4,128)(2,1)S(1)} %collective-permute-done.3.refs_0_), channel_id=1, source_target_pairs={{0,2},{1,3},{2,0},{3,1},{4,6},{5,7},{6,4},{7,5},{8,10},{9,11},{10,... | collective-permute-start | bytes 258056 | tf_op jit(solution)/shard_map/ppermute | solution.py:39
  11.2 4.5 %collective-permute-start.6 = (bf16[3,4,3584]{2,1,0:T(4,128)(2,1)S(1)}, bf16[3,4,3584]{2,1,0:T(4,128)(2,1)S(1)}, u32[]{:S(2)}, u32[]{:S(2)}) collective-permute-start(bf16[3,4,3584]{2,1,0:T(4,128)(2,1)S(1)} %collective-permute-done.3.refs_0_), channel_id=1, source_target_pairs={{0,1},{1,0},{2,3},{3,2},{4,5},{5,4},{6,7},{7,6},{8,9},{9,8},{10,11... | collective-permute-start | bytes 258056 | tf_op jit(solution)/shard_map/ppermute | solution.py:39
  15.7 14.4 %copy-start = (bf16[8,3584]{1,0:T(8,128)(2,1)S(1)}, bf16[8,3584]{1,0:T(8,128)(2,1)}, u32[]{:S(2)}) copy-start(bf16[8,3584]{1,0:T(8,128)(2,1)} %base.3) | copy-start | bytes 172036
  15.7 20.1 %copy-start.1 = (bf16[8,3584]{1,0:T(8,128)(2,1)S(1)}, bf16[8,3584]{1,0:T(8,128)(2,1)}, u32[]{:S(2)}) copy-start(bf16[8,3584]{1,0:T(8,128)(2,1)} %base.2) | copy-start | bytes 172036
  18.4 5.2 %collective-permute-start.10 = (bf16[3,4,3584]{2,1,0:T(4,128)(2,1)S(1)}, bf16[3,4,3584]{2,1,0:T(4,128)(2,1)S(1)}, u32[]{:S(2)}, u32[]{:S(2)}) collective-permute-start(bf16[3,4,3584]{2,1,0:T(4,128)(2,1)S(1)} %get-tuple-element.31), channel_id=1, source_target_pairs={{0,3},{1,2},{2,1},{3,0},{4,7},{5,6},{6,5},{7,4},{8,11},{9,10},{10,... | collective-permute-start | bytes 258056 | tf_op jit(solution)/shard_map/ppermute | solution.py:39
  20.6 4.2 %collective-permute-start.11 = (bf16[3,4,3584]{2,1,0:T(4,128)(2,1)S(1)}, bf16[3,4,3584]{2,1,0:T(4,128)(2,1)S(1)}, u32[]{:S(2)}, u32[]{:S(2)}) collective-permute-start(bf16[3,4,3584]{2,1,0:T(4,128)(2,1)S(1)} %get-tuple-element.32), channel_id=1, source_target_pairs={{0,2},{1,3},{2,0},{3,1},{4,6},{5,7},{6,4},{7,5},{8,10},{9,11},{10,... | collective-permute-start | bytes 258056 | tf_op jit(solution)/shard_map/ppermute | solution.py:39
  20.7 4.2 %collective-permute-start.12 = (bf16[3,4,3584]{2,1,0:T(4,128)(2,1)S(1)}, bf16[3,4,3584]{2,1,0:T(4,128)(2,1)S(1)}, u32[]{:S(2)}, u32[]{:S(2)}) collective-permute-start(bf16[3,4,3584]{2,1,0:T(4,128)(2,1)S(1)} %get-tuple-element.33), channel_id=1, source_target_pairs={{0,1},{1,0},{2,3},{3,2},{4,5},{5,4},{6,7},{7,6},{8,9},{9,8},{10,11... | collective-permute-start | bytes 258056 | tf_op jit(solution)/shard_map/ppermute | solution.py:39
  21.3 7.2 %collective-permute-start.7 = (bf16[3,4,3584]{2,1,0:T(4,128)(2,1)S(1)}, bf16[3,4,3584]{2,1,0:T(4,128)(2,1)S(1)}, u32[]{:S(2)}, u32[]{:S(2)}) collective-permute-start(bf16[3,4,3584]{2,1,0:T(4,128)(2,1)S(1)} %get-tuple-element.27), channel_id=1, source_target_pairs={{0,1},{1,0},{2,3},{3,2},{4,5},{5,4},{6,7},{7,6},{8,9},{9,8},{10,11... | collective-permute-start | bytes 258056 | tf_op jit(solution)/shard_map/ppermute | solution.py:39
  22.2 6.4 %collective-permute-start.8 = (bf16[3,4,3584]{2,1,0:T(4,128)(2,1)S(1)}, bf16[3,4,3584]{2,1,0:T(4,128)(2,1)S(1)}, u32[]{:S(2)}, u32[]{:S(2)}) collective-permute-start(bf16[3,4,3584]{2,1,0:T(4,128)(2,1)S(1)} %get-tuple-element.28), channel_id=1, source_target_pairs={{0,2},{1,3},{2,0},{3,1},{4,6},{5,7},{6,4},{7,5},{8,10},{9,11},{10,... | collective-permute-start | bytes 258056 | tf_op jit(solution)/shard_map/ppermute | solution.py:39
  23.6 5.0 %collective-permute-start.9 = (bf16[3,4,3584]{2,1,0:T(4,128)(2,1)S(1)}, bf16[3,4,3584]{2,1,0:T(4,128)(2,1)S(1)}, u32[]{:S(2)}, u32[]{:S(2)}) collective-permute-start(bf16[3,4,3584]{2,1,0:T(4,128)(2,1)S(1)} %get-tuple-element.29), channel_id=1, source_target_pairs={{0,3},{1,2},{2,1},{3,0},{4,7},{5,6},{6,5},{7,4},{8,11},{9,10},{10,... | collective-permute-start | bytes 258056 | tf_op jit(solution)/shard_map/ppermute | solution.py:39
  24.9 5.1 %collective-permute-start.13 = (bf16[3,4,3584]{2,1,0:T(4,128)(2,1)S(1)}, bf16[3,4,3584]{2,1,0:T(4,128)(2,1)S(1)}, u32[]{:S(2)}, u32[]{:S(2)}) collective-permute-start(bf16[3,4,3584]{2,1,0:T(4,128)(2,1)S(1)} %total.1), channel_id=1, source_target_pairs={{0,4},{2,6},{4,0},{6,2},{1,5},{3,7},{5,1},{7,3},{8,12},{10,14},{12... | collective-permute-start | bytes 258056 | tf_op jit(solution)/shard_map/ppermute | solution.py:44
  30.4 8.3 %collective-permute-start.14 = (bf16[8,3584]{1,0:T(8,128)(2,1)S(1)}, bf16[8,3584]{1,0:T(8,128)(2,1)S(1)}, u32[]{:S(2)}, u32[]{:S(2)}) collective-permute-start(bf16[8,3584]{1,0:T(8,128)(2,1)S(1)} %grad.1), channel_id=1, source_target_pairs={{8,0},{16,8},{24,16},{9,1},{17,9},{25,17},{10,2},{18,10},{26,18},{... | collective-permute-start | bytes 172040 | tf_op jit(solution)/shard_map/ppermute | solution.py:48

commit v5 on v4

--- a/solution.py
+++ b/solution.py
@@ -10,6 +10,7 @@
 CROSS = (((1,), (1,)), ((), ()))
 LANES = 128
 TILE = 4
+SPLIT = 1
 MIB = 1024 * 1024
 
 
@@ -98,16 +99,22 @@
 
 def fill(rows, at, ins, first, deep, tiles):
     spots = [(ref, b + first + i) for ref in ins for b in range(0, ref.shape[0], tiles) for i in range(deep)]
-    for i in range(0, len(spots), 2):
-        pair = [ref[b] for ref, b in spots[i : i + 2]]
-        rows[at + i * TILE : at + (i + 2) * TILE] = jnp.concatenate(pair, axis=0)
-
-
-def near_kernel(cap, count, *refs):
+    while spots:
+        take = 2 if at % (2 * TILE) == 0 and len(spots) > 1 else 1
+        some = [ref[b] for ref, b in spots[:take]]
+        rows[at : at + take * TILE] = jnp.concatenate(some, axis=0) if take > 1 else some[0]
+        at, spots = at + take * TILE, spots[take:]
+
+
+def near_kernel(cap, count, split, *refs):
     stored, ins, (acts, cot), held, sems = refs[:3], refs[3 : 3 + count], refs[3 + count : 5 + count], refs[5 + count : -1], refs[-1]
-    copies = [pltpu.make_async_copy(s, h, sems.at[i]) for i, (s, h) in enumerate(zip(stored, held))]
-    for copy in copies:
-        copy.start()
+    copies = []
+    for store, hold in zip(stored, held):
+        part = store.shape[0] // split
+        for i in range(split):
+            span = pl.ds(i * part, part)
+            copies.append(pltpu.make_async_copy(store.at[span], hold.at[span], sems.at[len(copies)]))
+            copies[-1].start()
     deep, tiles = -(-cap // TILE), 2 * cap // TILE
     fill(acts, 0, ins, 0, deep, tiles)
     fill(cot, 0, ins, tiles - deep, deep, tiles)
@@ -116,7 +123,8 @@
 
 
 def expert_kernel(cap, count, w_gate, w_up, w_down, acts_in, cot_in, *refs):
-    ins, outs, (acts, cot) = (refs[0], *refs[count - 1 : 0 : -1]), refs[count : 3 * count], refs[3 * count :]
+    late, *ins = refs[: count + 1]
+    ins, outs, (acts, cot) = [ins[0], *ins[:0:-1]], refs[count + 1 : 3 * count + 1], refs[3 * count + 1 :]
     width = acts.shape[1]
     tiles = 2 * cap // TILE
     deep = -(-cap // TILE)
@@ -124,8 +132,9 @@
     places = [(out, b) for out in outs for b in range(0, out.shape[0], tiles)]
     tall = len(places) * deep * TILE
     near = count * deep * TILE
-    fill(acts, near, ins, 0, deep, tiles)
-    fill(cot, near, ins, tiles - deep, deep, tiles)
+    near -= deep * TILE
+    fill(acts, near, [late, *ins], 0, deep, tiles)
+    fill(cot, near, [late, *ins], tiles - deep, deep, tiles)
     grad_hidden = dot(w_down[...], cot[...], CROSS).T
     gate_pre = dot(acts[...], w_gate[...])
     up_pre = dot(acts[...], w_up[...])
@@ -215,23 +224,23 @@
     count = len(members)
     laid = pltpu.VMEM((tall, width), jnp.bfloat16)
     acts_rows, cot_rows, *held = pl.pallas_call(
-        functools.partial(near_kernel, capacity, count),
-        in_specs=[far_off] * 3 + [vmem] * count,
+        functools.partial(near_kernel, capacity, count - 1, SPLIT),
+        in_specs=[far_off] * 3 + [vmem] * (count - 1),
         out_specs=[vmem] * 5,
         out_shape=[laid] * 2 + [pltpu.VMEM(w.shape, w.dtype) for w in weights],
-        scratch_shapes=[pltpu.SemaphoreType.DMA((3,))],
+        scratch_shapes=[pltpu.SemaphoreType.DMA((3 * SPLIT,))],
         compiler_params=room(4),
         name="near",
-    )(*map(in_hbm, weights), *map(near_core, near))
+    )(*map(in_hbm, weights), *map(near_core, near[:-1]))
     *parts, _, _ = pl.pallas_call(
         functools.partial(expert_kernel, capacity, count),
-        in_specs=[vmem] * (5 + count),
+        in_specs=[vmem] * (6 + count),
         out_specs=[vmem] * (2 * count + 2),
         out_shape=[block] * count + [rest] * count + [laid] * 2,
         input_output_aliases={3: 2 * count, 4: 2 * count + 1},
         compiler_params=room(8),
         name="expert",
-    )(*map(near_core, (*held, acts_rows, cot_rows, far[0], *far[:0:-1])))
+    )(*map(near_core, (*held, acts_rows, cot_rows, near[-1], far[0], *far[:0:-1])))
     near, far = parts[:count], parts[count:]
     far = [far[0]] + [to_member(x, half, -by) for x, (half, by) in zip(far[:0:-1], members[:0:-1])]
     near = [near[0]] + [to_member(x, half, -by) for x, (half, by) in zip(near[1:], members[1:])]

time: 39.9 us -> 39.9 us (level)
  transfers between devices with their start and end apart: 15 -> 15, of which waited for: 5 -> 4; matrix products, arithmetic and copies ran while one was open for 0% -> 0% of each run, Pallas kernels for 9% -> 9%
where the time goes in v5:
time: 39.9 us; the launch traced here: 39.4 us
  starting transfers between devices  24.2 us (61%)
  Pallas kernels  7.95 us (20%)
  waiting for transfers between devices  5.22 us (13%)
  between operations  1.38 us (3%)
  local copies, waits for them, and re-layouts  0.63 us (2%)
    ppermute x12, starting transfers between devices, to_member(): return lax.ppermute(shard, ('expert', 'dp'), pairs)  12.9 us
    ppermute x2, starting transfers between devices, to_expert(): lax.ppermute(shard, 'expert', [(e, (e + 2 * by) % n) for e in range(n)])  6.2 us
    ppermute x1, starting transfers between devices, to_below(): lax.ppermute(shard, 'pipe', [(p, p - 1) for p in range(1, lax.axis_size('...  5.19 us
    pallas_call x1, Pallas kernels, shards(): pl.pallas_call(functools.partial(expert_kernel, capacity, count), in_spec...  2.73 us
    pallas_call x1, Pallas kernels, shards(): pl.pallas_call(functools.partial(near_kernel, capacity, count - 1, SPLIT)...  2.63 us
    ppermute x1, waiting for transfers between devices, to_below(): lax.ppermute(shard, 'pipe', [(p, p - 1) for p in range(1, lax.axis_size('...  2 us
    ppermute x2, waiting for transfers between devices, to_expert(): lax.ppermute(shard, 'expert', [(e, (e + 2 * by) % n) for e in range(n)])  1.64 us
    ppermute x12, waiting for transfers between devices, to_member(): return lax.ppermute(shard, ('expert', 'dp'), pairs)  1.58 us
  transfers between devices with their start and end apart: 15, of which 4 were waited for; matrix products, arithmetic and copies ran while one was open for 0% of the time, Pallas kernels for 9%

profile of v5, /device:TPU:1, one launch (start us, length us, event | category | flops | bytes accessed | tf_op | source)
XLA Modules:
  0.0 39.4 jit_solution(18297340157370472788)
XLA Ops:
  0.6 1.2 %pack.1 = (f32[2,8,128]{2,1,0:T(8,128)S(1)}, bf16[3,4,3584]{2,1,0:T(4,128)(2,1)S(1)}, bf16[3,4,3584]{2,1,0:T(4,128)(2,1)S(1)}) custom-call(s32[1,8]{1,0:T(1,128)} %bitcast.8, bf16[1,8]{1,0:T(2,128)(2,1)} %bitcast.9, bf16[8,3584]{1,0:T(8,128)(2,1)} %base.2, bf16[8,3584]{1,0:T(8,128)(2,1)} %base.3), custom_call_target="tpu_custom_call" | custom-call | tf_op jit(solution)/shard_map/pack/pallas_call | solution.py:206
  1.9 3.2 %collective-permute-start.3 = (bf16[3,4,3584]{2,1,0:T(4,128)(2,1)S(1)}, bf16[3,4,3584]{2,1,0:T(4,128)(2,1)S(1)}, u32[]{:S(2)}, u32[]{:S(2)}) collective-permute-start(bf16[3,4,3584]{2,1,0:T(4,128)(2,1)S(1)} %get-tuple-element.25), channel_id=1, source_target_pairs={{0,4},{2,6},{4,0},{6,2},{1,5},{3,7},{5,1},{7,3},{8,12},{10,14},{12... | collective-permute-start | bytes 258056 | tf_op jit(solution)/shard_map/ppermute | solution.py:45
  5.1 1.2 %collective-permute-start = (bf16[3,4,3584]{2,1,0:T(4,128)(2,1)S(1)}, bf16[3,4,3584]{2,1,0:T(4,128)(2,1)S(1)}, u32[]{:S(2)}, u32[]{:S(2)}) collective-permute-start(bf16[3,4,3584]{2,1,0:T(4,128)(2,1)S(1)} %get-tuple-element.19.refs_3_), channel_id=1, source_target_pairs={{0,1},{1,0},{2,3},{3,2},{4,5},{5,4},{6,7},{7,6},{8,9},{9,8},{10,11... | collective-permute-start | bytes 258056 | tf_op jit(solution)/shard_map/ppermute | solution.py:40
  6.3 1.3 %collective-permute-start.1 = (bf16[3,4,3584]{2,1,0:T(4,128)(2,1)S(1)}, bf16[3,4,3584]{2,1,0:T(4,128)(2,1)S(1)}, u32[]{:S(2)}, u32[]{:S(2)}) collective-permute-start(bf16[3,4,3584]{2,1,0:T(4,128)(2,1)S(1)} %get-tuple-element.19.refs_3_), channel_id=1, source_target_pairs={{0,2},{1,3},{2,0},{3,1},{4,6},{5,7},{6,4},{7,5},{8,10},{9,11},{10,... | collective-permute-start | bytes 258056 | tf_op jit(solution)/shard_map/ppermute | solution.py:40
  7.6 0.1 collective-permute-start.2
  7.7 0.0 collective-permute-done.3.refs_1_
  7.7 3.4 %collective-permute-start.4 = (bf16[3,4,3584]{2,1,0:T(4,128)(2,1)S(1)}, bf16[3,4,3584]{2,1,0:T(4,128)(2,1)S(1)}, u32[]{:S(2)}, u32[]{:S(2)}) collective-permute-start(bf16[3,4,3584]{2,1,0:T(4,128)(2,1)S(1)} %collective-permute-done.3.refs_1_), channel_id=1, source_target_pairs={{0,3},{1,2},{2,1},{3,0},{4,7},{5,6},{6,5},{7,4},{8,11},{9,10},{10,... | collective-permute-start | bytes 258056 | tf_op jit(solution)/shard_map/ppermute | solution.py:40
  11.2 0.0 collective-permute-start.5
  11.2 0.0 collective-permute-done.refs_4_
  11.2 0.3 collective-permute-start.6
  11.5 0.0 collective-permute-done.1.refs_5_
  11.5 2.6 %near.1 = (bf16[64,3584]{1,0:T(8,128)(2,1)S(1)}, bf16[64,3584]{1,0:T(8,128)(2,1)S(1)}, bf16[3584,256]{1,0:T(8,128)(2,1)S(1)}, bf16[3584,256]{1,0:T(8,128)(2,1)S(1)}, bf16[256,3584]{1,0:T(8,128)(2,1)S(1)}) custom-call(bf16[3584,256]{1,0:T(8,128)(2,1)} %bitcast.5, bf16[3584,256]{1,0:T(8,128)(2,1)} %bitcast.6, bf16[256,3584]{1,0:T(8,128)(2,1)} %bitcast.7, ...), custom_call_target="tpu_custom_call" | custom-call | tf_op jit(solution)/shard_map/near/pallas_call | solution.py:226
  14.1 0.0 collective-permute-done.2.refs_0_
  14.1 0.0 collective-permute-done.4.refs_2_
  14.2 1.4 %collective-permute-done.5.refs_3_ = bf16[3,4,3584]{2,1,0:T(4,128)(2,1)S(1)} collective-permute-done((bf16[3,4,3584]{2,1,0:T(4,128)(2,1)S(1)}, bf16[3,4,3584]{2,1,0:T(4,128)(2,1)S(1)}, u32[]{:S(2)}, u32[]{:S(2)}) %collective-permute-start.5) | collective-permute-done | bytes 86048 | tf_op jit(solution)/shard_map/ppermute | solution.py:40
  15.6 0.1 collective-permute-done.6.refs_4_
  15.7 0.0 copy-start
  15.7 0.0 copy-start.1
  15.7 2.7 %expert.1 = (bf16[3,4,3584]{2,1,0:T(4,128)(2,1)S(1)}, bf16[3,4,3584]{2,1,0:T(4,128)(2,1)S(1)}, bf16[3,4,3584]{2,1,0:T(4,128)(2,1)S(1)}, bf16[3,4,3584]{2,1,0:T(4...) custom-call(bf16[3584,256]{1,0:T(8,128)(2,1)S(1)} %get-tuple-element, ...), custom_call_target="tpu_custom_call", output_to_operand_aliasing={{8}: (3, {}), {9}: (4, {})} | custom-call | tf_op jit(solution)/shard_map/expert/pallas_call | solution.py:235
  18.5 2.2 %collective-permute-start.10 = (bf16[3,4,3584]{2,1,0:T(4,128)(2,1)S(1)}, bf16[3,4,3584]{2,1,0:T(4,128)(2,1)S(1)}, u32[]{:S(2)}, u32[]{:S(2)}) collective-permute-start(bf16[3,4,3584]{2,1,0:T(4,128)(2,1)S(1)} %get-tuple-element.31), channel_id=1, source_target_pairs={{0,3},{1,2},{2,1},{3,0},{4,7},{5,6},{6,5},{7,4},{8,11},{9,10},{10,... | collective-permute-start | bytes 258056 | tf_op jit(solution)/shard_map/ppermute | solution.py:40
  20.7 0.1 collective-permute-start.11
  20.7 0.6 %collective-permute-start.12 = (bf16[3,4,3584]{2,1,0:T(4,128)(2,1)S(1)}, bf16[3,4,3584]{2,1,0:T(4,128)(2,1)S(1)}, u32[]{:S(2)}, u32[]{:S(2)}) collective-permute-start(bf16[3,4,3584]{2,1,0:T(4,128)(2,1)S(1)} %get-tuple-element.33), channel_id=1, source_target_pairs={{0,1},{1,0},{2,3},{3,2},{4,5},{5,4},{6,7},{7,6},{8,9},{9,8},{10,11... | collective-permute-start | bytes 258056 | tf_op jit(solution)/shard_map/ppermute | solution.py:40
  21.4 0.8 %collective-permute-start.7 = (bf16[3,4,3584]{2,1,0:T(4,128)(2,1)S(1)}, bf16[3,4,3584]{2,1,0:T(4,128)(2,1)S(1)}, u32[]{:S(2)}, u32[]{:S(2)}) collective-permute-start(bf16[3,4,3584]{2,1,0:T(4,128)(2,1)S(1)} %get-tuple-element.27), channel_id=1, source_target_pairs={{0,1},{1,0},{2,3},{3,2},{4,5},{5,4},{6,7},{7,6},{8,9},{9,8},{10,11... | collective-permute-start | bytes 258056 | tf_op jit(solution)/shard_map/ppermute | solution.py:40
  22.2 1.4 %collective-permute-start.8 = (bf16[3,4,3584]{2,1,0:T(4,128)(2,1)S(1)}, bf16[3,4,3584]{2,1,0:T(4,128)(2,1)S(1)}, u32[]{:S(2)}, u32[]{:S(2)}) collective-permute-start(bf16[3,4,3584]{2,1,0:T(4,128)(2,1)S(1)} %get-tuple-element.28), channel_id=1, source_target_pairs={{0,2},{1,3},{2,0},{3,1},{4,6},{5,7},{6,4},{7,5},{8,10},{9,11},{10,... | collective-permute-start | bytes 258056 | tf_op jit(solution)/shard_map/ppermute | solution.py:40
  23.6 0.0 collective-permute-done.10.refs_1_
  23.6 1.3 %collective-permute-start.9 = (bf16[3,4,3584]{2,1,0:T(4,128)(2,1)S(1)}, bf16[3,4,3584]{2,1,0:T(4,128)(2,1)S(1)}, u32[]{:S(2)}, u32[]{:S(2)}) collective-permute-start(bf16[3,4,3584]{2,1,0:T(4,128)(2,1)S(1)} %get-tuple-element.29), channel_id=1, source_target_pairs={{0,3},{1,2},{2,1},{3,0},{4,7},{5,6},{6,5},{7,4},{8,11},{9,10},{10,... | collective-permute-start | bytes 258056 | tf_op jit(solution)/shard_map/ppermute | solution.py:40
  24.9 0.0 collective-permute-done.11.refs_2_
  24.9 0.0 collective-permute-done.12.refs_3_
  24.9 0.1 total.1
  25.0 3.0 %collective-permute-start.13 = (bf16[3,4,3584]{2,1,0:T(4,128)(2,1)S(1)}, bf16[3,4,3584]{2,1,0:T(4,128)(2,1)S(1)}, u32[]{:S(2)}, u32[]{:S(2)}) collective-permute-start(bf16[3,4,3584]{2,1,0:T(4,128)(2,1)S(1)} %total.1), channel_id=1, source_target_pairs={{0,4},{2,6},{4,0},{6,2},{1,5},{3,7},{5,1},{7,3},{8,12},{10,14},{12... | collective-permute-start | bytes 258056 | tf_op jit(solution)/shard_map/ppermute | solution.py:45
  28.6 0.0 collective-permute-done.7.refs_1_
  28.7 0.0 collective-permute-done.8.refs_2_
  28.7 0.0 collective-permute-done.9.refs_3_
  28.7 1.6 %collective-permute-done.13.refs_4_ = bf16[3,4,3584]{2,1,0:T(4,128)(2,1)S(1)} collective-permute-done((bf16[3,4,3584]{2,1,0:T(4,128)(2,1)S(1)}, bf16[3,4,3584]{2,1,0:T(4,128)(2,1)S(1)}, u32[]{:S(2)}, u32[]{:S(2)}) %collective-permute-start.13) | collective-permute-done | bytes 86048 | tf_op jit(solution)/shard_map/ppermute | solution.py:45
  30.3 0.0 copy-done
  30.3 0.3 grad.1
  30.6 5.2 %collective-permute-start.14 = (bf16[8,3584]{1,0:T(8,128)(2,1)S(1)}, bf16[8,3584]{1,0:T(8,128)(2,1)S(1)}, u32[]{:S(2)}, u32[]{:S(2)}) collective-permute-start(bf16[8,3584]{1,0:T(8,128)(2,1)S(1)} %grad.1), channel_id=1, source_target_pairs={{8,0},{16,8},{24,16},{9,1},{17,9},{25,17},{10,2},{18,10},{26,18},{... | collective-permute-start | bytes 172040 | tf_op jit(solution)/shard_map/ppermute | solution.py:49
  35.8 0.0 copy-done.1
  35.9 1.0 %out.1 = bf16[8,3584]{1,0:T(8,128)(2,1)} custom-call(s32[1,1]{1,0:T(1,128)S(6)} %copy.15.keep, f32[2,8,128]{2,1,0:T(8,128)S(1)} %get-tuple-element.18.mix, bf16[8,3584]{1,0:T(8,128)(2,1)S(1)} %copy-done.1, bf16[3,4,3584]{2,1,0:T(4,128)(2,1)S(1)} %get-tuple-element.26.refs_0_, bf16[3,4,3584]{2,1,0:T(4,128)(2,1)S(1)} %collective-permute-done.7.refs_1_, ...), custom_call_target="tpu_custom_call" | custom-call | tf_op jit(solution)/shard_map/out/pallas_call | solution.py:250
  36.8 2.0 %collective-permute-done.14 = bf16[8,3584]{1,0:T(8,128)(2,1)S(1)} collective-permute-done((bf16[8,3584]{1,0:T(8,128)(2,1)S(1)}, bf16[8,3584]{1,0:T(8,128)(2,1)S(1)}, u32[]{:S(2)}, u32[]{:S(2)}) %collective-permute-start.14) | collective-permute-done | bytes 57376 | tf_op jit(solution)/shard_map/ppermute | solution.py:49
  38.8 0.6 %copy.16 = bf16[8,3584]{1,0:T(8,128)(2,1)} copy(bf16[8,3584]{1,0:T(8,128)(2,1)S(1)} %collective-permute-done.14) | data formatting | bytes 114688
Async XLA Ops:
  1.9 5.9 %collective-permute-start.3 = (bf16[3,4,3584]{2,1,0:T(4,128)(2,1)S(1)}, bf16[3,4,3584]{2,1,0:T(4,128)(2,1)S(1)}, u32[]{:S(2)}, u32[]{:S(2)}) collective-permute-start(bf16[3,4,3584]{2,1,0:T(4,128)(2,1)S(1)} %get-tuple-element.25), channel_id=1, source_target_pairs={{0,4},{2,6},{4,0},{6,2},{1,5},{3,7},{5,1},{7,3},{8,12},{10,14},{12... | collective-permute-start | bytes 258056 | tf_op jit(solution)/shard_map/ppermute | solution.py:45
  5.1 6.1 %collective-permute-start = (bf16[3,4,3584]{2,1,0:T(4,128)(2,1)S(1)}, bf16[3,4,3584]{2,1,0:T(4,128)(2,1)S(1)}, u32[]{:S(2)}, u32[]{:S(2)}) collective-permute-start(bf16[3,4,3584]{2,1,0:T(4,128)(2,1)S(1)} %get-tuple-element.19.refs_3_), channel_id=1, source_target_pairs={{0,1},{1,0},{2,3},{3,2},{4,5},{5,4},{6,7},{7,6},{8,9},{9,8},{10,11... | collective-permute-start | bytes 258056 | tf_op jit(solution)/shard_map/ppermute | solution.py:40
  6.3 5.2 %collective-permute-start.1 = (bf16[3,4,3584]{2,1,0:T(4,128)(2,1)S(1)}, bf16[3,4,3584]{2,1,0:T(4,128)(2,1)S(1)}, u32[]{:S(2)}, u32[]{:S(2)}) collective-permute-start(bf16[3,4,3584]{2,1,0:T(4,128)(2,1)S(1)} %get-tuple-element.19.refs_3_), channel_id=1, source_target_pairs={{0,2},{1,3},{2,0},{3,1},{4,6},{5,7},{6,4},{7,5},{8,10},{9,11},{10,... | collective-permute-start | bytes 258056 | tf_op jit(solution)/shard_map/ppermute | solution.py:40
  7.6 6.5 %collective-permute-start.2 = (bf16[3,4,3584]{2,1,0:T(4,128)(2,1)S(1)}, bf16[3,4,3584]{2,1,0:T(4,128)(2,1)S(1)}, u32[]{:S(2)}, u32[]{:S(2)}) collective-permute-start(bf16[3,4,3584]{2,1,0:T(4,128)(2,1)S(1)} %get-tuple-element.19.refs_3_), channel_id=1, source_target_pairs={{0,3},{1,2},{2,1},{3,0},{4,7},{5,6},{6,5},{7,4},{8,11},{9,10},{10,... | collective-permute-start | bytes 258056 | tf_op jit(solution)/shard_map/ppermute | solution.py:40
  7.7 6.4 %collective-permute-start.4 = (bf16[3,4,3584]{2,1,0:T(4,128)(2,1)S(1)}, bf16[3,4,3584]{2,1,0:T(4,128)(2,1)S(1)}, u32[]{:S(2)}, u32[]{:S(2)}) collective-permute-start(bf16[3,4,3584]{2,1,0:T(4,128)(2,1)S(1)} %collective-permute-done.3.refs_1_), channel_id=1, source_target_pairs={{0,3},{1,2},{2,1},{3,0},{4,7},{5,6},{6,5},{7,4},{8,11},{9,10},{10,... | collective-permute-start | bytes 258056 | tf_op jit(solution)/shard_map/ppermute | solution.py:40
  11.2 4.4 %collective-permute-start.5 = (bf16[3,4,3584]{2,1,0:T(4,128)(2,1)S(1)}, bf16[3,4,3584]{2,1,0:T(4,128)(2,1)S(1)}, u32[]{:S(2)}, u32[]{:S(2)}) collective-permute-start(bf16[3,4,3584]{2,1,0:T(4,128)(2,1)S(1)} %collective-permute-done.3.refs_1_), channel_id=1, source_target_pairs={{0,2},{1,3},{2,0},{3,1},{4,6},{5,7},{6,4},{7,5},{8,10},{9,11},{10,... | collective-permute-start | bytes 258056 | tf_op jit(solution)/shard_map/ppermute | solution.py:40
  11.2 4.5 %collective-permute-start.6 = (bf16[3,4,3584]{2,1,0:T(4,128)(2,1)S(1)}, bf16[3,4,3584]{2,1,0:T(4,128)(2,1)S(1)}, u32[]{:S(2)}, u32[]{:S(2)}) collective-permute-start(bf16[3,4,3584]{2,1,0:T(4,128)(2,1)S(1)} %collective-permute-done.3.refs_1_), channel_id=1, source_target_pairs={{0,1},{1,0},{2,3},{3,2},{4,5},{5,4},{6,7},{7,6},{8,9},{9,8},{10,11... | collective-permute-start | bytes 258056 | tf_op jit(solution)/shard_map/ppermute | solution.py:40
  15.7 14.6 %copy-start = (bf16[8,3584]{1,0:T(8,128)(2,1)S(1)}, bf16[8,3584]{1,0:T(8,128)(2,1)}, u32[]{:S(2)}) copy-start(bf16[8,3584]{1,0:T(8,128)(2,1)} %base.3) | copy-start | bytes 172036
  15.7 20.1 %copy-start.1 = (bf16[8,3584]{1,0:T(8,128)(2,1)S(1)}, bf16[8,3584]{1,0:T(8,128)(2,1)}, u32[]{:S(2)}) copy-start(bf16[8,3584]{1,0:T(8,128)(2,1)} %base.2) | copy-start | bytes 172036
  18.5 5.2 %collective-permute-start.10 = (bf16[3,4,3584]{2,1,0:T(4,128)(2,1)S(1)}, bf16[3,4,3584]{2,1,0:T(4,128)(2,1)S(1)}, u32[]{:S(2)}, u32[]{:S(2)}) collective-permute-start(bf16[3,4,3584]{2,1,0:T(4,128)(2,1)S(1)} %get-tuple-element.31), channel_id=1, source_target_pairs={{0,3},{1,2},{2,1},{3,0},{4,7},{5,6},{6,5},{7,4},{8,11},{9,10},{10,... | collective-permute-start | bytes 258056 | tf_op jit(solution)/shard_map/ppermute | solution.py:40
  20.7 4.2 %collective-permute-start.11 = (bf16[3,4,3584]{2,1,0:T(4,128)(2,1)S(1)}, bf16[3,4,3584]{2,1,0:T(4,128)(2,1)S(1)}, u32[]{:S(2)}, u32[]{:S(2)}) collective-permute-start(bf16[3,4,3584]{2,1,0:T(4,128)(2,1)S(1)} %get-tuple-element.32), channel_id=1, source_target_pairs={{0,2},{1,3},{2,0},{3,1},{4,6},{5,7},{6,4},{7,5},{8,10},{9,11},{10,... | collective-permute-start | bytes 258056 | tf_op jit(solution)/shard_map/ppermute | solution.py:40
  20.7 4.2 %collective-permute-start.12 = (bf16[3,4,3584]{2,1,0:T(4,128)(2,1)S(1)}, bf16[3,4,3584]{2,1,0:T(4,128)(2,1)S(1)}, u32[]{:S(2)}, u32[]{:S(2)}) collective-permute-start(bf16[3,4,3584]{2,1,0:T(4,128)(2,1)S(1)} %get-tuple-element.33), channel_id=1, source_target_pairs={{0,1},{1,0},{2,3},{3,2},{4,5},{5,4},{6,7},{7,6},{8,9},{9,8},{10,11... | collective-permute-start | bytes 258056 | tf_op jit(solution)/shard_map/ppermute | solution.py:40
  21.4 7.3 %collective-permute-start.7 = (bf16[3,4,3584]{2,1,0:T(4,128)(2,1)S(1)}, bf16[3,4,3584]{2,1,0:T(4,128)(2,1)S(1)}, u32[]{:S(2)}, u32[]{:S(2)}) collective-permute-start(bf16[3,4,3584]{2,1,0:T(4,128)(2,1)S(1)} %get-tuple-element.27), channel_id=1, source_target_pairs={{0,1},{1,0},{2,3},{3,2},{4,5},{5,4},{6,7},{7,6},{8,9},{9,8},{10,11... | collective-permute-start | bytes 258056 | tf_op jit(solution)/shard_map/ppermute | solution.py:40
  22.2 6.4 %collective-permute-start.8 = (bf16[3,4,3584]{2,1,0:T(4,128)(2,1)S(1)}, bf16[3,4,3584]{2,1,0:T(4,128)(2,1)S(1)}, u32[]{:S(2)}, u32[]{:S(2)}) collective-permute-start(bf16[3,4,3584]{2,1,0:T(4,128)(2,1)S(1)} %get-tuple-element.28), channel_id=1, source_target_pairs={{0,2},{1,3},{2,0},{3,1},{4,6},{5,7},{6,4},{7,5},{8,10},{9,11},{10,... | collective-permute-start | bytes 258056 | tf_op jit(solution)/shard_map/ppermute | solution.py:40
  23.6 5.0 %collective-permute-start.9 = (bf16[3,4,3584]{2,1,0:T(4,128)(2,1)S(1)}, bf16[3,4,3584]{2,1,0:T(4,128)(2,1)S(1)}, u32[]{:S(2)}, u32[]{:S(2)}) collective-permute-start(bf16[3,4,3584]{2,1,0:T(4,128)(2,1)S(1)} %get-tuple-element.29), channel_id=1, source_target_pairs={{0,3},{1,2},{2,1},{3,0},{4,7},{5,6},{6,5},{7,4},{8,11},{9,10},{10,... | collective-permute-start | bytes 258056 | tf_op jit(solution)/shard_map/ppermute | solution.py:40
  25.0 5.3 %collective-permute-start.13 = (bf16[3,4,3584]{2,1,0:T(4,128)(2,1)S(1)}, bf16[3,4,3584]{2,1,0:T(4,128)(2,1)S(1)}, u32[]{:S(2)}, u32[]{:S(2)}) collective-permute-start(bf16[3,4,3584]{2,1,0:T(4,128)(2,1)S(1)} %total.1), channel_id=1, source_target_pairs={{0,4},{2,6},{4,0},{6,2},{1,5},{3,7},{5,1},{7,3},{8,12},{10,14},{12... | collective-permute-start | bytes 258056 | tf_op jit(solution)/shard_map/ppermute | solution.py:45
  30.6 8.2 %collective-permute-start.14 = (bf16[8,3584]{1,0:T(8,128)(2,1)S(1)}, bf16[8,3584]{1,0:T(8,128)(2,1)S(1)}, u32[]{:S(2)}, u32[]{:S(2)}) collective-permute-start(bf16[8,3584]{1,0:T(8,128)(2,1)S(1)} %grad.1), channel_id=1, source_target_pairs={{8,0},{16,8},{24,16},{9,1},{17,9},{25,17},{10,2},{18,10},{26,18},{... | collective-permute-start | bytes 172040 | tf_op jit(solution)/shard_map/ppermute | solution.py:49

commit v6 on v4

--- a/solution.py
+++ b/solution.py
@@ -51,12 +51,13 @@
 def pack_kernel(experts, cap, top, *refs):
     stored, mix_out, blocks = refs[:4], refs[4], refs[5 : 5 + experts]
     held, sems = refs[5 + experts : -1], refs[-1]
-    copies = [pltpu.make_async_copy(s, h, sems.at[i]) for i, (s, h) in enumerate(zip(stored, held))]
+    routes, probs, rows = held
+    pairs = routes.shape[1]
+    tokens = pairs // top
+    places = (routes, probs, rows.at[:tokens], rows.at[tokens:])
+    copies = [pltpu.make_async_copy(s, h, sems.at[i]) for i, (s, h) in enumerate(zip(stored, places))]
     for copy in copies:
         copy.start()
-    routes, probs, acts, cot = held
-    pairs = routes.shape[1]
-    tokens = pairs // top
     copies[0].wait()
     chosen = jnp.broadcast_to(routes[...], (pairs, pairs))
     p = lax.broadcasted_iota(jnp.int32, (pairs, pairs), 0)
@@ -78,10 +79,10 @@
         owner = lax.broadcasted_iota(jnp.int32, (tokens, pairs), 1) // top
         owner = rounded(jnp.where(owner == lax.broadcasted_iota(jnp.int32, (tokens, pairs), 0), 1.0, 0.0))
         scatter = [dot(rounded(s), owner, CROSS) for s in scatter]
+    scatter = rounded(jnp.concatenate(scatter, axis=1))
     copies[2].wait()
-    packed = dot(rounded(scatter[0]), acts[...])
     copies[3].wait()
-    packed = rounded(packed + dot(rounded(scatter[1]), cot[...]))
+    packed = rounded(dot(scatter, rows[...]))
     tiles = blocks[0].shape[0]
     for k, block in enumerate(blocks):
         for i in range(tiles):
@@ -199,7 +200,8 @@
         in_specs=[far_off] * 4,
         out_specs=[vmem] * (1 + experts),
         out_shape=[pltpu.VMEM((2, token_count, LANES), jnp.float32)] + [block] * experts,
-        scratch_shapes=[pltpu.VMEM(x.shape, x.dtype) for x in inputs] + [pltpu.SemaphoreType.DMA((4,))],
+        scratch_shapes=[pltpu.VMEM(x.shape, x.dtype) for x in inputs[:2]]
+        + [pltpu.VMEM((2 * token_count, width), acts.dtype), pltpu.SemaphoreType.DMA((4,))],
         compiler_params=room(4),
         name="pack",
     )(*map(in_hbm, inputs))

time: 39.9 us -> 39.8 us (level)
  no operation moved by 1% of the time
where the time goes in v6:
time: 39.8 us; the launch traced here: 39.3 us
  starting transfers between devices  24.4 us (61%)
  Pallas kernels  7.83 us (20%)
  waiting for transfers between devices  5.1 us (13%)
  between operations  1.38 us (3%)
  local copies, waits for them, and re-layouts  0.63 us (2%)
    ppermute x12, starting transfers between devices, to_member(): return lax.ppermute(shard, ('expert', 'dp'), pairs)  12.9 us
    ppermute x2, starting transfers between devices, to_expert(): lax.ppermute(shard, 'expert', [(e, (e + 2 * by) % n) for e in range(n)])  6.14 us
    ppermute x1, starting transfers between devices, to_below(): lax.ppermute(shard, 'pipe', [(p, p - 1) for p in range(1, lax.axis_size('...  5.36 us
    pallas_call x1, Pallas kernels, shards(): pl.pallas_call(functools.partial(expert_kernel, capacity, count), in_spec...  2.66 us
    pallas_call x1, Pallas kernels, shards(): pl.pallas_call(functools.partial(near_kernel, capacity, count), in_specs=...  2.63 us
    ppermute x1, waiting for transfers between devices, to_below(): lax.ppermute(shard, 'pipe', [(p, p - 1) for p in range(1, lax.axis_size('...  2.01 us
    ppermute x12, waiting for transfers between devices, to_member(): return lax.ppermute(shard, ('expert', 'dp'), pairs)  1.58 us
    ppermute x2, waiting for transfers between devices, to_expert(): lax.ppermute(shard, 'expert', [(e, (e + 2 * by) % n) for e in range(n)])  1.5 us
  transfers between devices with their start and end apart: 15, of which 5 were waited for; matrix products, arithmetic and copies ran while one was open for 0% of the time, Pallas kernels for 9%

profile of v6, /device:TPU:1, one launch (start us, length us, event | category | flops | bytes accessed | tf_op | source)
XLA Modules:
  0.0 39.3 jit_solution(11666562475083357726)
XLA Ops:
  0.6 1.2 %pack.1 = (f32[2,8,128]{2,1,0:T(8,128)S(1)}, bf16[3,4,3584]{2,1,0:T(4,128)(2,1)S(1)}, bf16[3,4,3584]{2,1,0:T(4,128)(2,1)S(1)}) custom-call(s32[1,8]{1,0:T(1,128)} %bitcast.8, bf16[1,8]{1,0:T(2,128)(2,1)} %bitcast.9, bf16[8,3584]{1,0:T(8,128)(2,1)} %base.2, bf16[8,3584]{1,0:T(8,128)(2,1)} %base.3), custom_call_target="tpu_custom_call" | custom-call | tf_op jit(solution)/shard_map/pack/pallas_call | solution.py:198
  1.8 3.2 %collective-permute-start.3 = (bf16[3,4,3584]{2,1,0:T(4,128)(2,1)S(1)}, bf16[3,4,3584]{2,1,0:T(4,128)(2,1)S(1)}, u32[]{:S(2)}, u32[]{:S(2)}) collective-permute-start(bf16[3,4,3584]{2,1,0:T(4,128)(2,1)S(1)} %get-tuple-element.25), channel_id=1, source_target_pairs={{0,4},{2,6},{4,0},{6,2},{1,5},{3,7},{5,1},{7,3},{8,12},{10,14},{12... | collective-permute-start | bytes 258056 | tf_op jit(solution)/shard_map/ppermute | solution.py:44
  5.0 1.2 %collective-permute-start = (bf16[3,4,3584]{2,1,0:T(4,128)(2,1)S(1)}, bf16[3,4,3584]{2,1,0:T(4,128)(2,1)S(1)}, u32[]{:S(2)}, u32[]{:S(2)}) collective-permute-start(bf16[3,4,3584]{2,1,0:T(4,128)(2,1)S(1)} %get-tuple-element.19.refs_3_), channel_id=1, source_target_pairs={{0,1},{1,0},{2,3},{3,2},{4,5},{5,4},{6,7},{7,6},{8,9},{9,8},{10,11... | collective-permute-start | bytes 258056 | tf_op jit(solution)/shard_map/ppermute | solution.py:39
  6.2 1.3 %collective-permute-start.1 = (bf16[3,4,3584]{2,1,0:T(4,128)(2,1)S(1)}, bf16[3,4,3584]{2,1,0:T(4,128)(2,1)S(1)}, u32[]{:S(2)}, u32[]{:S(2)}) collective-permute-start(bf16[3,4,3584]{2,1,0:T(4,128)(2,1)S(1)} %get-tuple-element.19.refs_3_), channel_id=1, source_target_pairs={{0,2},{1,3},{2,0},{3,1},{4,6},{5,7},{6,4},{7,5},{8,10},{9,11},{10,... | collective-permute-start | bytes 258056 | tf_op jit(solution)/shard_map/ppermute | solution.py:39
  7.5 0.1 collective-permute-start.2
  7.7 0.0 collective-permute-done.3.refs_0_
  7.7 3.4 %collective-permute-start.4 = (bf16[3,4,3584]{2,1,0:T(4,128)(2,1)S(1)}, bf16[3,4,3584]{2,1,0:T(4,128)(2,1)S(1)}, u32[]{:S(2)}, u32[]{:S(2)}) collective-permute-start(bf16[3,4,3584]{2,1,0:T(4,128)(2,1)S(1)} %collective-permute-done.3.refs_0_), channel_id=1, source_target_pairs={{0,3},{1,2},{2,1},{3,0},{4,7},{5,6},{6,5},{7,4},{8,11},{9,10},{10,... | collective-permute-start | bytes 258056 | tf_op jit(solution)/shard_map/ppermute | solution.py:39
  11.1 0.0 collective-permute-start.5
  11.1 0.0 collective-permute-done.refs_4_
  11.1 0.3 collective-permute-start.6
  11.4 0.0 collective-permute-done.1.refs_5_
  11.4 0.8 %collective-permute-done.2.refs_6_ = bf16[3,4,3584]{2,1,0:T(4,128)(2,1)S(1)} collective-permute-done((bf16[3,4,3584]{2,1,0:T(4,128)(2,1)S(1)}, bf16[3,4,3584]{2,1,0:T(4,128)(2,1)S(1)}, u32[]{:S(2)}, u32[]{:S(2)}) %collective-permute-start.2) | collective-permute-done | bytes 86048 | tf_op jit(solution)/shard_map/ppermute | solution.py:39
  12.3 2.6 %near.1 = (bf16[64,3584]{1,0:T(8,128)(2,1)S(1)}, bf16[64,3584]{1,0:T(8,128)(2,1)S(1)}, bf16[3584,256]{1,0:T(8,128)(2,1)S(1)}, bf16[3584,256]{1,0:T(8,128)(2,1)S(1)}, bf16[256,3584]{1,0:T(8,128)(2,1)S(1)}) custom-call(bf16[3584,256]{1,0:T(8,128)(2,1)} %bitcast.5, bf16[3584,256]{1,0:T(8,128)(2,1)} %bitcast.6, bf16[256,3584]{1,0:T(8,128)(2,1)} %bitcast.7, ...), custom_call_target="tpu_custom_call" | custom-call | tf_op jit(solution)/shard_map/near/pallas_call | solution.py:219
  14.9 0.0 collective-permute-done.4.refs_1_
  14.9 0.7 %collective-permute-done.5.refs_2_ = bf16[3,4,3584]{2,1,0:T(4,128)(2,1)S(1)} collective-permute-done((bf16[3,4,3584]{2,1,0:T(4,128)(2,1)S(1)}, bf16[3,4,3584]{2,1,0:T(4,128)(2,1)S(1)}, u32[]{:S(2)}, u32[]{:S(2)}) %collective-permute-start.5) | collective-permute-done | bytes 86048 | tf_op jit(solution)/shard_map/ppermute | solution.py:39
  15.6 0.1 collective-permute-done.6.refs_3_
  15.6 0.0 copy-start
  15.6 0.0 copy-start.1
  15.6 2.7 %expert.1 = (bf16[3,4,3584]{2,1,0:T(4,128)(2,1)S(1)}, bf16[3,4,3584]{2,1,0:T(4,128)(2,1)S(1)}, bf16[3,4,3584]{2,1,0:T(4,128)(2,1)S(1)}, bf16[3,4,3584]{2,1,0:T(4...) custom-call(bf16[3584,256]{1,0:T(8,128)(2,1)S(1)} %get-tuple-element, ...), custom_call_target="tpu_custom_call", output_to_operand_aliasing={{8}: (3, {}), {9}: (4, {})} | custom-call | tf_op jit(solution)/shard_map/expert/pallas_call | solution.py:228
  18.3 2.2 %collective-permute-start.10 = (bf16[3,4,3584]{2,1,0:T(4,128)(2,1)S(1)}, bf16[3,4,3584]{2,1,0:T(4,128)(2,1)S(1)}, u32[]{:S(2)}, u32[]{:S(2)}) collective-permute-start(bf16[3,4,3584]{2,1,0:T(4,128)(2,1)S(1)} %get-tuple-element.31), channel_id=1, source_target_pairs={{0,3},{1,2},{2,1},{3,0},{4,7},{5,6},{6,5},{7,4},{8,11},{9,10},{10,... | collective-permute-start | bytes 258056 | tf_op jit(solution)/shard_map/ppermute | solution.py:39
  20.6 0.1 collective-permute-start.11
  20.7 0.6 %collective-permute-start.12 = (bf16[3,4,3584]{2,1,0:T(4,128)(2,1)S(1)}, bf16[3,4,3584]{2,1,0:T(4,128)(2,1)S(1)}, u32[]{:S(2)}, u32[]{:S(2)}) collective-permute-start(bf16[3,4,3584]{2,1,0:T(4,128)(2,1)S(1)} %get-tuple-element.33), channel_id=1, source_target_pairs={{0,1},{1,0},{2,3},{3,2},{4,5},{5,4},{6,7},{7,6},{8,9},{9,8},{10,11... | collective-permute-start | bytes 258056 | tf_op jit(solution)/shard_map/ppermute | solution.py:39
  21.3 0.9 %collective-permute-start.7 = (bf16[3,4,3584]{2,1,0:T(4,128)(2,1)S(1)}, bf16[3,4,3584]{2,1,0:T(4,128)(2,1)S(1)}, u32[]{:S(2)}, u32[]{:S(2)}) collective-permute-start(bf16[3,4,3584]{2,1,0:T(4,128)(2,1)S(1)} %get-tuple-element.27), channel_id=1, source_target_pairs={{0,1},{1,0},{2,3},{3,2},{4,5},{5,4},{6,7},{7,6},{8,9},{9,8},{10,11... | collective-permute-start | bytes 258056 | tf_op jit(solution)/shard_map/ppermute | solution.py:39
  22.1 1.3 %collective-permute-start.8 = (bf16[3,4,3584]{2,1,0:T(4,128)(2,1)S(1)}, bf16[3,4,3584]{2,1,0:T(4,128)(2,1)S(1)}, u32[]{:S(2)}, u32[]{:S(2)}) collective-permute-start(bf16[3,4,3584]{2,1,0:T(4,128)(2,1)S(1)} %get-tuple-element.28), channel_id=1, source_target_pairs={{0,2},{1,3},{2,0},{3,1},{4,6},{5,7},{6,4},{7,5},{8,10},{9,11},{10,... | collective-permute-start | bytes 258056 | tf_op jit(solution)/shard_map/ppermute | solution.py:39
  23.5 0.0 collective-permute-done.10.refs_1_
  23.5 1.3 %collective-permute-start.9 = (bf16[3,4,3584]{2,1,0:T(4,128)(2,1)S(1)}, bf16[3,4,3584]{2,1,0:T(4,128)(2,1)S(1)}, u32[]{:S(2)}, u32[]{:S(2)}) collective-permute-start(bf16[3,4,3584]{2,1,0:T(4,128)(2,1)S(1)} %get-tuple-element.29), channel_id=1, source_target_pairs={{0,3},{1,2},{2,1},{3,0},{4,7},{5,6},{6,5},{7,4},{8,11},{9,10},{10,... | collective-permute-start | bytes 258056 | tf_op jit(solution)/shard_map/ppermute | solution.py:39
  24.8 0.0 collective-permute-done.11.refs_2_
  24.8 0.0 collective-permute-done.12.refs_3_
  24.8 0.1 total.1
  24.9 2.9 %collective-permute-start.13 = (bf16[3,4,3584]{2,1,0:T(4,128)(2,1)S(1)}, bf16[3,4,3584]{2,1,0:T(4,128)(2,1)S(1)}, u32[]{:S(2)}, u32[]{:S(2)}) collective-permute-start(bf16[3,4,3584]{2,1,0:T(4,128)(2,1)S(1)} %total.1), channel_id=1, source_target_pairs={{0,4},{2,6},{4,0},{6,2},{1,5},{3,7},{5,1},{7,3},{8,12},{10,14},{12... | collective-permute-start | bytes 258056 | tf_op jit(solution)/shard_map/ppermute | solution.py:44
  28.5 0.0 collective-permute-done.7.refs_1_
  28.5 0.0 collective-permute-done.8.refs_2_
  28.5 0.0 collective-permute-done.9.refs_3_
  28.5 1.5 %collective-permute-done.13.refs_4_ = bf16[3,4,3584]{2,1,0:T(4,128)(2,1)S(1)} collective-permute-done((bf16[3,4,3584]{2,1,0:T(4,128)(2,1)S(1)}, bf16[3,4,3584]{2,1,0:T(4,128)(2,1)S(1)}, u32[]{:S(2)}, u32[]{:S(2)}) %collective-permute-start.13) | collective-permute-done | bytes 86048 | tf_op jit(solution)/shard_map/ppermute | solution.py:44
  30.0 0.0 copy-done
  30.0 0.3 grad.1
  30.3 5.4 %collective-permute-start.14 = (bf16[8,3584]{1,0:T(8,128)(2,1)S(1)}, bf16[8,3584]{1,0:T(8,128)(2,1)S(1)}, u32[]{:S(2)}, u32[]{:S(2)}) collective-permute-start(bf16[8,3584]{1,0:T(8,128)(2,1)S(1)} %grad.1), channel_id=1, source_target_pairs={{8,0},{16,8},{24,16},{9,1},{17,9},{25,17},{10,2},{18,10},{26,18},{... | collective-permute-start | bytes 172040 | tf_op jit(solution)/shard_map/ppermute | solution.py:48
  35.7 0.0 copy-done.1
  35.7 1.0 %out.1 = bf16[8,3584]{1,0:T(8,128)(2,1)} custom-call(s32[1,1]{1,0:T(1,128)S(6)} %copy.15.keep, f32[2,8,128]{2,1,0:T(8,128)S(1)} %get-tuple-element.18.mix, bf16[8,3584]{1,0:T(8,128)(2,1)S(1)} %copy-done.1, bf16[3,4,3584]{2,1,0:T(4,128)(2,1)S(1)} %get-tuple-element.26.refs_0_, bf16[3,4,3584]{2,1,0:T(4,128)(2,1)S(1)} %collective-permute-done.7.refs_1_, ...), custom_call_target="tpu_custom_call" | custom-call | tf_op jit(solution)/shard_map/out/pallas_call | solution.py:243
  36.7 2.0 %collective-permute-done.14 = bf16[8,3584]{1,0:T(8,128)(2,1)S(1)} collective-permute-done((bf16[8,3584]{1,0:T(8,128)(2,1)S(1)}, bf16[8,3584]{1,0:T(8,128)(2,1)S(1)}, u32[]{:S(2)}, u32[]{:S(2)}) %collective-permute-start.14) | collective-permute-done | bytes 57376 | tf_op jit(solution)/shard_map/ppermute | solution.py:48
  38.7 0.6 %copy.16 = bf16[8,3584]{1,0:T(8,128)(2,1)} copy(bf16[8,3584]{1,0:T(8,128)(2,1)S(1)} %collective-permute-done.14) | data formatting | bytes 114688
Async XLA Ops:
  1.8 5.8 %collective-permute-start.3 = (bf16[3,4,3584]{2,1,0:T(4,128)(2,1)S(1)}, bf16[3,4,3584]{2,1,0:T(4,128)(2,1)S(1)}, u32[]{:S(2)}, u32[]{:S(2)}) collective-permute-start(bf16[3,4,3584]{2,1,0:T(4,128)(2,1)S(1)} %get-tuple-element.25), channel_id=1, source_target_pairs={{0,4},{2,6},{4,0},{6,2},{1,5},{3,7},{5,1},{7,3},{8,12},{10,14},{12... | collective-permute-start | bytes 258056 | tf_op jit(solution)/shard_map/ppermute | solution.py:44
  5.0 6.1 %collective-permute-start = (bf16[3,4,3584]{2,1,0:T(4,128)(2,1)S(1)}, bf16[3,4,3584]{2,1,0:T(4,128)(2,1)S(1)}, u32[]{:S(2)}, u32[]{:S(2)}) collective-permute-start(bf16[3,4,3584]{2,1,0:T(4,128)(2,1)S(1)} %get-tuple-element.19.refs_3_), channel_id=1, source_target_pairs={{0,1},{1,0},{2,3},{3,2},{4,5},{5,4},{6,7},{7,6},{8,9},{9,8},{10,11... | collective-permute-start | bytes 258056 | tf_op jit(solution)/shard_map/ppermute | solution.py:39
  6.2 5.2 %collective-permute-start.1 = (bf16[3,4,3584]{2,1,0:T(4,128)(2,1)S(1)}, bf16[3,4,3584]{2,1,0:T(4,128)(2,1)S(1)}, u32[]{:S(2)}, u32[]{:S(2)}) collective-permute-start(bf16[3,4,3584]{2,1,0:T(4,128)(2,1)S(1)} %get-tuple-element.19.refs_3_), channel_id=1, source_target_pairs={{0,2},{1,3},{2,0},{3,1},{4,6},{5,7},{6,4},{7,5},{8,10},{9,11},{10,... | collective-permute-start | bytes 258056 | tf_op jit(solution)/shard_map/ppermute | solution.py:39
  7.5 4.7 %collective-permute-start.2 = (bf16[3,4,3584]{2,1,0:T(4,128)(2,1)S(1)}, bf16[3,4,3584]{2,1,0:T(4,128)(2,1)S(1)}, u32[]{:S(2)}, u32[]{:S(2)}) collective-permute-start(bf16[3,4,3584]{2,1,0:T(4,128)(2,1)S(1)} %get-tuple-element.19.refs_3_), channel_id=1, source_target_pairs={{0,3},{1,2},{2,1},{3,0},{4,7},{5,6},{6,5},{7,4},{8,11},{9,10},{10,... | collective-permute-start | bytes 258056 | tf_op jit(solution)/shard_map/ppermute | solution.py:39
  7.7 7.2 %collective-permute-start.4 = (bf16[3,4,3584]{2,1,0:T(4,128)(2,1)S(1)}, bf16[3,4,3584]{2,1,0:T(4,128)(2,1)S(1)}, u32[]{:S(2)}, u32[]{:S(2)}) collective-permute-start(bf16[3,4,3584]{2,1,0:T(4,128)(2,1)S(1)} %collective-permute-done.3.refs_0_), channel_id=1, source_target_pairs={{0,3},{1,2},{2,1},{3,0},{4,7},{5,6},{6,5},{7,4},{8,11},{9,10},{10,... | collective-permute-start | bytes 258056 | tf_op jit(solution)/shard_map/ppermute | solution.py:39
  11.1 4.5 %collective-permute-start.5 = (bf16[3,4,3584]{2,1,0:T(4,128)(2,1)S(1)}, bf16[3,4,3584]{2,1,0:T(4,128)(2,1)S(1)}, u32[]{:S(2)}, u32[]{:S(2)}) collective-permute-start(bf16[3,4,3584]{2,1,0:T(4,128)(2,1)S(1)} %collective-permute-done.3.refs_0_), channel_id=1, source_target_pairs={{0,2},{1,3},{2,0},{3,1},{4,6},{5,7},{6,4},{7,5},{8,10},{9,11},{10,... | collective-permute-start | bytes 258056 | tf_op jit(solution)/shard_map/ppermute | solution.py:39
  11.1 4.5 %collective-permute-start.6 = (bf16[3,4,3584]{2,1,0:T(4,128)(2,1)S(1)}, bf16[3,4,3584]{2,1,0:T(4,128)(2,1)S(1)}, u32[]{:S(2)}, u32[]{:S(2)}) collective-permute-start(bf16[3,4,3584]{2,1,0:T(4,128)(2,1)S(1)} %collective-permute-done.3.refs_0_), channel_id=1, source_target_pairs={{0,1},{1,0},{2,3},{3,2},{4,5},{5,4},{6,7},{7,6},{8,9},{9,8},{10,11... | collective-permute-start | bytes 258056 | tf_op jit(solution)/shard_map/ppermute | solution.py:39
  15.6 14.4 %copy-start = (bf16[8,3584]{1,0:T(8,128)(2,1)S(1)}, bf16[8,3584]{1,0:T(8,128)(2,1)}, u32[]{:S(2)}) copy-start(bf16[8,3584]{1,0:T(8,128)(2,1)} %base.3) | copy-start | bytes 172036
  15.6 20.1 %copy-start.1 = (bf16[8,3584]{1,0:T(8,128)(2,1)S(1)}, bf16[8,3584]{1,0:T(8,128)(2,1)}, u32[]{:S(2)}) copy-start(bf16[8,3584]{1,0:T(8,128)(2,1)} %base.2) | copy-start | bytes 172036
  18.3 5.2 %collective-permute-start.10 = (bf16[3,4,3584]{2,1,0:T(4,128)(2,1)S(1)}, bf16[3,4,3584]{2,1,0:T(4,128)(2,1)S(1)}, u32[]{:S(2)}, u32[]{:S(2)}) collective-permute-start(bf16[3,4,3584]{2,1,0:T(4,128)(2,1)S(1)} %get-tuple-element.31), channel_id=1, source_target_pairs={{0,3},{1,2},{2,1},{3,0},{4,7},{5,6},{6,5},{7,4},{8,11},{9,10},{10,... | collective-permute-start | bytes 258056 | tf_op jit(solution)/shard_map/ppermute | solution.py:39
  20.6 4.2 %collective-permute-start.11 = (bf16[3,4,3584]{2,1,0:T(4,128)(2,1)S(1)}, bf16[3,4,3584]{2,1,0:T(4,128)(2,1)S(1)}, u32[]{:S(2)}, u32[]{:S(2)}) collective-permute-start(bf16[3,4,3584]{2,1,0:T(4,128)(2,1)S(1)} %get-tuple-element.32), channel_id=1, source_target_pairs={{0,2},{1,3},{2,0},{3,1},{4,6},{5,7},{6,4},{7,5},{8,10},{9,11},{10,... | collective-permute-start | bytes 258056 | tf_op jit(solution)/shard_map/ppermute | solution.py:39
  20.7 4.1 %collective-permute-start.12 = (bf16[3,4,3584]{2,1,0:T(4,128)(2,1)S(1)}, bf16[3,4,3584]{2,1,0:T(4,128)(2,1)S(1)}, u32[]{:S(2)}, u32[]{:S(2)}) collective-permute-start(bf16[3,4,3584]{2,1,0:T(4,128)(2,1)S(1)} %get-tuple-element.33), channel_id=1, source_target_pairs={{0,1},{1,0},{2,3},{3,2},{4,5},{5,4},{6,7},{7,6},{8,9},{9,8},{10,11... | collective-permute-start | bytes 258056 | tf_op jit(solution)/shard_map/ppermute | solution.py:39
  21.3 7.2 %collective-permute-start.7 = (bf16[3,4,3584]{2,1,0:T(4,128)(2,1)S(1)}, bf16[3,4,3584]{2,1,0:T(4,128)(2,1)S(1)}, u32[]{:S(2)}, u32[]{:S(2)}) collective-permute-start(bf16[3,4,3584]{2,1,0:T(4,128)(2,1)S(1)} %get-tuple-element.27), channel_id=1, source_target_pairs={{0,1},{1,0},{2,3},{3,2},{4,5},{5,4},{6,7},{7,6},{8,9},{9,8},{10,11... | collective-permute-start | bytes 258056 | tf_op jit(solution)/shard_map/ppermute | solution.py:39
  22.1 6.3 %collective-permute-start.8 = (bf16[3,4,3584]{2,1,0:T(4,128)(2,1)S(1)}, bf16[3,4,3584]{2,1,0:T(4,128)(2,1)S(1)}, u32[]{:S(2)}, u32[]{:S(2)}) collective-permute-start(bf16[3,4,3584]{2,1,0:T(4,128)(2,1)S(1)} %get-tuple-element.28), channel_id=1, source_target_pairs={{0,2},{1,3},{2,0},{3,1},{4,6},{5,7},{6,4},{7,5},{8,10},{9,11},{10,... | collective-permute-start | bytes 258056 | tf_op jit(solution)/shard_map/ppermute | solution.py:39
  23.5 5.0 %collective-permute-start.9 = (bf16[3,4,3584]{2,1,0:T(4,128)(2,1)S(1)}, bf16[3,4,3584]{2,1,0:T(4,128)(2,1)S(1)}, u32[]{:S(2)}, u32[]{:S(2)}) collective-permute-start(bf16[3,4,3584]{2,1,0:T(4,128)(2,1)S(1)} %get-tuple-element.29), channel_id=1, source_target_pairs={{0,3},{1,2},{2,1},{3,0},{4,7},{5,6},{6,5},{7,4},{8,11},{9,10},{10,... | collective-permute-start | bytes 258056 | tf_op jit(solution)/shard_map/ppermute | solution.py:39
  24.9 5.1 %collective-permute-start.13 = (bf16[3,4,3584]{2,1,0:T(4,128)(2,1)S(1)}, bf16[3,4,3584]{2,1,0:T(4,128)(2,1)S(1)}, u32[]{:S(2)}, u32[]{:S(2)}) collective-permute-start(bf16[3,4,3584]{2,1,0:T(4,128)(2,1)S(1)} %total.1), channel_id=1, source_target_pairs={{0,4},{2,6},{4,0},{6,2},{1,5},{3,7},{5,1},{7,3},{8,12},{10,14},{12... | collective-permute-start | bytes 258056 | tf_op jit(solution)/shard_map/ppermute | solution.py:44
  30.3 8.3 %collective-permute-start.14 = (bf16[8,3584]{1,0:T(8,128)(2,1)S(1)}, bf16[8,3584]{1,0:T(8,128)(2,1)S(1)}, u32[]{:S(2)}, u32[]{:S(2)}) collective-permute-start(bf16[8,3584]{1,0:T(8,128)(2,1)S(1)} %grad.1), channel_id=1, source_target_pairs={{8,0},{16,8},{24,16},{9,1},{17,9},{25,17},{10,2},{18,10},{26,18},{... | collective-permute-start | bytes 172040 | tf_op jit(solution)/shard_map/ppermute | solution.py:48
